TPU v7x, 32 devices: a whole 2x2x4 slice. The times are simulated.
32 devices in a mesh: dp: 4 (over y, core), tensor: 8 (over z, x).
Axes of the slice: x: 2, y: 2, z: 4, core: 2. Of those that a mesh axis runs over, the one named last changes fastest.
Arguments:
- tokens: bfloat16 [4, 2048, 1024], P('dp', 'tensor'), may hold values from -6 to 6
- cotangent: bfloat16 [4, 2048, 1024], P('dp', 'tensor'), may hold values from -6 to 6
- segments: int32 [4, 2048], P('dp'), may hold values from 0 to 2, as said below
- positions: int32 [4, 2048], P('dp'), may hold values from 0 to 1535, as said below
- attngain: float32 [1024], replicated, may hold values from 0.5 to 1.5
- ffngain: float32 [1024], replicated, may hold values from 0.5 to 1.5
- queryheads: bfloat16 [1024, 96], replicated, may hold values from -0.25 to 0.25
- querydims: bfloat16 [1024, 384], replicated, may hold values from -0.25 to 0.25
- keyheads: bfloat16 [1024, 32], replicated, may hold values from -0.25 to 0.25
- keydims: bfloat16 [1024, 128], replicated, may hold values from -0.25 to 0.25
- valueheads: bfloat16 [1024, 32], replicated, may hold values from -0.25 to 0.25
- valuedims: bfloat16 [1024, 128], replicated, may hold values from -0.25 to 0.25
- outproj: bfloat16 [1024, 1024], replicated, may hold values from -1 to 1
- gateproj: bfloat16 [1024, 2816], P(None, 'tensor'), may hold values from -0.1875 to 0.1875
- upproj: bfloat16 [1024, 2816], P(None, 'tensor'), may hold values from -0.1875 to 0.1875
- downproj: bfloat16 [2816, 1024], P('tensor'), may hold values from -0.109375 to 0.109375
Outputs:
- mixed: bfloat16 [4, 2048, 1024], P('dp', 'tensor')
- tokens_grad: bfloat16 [4, 2048, 1024], P('dp', 'tensor')
- attngain_grad: float32 [1024], replicated
- ffngain_grad: float32 [1024], replicated
- queryheads_grad: float32 [1024, 96], replicated
- querydims_grad: float32 [1024, 384], replicated
- keyheads_grad: float32 [1024, 32], replicated
- keydims_grad: float32 [1024, 128], replicated
- valueheads_grad: float32 [1024, 32], replicated
- valuedims_grad: float32 [1024, 128], replicated
- outproj_grad: float32 [1024, 1024], replicated
- gateproj_grad: float32 [1024, 2816], P(None, 'tensor')
- upproj_grad: float32 [1024, 2816], P(None, 'tensor')
- downproj_grad: float32 [2816, 1024], P('tensor')
Inputs may be any that keep to these rules, and one draw needn't show every extreme that they name: `segments`: within a row the numbers never fall and every number is one contiguous document; every row holds exactly 3 documents: one of exactly 1536 tokens, and the others of 128 to 384 tokens. `positions`: each token's place within its document: 0 at a document's first token, rising by one along it.
All inputs are finite; a program needn't handle non-finite values.
Results may differ from a plain program's by a relative error of at most 0.022.
The roundings to bfloat16 on the way count: a program that leaves them out, or rounds other values in their place, can miss the bound.
Values may be sent and summed in bfloat16 or wider, within the bound.
No kernel may reach another device: no remote copies, remote signals or barrier semaphores. Data moves between devices by JAX's collectives and lax.ppermute only.
A program may use at most 256 MiB of HBM per device.

v0:
```python
import math

import jax
import jax.numpy as jnp
from jax import lax
from jax.sharding import PartitionSpec as P

HEADS = 16
HEAD_DIM = 64
QRANK = 6
KRANK = 2


highest = lax.Precision.HIGHEST
epsilon = 1e-06


def contract(left, right, left_dim, right_dim):
    return lax.dot_general(
        left, right, (((left_dim,), (right_dim,)), ((), ())), preferred_element_type=jnp.float32
    )


def angle_tables(places, width):
    half = width // 2
    freqs = 10000.0 ** (-jnp.arange(half, dtype=jnp.float32) * 2.0 / width)
    angles = places.astype(jnp.float32)[:, None] * freqs[None, :]
    return (jnp.cos(angles)[:, None, :], jnp.sin(angles)[:, None, :])


def rotate(values, cosine, sine, sign):
    half = values.shape[-1] // 2
    first = values[..., :half]
    second = values[..., half:]
    return jnp.concatenate(
        [first * cosine - sign * second * sine, second * cosine + sign * first * sine], axis=-1
    )


def norm_back(grad_out, normed, inverse, gain):
    scaled = grad_out * gain
    gain_part = jnp.sum(grad_out * normed, axis=0)
    grad_in = inverse * (scaled - normed * jnp.mean(scaled * normed, axis=-1, keepdims=True))
    return (grad_in, gain_part)


def body(
    tokens,
    cotangent,
    segments,
    positions,
    attngain,
    ffngain,
    queryheads,
    querydims,
    keyheads,
    keydims,
    valueheads,
    valuedims,
    outproj,
    gateproj,
    upproj,
    downproj,
):
    local = tokens[0].astype(jnp.float32)
    upstream = cotangent[0]
    length = local.shape[0]
    whole = length * lax.axis_size("tensor")
    offset = lax.axis_index("tensor") * length
    seg_row = segments[0]
    my_seg = lax.dynamic_slice_in_dim(seg_row, offset, length)
    my_pos = lax.dynamic_slice_in_dim(positions[0], offset, length)
    cosine, sine = angle_tables(my_pos, HEAD_DIM)
    qheads_width = HEADS * QRANK
    qdims_width = QRANK * HEAD_DIM
    kdims_width = KRANK * HEAD_DIM
    kheads_width = HEADS * KRANK
    edge_two = qheads_width + qdims_width
    edge_three = edge_two + kdims_width
    edge_four = edge_three + kdims_width
    edge_five = edge_four + kheads_width
    inverse_one = lax.rsqrt(jnp.mean(local * local, axis=-1, keepdims=True) + epsilon)
    normed_one = local * inverse_one
    input_one = (normed_one * attngain).astype(jnp.bfloat16)
    stacked_proj = jnp.concatenate(
        [queryheads, querydims, keydims, valuedims, keyheads, valueheads], axis=1
    )
    raw_factors = jnp.dot(input_one, stacked_proj, preferred_element_type=jnp.float32)
    qheads_low = raw_factors[:, :qheads_width].astype(jnp.bfloat16).reshape(length, HEADS, QRANK)
    qdims_low = rotate(
        raw_factors[:, qheads_width:edge_two].reshape(length, QRANK, HEAD_DIM), cosine, sine, 1.0
    ).astype(jnp.bfloat16)
    kdims_turned = rotate(
        raw_factors[:, edge_two:edge_three].reshape(length, KRANK, HEAD_DIM), cosine, sine, 1.0
    )
    factors = jnp.concatenate(
        [kdims_turned.reshape(length, kdims_width), raw_factors[:, edge_three:]], axis=1
    ).astype(jnp.bfloat16)
    gathered = lax.all_gather(factors, "tensor", axis=0, tiled=True)
    query = (
        jnp.einsum(
            "thr,trd->thd",
            qheads_low.astype(jnp.float32),
            qdims_low.astype(jnp.float32),
            precision=highest,
        )
        / QRANK
    ).astype(jnp.bfloat16)
    span = math.gcd(whole, 1024)
    begins = jnp.arange(whole // span, dtype=jnp.int32) * span
    query_index = offset + jnp.arange(length, dtype=jnp.int32)
    scale = HEAD_DIM ** (-0.5)

    def key_block(begin):
        piece = lax.dynamic_slice_in_dim(gathered, begin, span, 0).astype(jnp.float32)
        kdims_f = piece[:, :kdims_width].reshape(span, KRANK, HEAD_DIM)
        vdims_f = piece[:, kdims_width : 2 * kdims_width].reshape(span, KRANK, HEAD_DIM)
        kheads_f = piece[:, 2 * kdims_width : 2 * kdims_width + kheads_width].reshape(
            span, HEADS, KRANK
        )
        vheads_f = piece[:, 2 * kdims_width + kheads_width :].reshape(span, HEADS, KRANK)
        keys = (jnp.einsum("khr,krd->khd", kheads_f, kdims_f, precision=highest) / KRANK).astype(
            jnp.bfloat16
        )
        values = (jnp.einsum("khr,krd->khd", vheads_f, vdims_f, precision=highest) / KRANK).astype(
            jnp.bfloat16
        )
        key_seg = lax.dynamic_slice_in_dim(seg_row, begin, span)
        key_index = begin + jnp.arange(span, dtype=jnp.int32)
        allowed = (key_seg[None, :] == my_seg[:, None]) & (
            key_index[None, :] <= query_index[:, None]
        )
        scores = jnp.einsum("qhd,khd->hqk", query, keys, preferred_element_type=jnp.float32) * scale
        scores = jnp.where(allowed[None], scores, -1e30)
        return (scores, keys, values, (kdims_f, vdims_f, kheads_f, vheads_f))

    def stat_step(carry, begin):
        topmost, totals = carry
        scores = key_block(begin)[0]
        newtop = jnp.maximum(topmost, jnp.max(scores, axis=-1))
        totals = totals * jnp.exp(topmost - newtop) + jnp.sum(
            jnp.exp(scores - newtop[:, :, None]), axis=-1
        )
        return ((newtop, totals), None)

    start_stats = (
        jnp.full((HEADS, length), -1e30, jnp.float32),
        jnp.zeros((HEADS, length), jnp.float32),
    )
    (topmost, totals), unused = lax.scan(stat_step, start_stats, begins)
    logsum = topmost + jnp.log(totals)

    def value_step(accum, begin):
        scores, keys, values, parts = key_block(begin)
        probs = jnp.exp(scores - logsum[:, :, None]).astype(jnp.bfloat16)
        return (
            accum + jnp.einsum("hqk,khd->qhd", probs, values, preferred_element_type=jnp.float32),
            None,
        )

    attended, unused = lax.scan(
        value_step, jnp.zeros((length, HEADS, HEAD_DIM), jnp.float32), begins
    )
    attn_out = attended.reshape(length, HEADS * HEAD_DIM).astype(jnp.bfloat16)
    residual = local + jnp.dot(attn_out, outproj, preferred_element_type=jnp.float32)
    inverse_two = lax.rsqrt(jnp.mean(residual * residual, axis=-1, keepdims=True) + epsilon)
    normed_two = residual * inverse_two
    input_two = (normed_two * ffngain).astype(jnp.bfloat16)
    shard = gateproj.shape[1]
    whole_two = lax.all_gather(input_two, "tensor", axis=0, tiled=True)
    paired = jnp.concatenate([gateproj, upproj], axis=1)
    joined = jnp.dot(whole_two, paired, preferred_element_type=jnp.float32)
    gate = joined[:, :shard]
    upper = joined[:, shard:]
    sigma = jax.nn.sigmoid(gate)
    active = gate * sigma
    inner = (active * upper).astype(jnp.bfloat16)
    ffn_out = lax.psum_scatter(
        jnp.dot(inner, downproj, preferred_element_type=jnp.float32).astype(jnp.bfloat16),
        "tensor",
        scatter_dimension=0,
        tiled=True,
    ).astype(jnp.float32)
    piece = lax.all_gather(upstream, "tensor", axis=0, tiled=True)
    down_sum = contract(inner, piece, 0, 0)
    held = contract(piece, downproj, 1, 1)
    down_part = down_sum
    d_gate = (held * upper * sigma * (1.0 + gate * (1.0 - sigma))).astype(jnp.bfloat16)
    d_upper = (held * active).astype(jnp.bfloat16)
    d_paired = jnp.concatenate([d_gate, d_upper], axis=1)
    pair_part = contract(whole_two, d_paired, 0, 0)
    gate_part = pair_part[:, :shard]
    up_part = pair_part[:, shard:]
    d_norm_two = lax.psum_scatter(
        contract(d_paired, paired, 1, 1).astype(jnp.bfloat16),
        "tensor",
        scatter_dimension=0,
        tiled=True,
    ).astype(jnp.float32)
    gate_part, up_part, down_part = (
        lax.psum(gate_part.astype(jnp.bfloat16), "dp").astype(jnp.float32),
        lax.psum(up_part.astype(jnp.bfloat16), "dp").astype(jnp.float32),
        lax.psum(down_part.astype(jnp.bfloat16), "dp").astype(jnp.float32),
    )
    mixed = (residual + ffn_out).astype(jnp.bfloat16)
    grad_through, ffngain_part = norm_back(d_norm_two, normed_two, inverse_two, ffngain)
    d_residual = upstream.astype(jnp.float32) + grad_through
    d_res_low = d_residual.astype(jnp.bfloat16)
    outproj_part = contract(attn_out, d_res_low, 0, 0)
    d_attended = (
        contract(d_res_low, outproj, 1, 1).astype(jnp.bfloat16).reshape(length, HEADS, HEAD_DIM)
    )
    delta = jnp.einsum(
        "qhd,qhd->hq",
        d_attended.astype(jnp.float32),
        attn_out.reshape(length, HEADS, HEAD_DIM).astype(jnp.float32),
        precision=highest,
    )

    def back_step(d_query, begin):
        scores, keys, values, parts = key_block(begin)
        kdims_f, vdims_f, kheads_f, vheads_f = parts
        probs = jnp.exp(scores - logsum[:, :, None])
        probs_low = probs.astype(jnp.bfloat16)
        d_values = jnp.einsum(
            "hqk,qhd->khd", probs_low, d_attended, preferred_element_type=jnp.float32
        )
        d_probs = jnp.einsum("qhd,khd->hqk", d_attended, values, preferred_element_type=jnp.float32)
        d_scores = (probs * (d_probs - delta[:, :, None])).astype(jnp.bfloat16)
        d_query = (
            d_query
            + jnp.einsum("hqk,khd->qhd", d_scores, keys, preferred_element_type=jnp.float32) * scale
        )
        d_keys = (
            jnp.einsum("hqk,qhd->khd", d_scores, query, preferred_element_type=jnp.float32) * scale
        )
        d_kheads = jnp.einsum("khd,krd->khr", d_keys, kdims_f, precision=highest) / KRANK
        d_kdims = jnp.einsum("khd,khr->krd", d_keys, kheads_f, precision=highest) / KRANK
        d_vheads = jnp.einsum("khd,krd->khr", d_values, vdims_f, precision=highest) / KRANK
        d_vdims = jnp.einsum("khd,khr->krd", d_values, vheads_f, precision=highest) / KRANK
        terms = jnp.concatenate(
            [
                d_kdims.reshape(span, kdims_width),
                d_vdims.reshape(span, kdims_width),
                d_kheads.reshape(span, kheads_width),
                d_vheads.reshape(span, kheads_width),
            ],
            axis=1,
        )
        return (d_query, terms)

    d_query, term_blocks = lax.scan(
        back_step, jnp.zeros((length, HEADS, HEAD_DIM), jnp.float32), begins
    )
    key_terms = term_blocks.reshape(whole, term_blocks.shape[-1])
    key_grads = lax.psum_scatter(
        key_terms.astype(jnp.bfloat16), "tensor", scatter_dimension=0, tiled=True
    ).astype(jnp.float32)
    d_qheads = (
        jnp.einsum("thd,trd->thr", d_query, qdims_low.astype(jnp.float32), precision=highest)
        / QRANK
    )
    d_qdims = (
        jnp.einsum("thd,thr->trd", d_query, qheads_low.astype(jnp.float32), precision=highest)
        / QRANK
    )
    d_qdims = rotate(d_qdims, cosine, sine, -1.0)
    d_kdims = rotate(
        key_grads[:, :kdims_width].reshape(length, KRANK, HEAD_DIM), cosine, sine, -1.0
    )
    d_raw = jnp.concatenate(
        [
            d_qheads.reshape(length, qheads_width),
            d_qdims.reshape(length, qdims_width),
            d_kdims.reshape(length, kdims_width),
            key_grads[:, kdims_width:],
        ],
        axis=1,
    ).astype(jnp.bfloat16)
    proj_part = contract(input_one, d_raw, 0, 0)
    d_norm_one = contract(d_raw, stacked_proj, 1, 1)
    grad_first, attngain_part = norm_back(d_norm_one, normed_one, inverse_one, attngain)
    tokens_grad = (d_residual + grad_first).astype(jnp.bfloat16)
    proj_part, outproj_part, attngain_part, ffngain_part = lax.psum(
        (proj_part, outproj_part, attngain_part, ffngain_part), ("dp", "tensor")
    )
    return (
        mixed[None],
        tokens_grad[None],
        attngain_part,
        ffngain_part,
        proj_part[:, :qheads_width],
        proj_part[:, qheads_width:edge_two],
        proj_part[:, edge_four:edge_five],
        proj_part[:, edge_two:edge_three],
        proj_part[:, edge_five:],
        proj_part[:, edge_three:edge_four],
        outproj_part,
        gate_part,
        up_part,
        down_part,
    )


def solution(mesh):
    placed = (
        P("dp", "tensor", None),
        P("dp", "tensor", None),
        P("dp", None),
        P("dp", None),
        P(),
        P(),
        P(),
        P(),
        P(),
        P(),
        P(),
        P(),
        P(),
        P(None, "tensor"),
        P(None, "tensor"),
        P("tensor", None),
    )
    return jax.shard_map(
        body,
        mesh=mesh,
        in_specs=placed,
        out_specs=(
            P("dp", "tensor", None),
            P("dp", "tensor", None),
            P(),
            P(),
            P(),
            P(),
            P(),
            P(),
            P(),
            P(),
            P(),
            P(None, "tensor"),
            P(None, "tensor"),
            P("tensor", None),
        ),
        check_vma=False,
    )
```

profile of v0, /device:TPU:0, one launch (start us, length us, event | category | flops | bytes accessed | tf_op | source)
XLA Modules:
  0.0 1127.0 jit_solution(13615374108492912582)
XLA Ops:
  35.6 30.3 %all-gather.5.cloned.1.call-done = bf16[2048,320]{0,1:T(8,128)(2,1)} async-done(((bf16[256,320]{0,1:T(8,128)(2,1)}), bf16[2048,320]{0,1:T(8,128)(2,1)}) %all-gather.5.cloned.1.call-update) | async-done | bytes 1310736 | tf_op jit(solution)/shard_map/all_gather | solution.py:99
  65.9 53.4 %while.37 = (s32[]{:T(128)}, f32[16,256]{1,0:T(8,128)S(1)}, f32[16,256]{1,0:T(8,128)S(1)}, s32[2]{0:T(128)S(1)}, s32[2048]{0:T(1024)S(1)}, /*index=5*/s32[256]{0...) while((s32[]{:T(128)}, f32[16,256]{1,0:T(8,128)S(1)}, ...), condition=%wide.region_4.5_spmd.clone, body=%wide.region_1.4_spmd.clone.sunk | while | flops 573330688 | bytes 41065692 | solution.py:150
  83.4 9.1 exponential_reduce_fusion.2
  110.1 9.1 exponential_reduce_fusion.2
  119.3 60.2 %while.38 = (s32[]{:T(128)}, f32[256,16,64]{0,2,1:T(8,128)}, s32[2]{0:T(128)S(1)}, bf16[2048,320]{0,1:T(8,128)(2,1)}, s32[2048]{0:T(1024)S(1)}, /*index=5*/s32[2...) while((s32[]{:T(128)}, f32[256,16,64]{0,2,1:T(8,128)}, ...), condition=%wide.region_6.7_spmd.clone, body=%wide.region_5.6_spmd.clone.sunk | while | flops 1104413952 | bytes 17472868 | solution.py:161
  138.6 10.8 fusion.209
  168.4 11.1 fusion.209
  189.2 67.6 %all-gather.7.cloned.1.call-done = bf16[2048,1024]{1,0:T(8,128)(2,1)} async-done(((bf16[256,1024]{1,0:T(8,128)(2,1)}), bf16[2048,1024]{1,0:T(8,128)(2,1)}) %all-gather.7.cloned.1.call-update) | async-done | bytes 4194320 | tf_op jit(solution)/shard_map/all_gather | solution.py:170
  256.7 8.3 fusion.107
  265.1 65.2 %all-gather.9.cloned.1.call-done = bf16[1,2048,1024]{2,1,0:T(8,128)(2,1)} async-done(((bf16[1,256,1024]{2,1,0:T(8,128)(2,1)}), bf16[1,2048,1024]{2,1,0:T(8,128)(2,1)}) %all-gather.9.cloned.1.call-update) | async-done | bytes 4194320 | tf_op jit(solution)/shard_map/all_gather | solution.py:184
  330.2 8.0 multiply_convert_fusion.9
  352.1 81.2 %reduce-scatter.6.cloned.1.call-done = bf16[256,1024]{1,0:T(8,128)(2,1)} async-done(((bf16[2048,1024]{1,0:T(8,128)(2,1)}), bf16[256,1024]{1,0:T(8,128)(2,1)}) %reduce-scatter.6.cloned.1.call-update) | async-done | bytes 524304 | tf_op jit(solution)/shard_map/reduce_scatter | solution.py:194
  435.7 89.0 %reduce-scatter.4.cloned.1.call-done = bf16[256,1024]{1,0:T(8,128)(2,1)} async-done(((bf16[2048,1024]{1,0:T(8,128)(2,1)}), bf16[256,1024]{1,0:T(8,128)(2,1)}) %reduce-scatter.4.cloned.1.call-update) | async-done | bytes 524304 | tf_op jit(solution)/shard_map/reduce_scatter | solution.py:178
  531.7 273.3 %while.39 = (s32[]{:T(128)}, f32[256,16,64]{0,2,1:T(8,128)}, bf16[2,1024,320]{1,2,0:T(8,128)(2,1)}, s32[2]{0:T(128)S(1)}, bf16[2048,320]{0,1:T(8,128)(2,1)}, /*i...) while((s32[]{:T(128)}, f32[256,16,64]{0,2,1:T(8,128)}, ...), condition=%wide.region_12.13_spmd.clone, body=%wide.region_11.12_spmd.clone.sunk | while | flops 2847540480 | bytes 251862432 | solution.py:252
  580.8 10.5 fusion.232
  591.3 10.8 fusion.234
  602.1 11.9 %fusion.236 = f32[1024,16,64]{0,2,1:T(8,128)} fusion(bf16[256,16,64]{0,2,1:T(8,128)(2,1)} %get-tuple-element.938, f32[16,1024,256]{2,1,0:T(8,128)} %fusion.232, f32[16,256]{1,0:T(8,128)S(1)} %get-tuple-element.937, pred[256,1024]{0,1:T(8,128)(4,1)S(1)} %compare_and_fusion.8), kind=kOutput, calls=%fused_computation.44.clone.1 | convolution fusion | flops 553648128 | bytes 21774336 | tf_op jit(solution)/shard_map/while/body/eval_jaxpr/hqk,qhd->khd/dot_general | solution.py:225
  625.9 8.1 copy.345
  634.0 7.4 convolution_multiply_fusion.13
  649.1 8.1 copy.343
  657.2 7.4 convolution_multiply_fusion.12
  702.8 10.5 fusion.232
  713.2 10.8 fusion.234
  724.0 11.9 %fusion.236 = f32[1024,16,64]{0,2,1:T(8,128)} fusion(bf16[256,16,64]{0,2,1:T(8,128)(2,1)} %get-tuple-element.938, f32[16,1024,256]{2,1,0:T(8,128)} %fusion.232, f32[16,256]{1,0:T(8,128)S(1)} %get-tuple-element.937, pred[256,1024]{0,1:T(8,128)(4,1)S(1)} %compare_and_fusion.8), kind=kOutput, calls=%fused_computation.44.clone.1 | convolution fusion | flops 553648128 | bytes 21774336 | tf_op jit(solution)/shard_map/while/body/eval_jaxpr/hqk,qhd->khd/dot_general | solution.py:225
  736.0 7.4 fusion.235
  748.1 8.1 copy.345
  756.2 7.4 convolution_multiply_fusion.13
  771.2 8.1 copy.343
  835.8 37.1 %reduce-scatter.8.cloned.1.call-done = bf16[256,320]{0,1:T(8,128)(2,1)} async-done(((bf16[2048,320]{0,1:T(8,128)(2,1)}), bf16[256,320]{0,1:T(8,128)(2,1)}) %reduce-scatter.8.cloned.1.call-update) | async-done | bytes 163856 | tf_op jit(solution)/shard_map/reduce_scatter | solution.py:256
  877.3 50.8 %all-reduce.8.cloned.1.call-done = (bf16[1024,352]{0,1:T(8,128)(2,1)}, bf16[1024,352]{0,1:T(8,128)(2,1)}, bf16[352,1024]{1,0:T(8,128)(2,1)}) async-done(((bf16[1024,352]{0,1:T(8,128)(2,1)}, bf16[1024,352]{0,1:T(8,128)(2,1)}, bf16[352,1024]{1,0:T(8,128)(2,1)}), (bf16[1024,352]{0,1:T(8,128)(2,1)}, bf16[1024,352]{0,1:T(8,128)(2,1)}, bf16[352,1024]{1,0:T(8,128)(2,1)})) %all-reduce.8.cloned.1.call-update) | async-done | bytes 2162704 | tf_op jit(solution)/shard_map/psum | solution.py:201
  935.2 41.3 %all-reduce = (f32[1024]{0:T(1024)}, f32[1024]{0:T(1024)}) all-reduce(f32[1024]{0:T(1024)S(1)} %get-tuple-element.498, f32[1024]{0:T(1024)S(1)} %copy-done.36), channel_id=1, replica_groups=mesh['dp'=4,'tensor'=8] {'dp','tensor'}, use_global_device_ids=true, to_apply=%region_16.17 | all-reduce | flops 2048 | bytes 16384 | tf_op jit(solution)/shard_map/psum | solution.py:284
  977.6 127.5 %all-reduce.6.cloned.1.call-done = (f32[1024,800]{0,1:T(8,128)}, f32[1024,1024]{1,0:T(8,128)}) async-done(((f32[1024,800]{0,1:T(8,128)}, f32[1024,1024]{1,0:T(8,128)}), (f32[1024,800]{0,1:T(8,128)}, f32[1024,1024]{1,0:T(8,128)})) %all-reduce.6.cloned.1.call-update) | async-done | bytes 7471120 | tf_op jit(solution)/shard_map/psum | solution.py:284
  (320 shorter events, 295.6 us)
Async XLA Ops:
  7.2 174.5 %copy-start = (bf16[1024,1024]{1,0:T(8,128)(2,1)S(1)}, bf16[1024,1024]{1,0:T(8,128)(2,1)}, u32[]{:S(2)}) copy-start(bf16[1024,1024]{1,0:T(8,128)(2,1)} %param.34) | copy-start | bytes 6291460
  7.2 8.8 copy-start.13
  7.2 8.8 copy-start.34
  7.2 58.6 %all-gather.5.cloned.1.call-start = ((), (), s32[]{:S(2)}) async-start(), calls=%async_computation.3 | async-start | bytes 1474560 | tf_op jit(solution)/shard_map/all_gather | solution.py:99
  8.7 9.7 copy-start.37
  20.7 10.0 copy-start.29
  21.4 235.3 %all-gather.7.cloned.1.call-start = ((), (), s32[]{:S(2)}) async-start(), calls=%async_computation.4 | async-start | bytes 4718592 | tf_op jit(solution)/shard_map/all_gather | solution.py:170
  27.5 8.0 copy-start.31
  185.5 144.8 %all-gather.9.cloned.1.call-start = ((), (), s32[]{:S(2)}) async-start(), calls=%async_computation.8 | async-start | bytes 4718592 | tf_op jit(solution)/shard_map/all_gather | solution.py:184
  186.2 247.0 %reduce-scatter.6.cloned.1.call-start = ((), (), s32[]{:S(2)}) async-start(), calls=%async_computation.6 | async-start | bytes 4718592 | tf_op jit(solution)/shard_map/reduce_scatter | solution.py:194
  189.2 141.1 %copy-start.40 = (bf16[352,1024]{1,0:T(8,128)(2,1)S(1)}, bf16[352,1024]{1,0:T(8,128)(2,1)}, u32[]{:S(2)}) copy-start(bf16[352,1024]{1,0:T(8,128)(2,1)} %param.37) | copy-start | bytes 2162692
  346.2 178.5 %reduce-scatter.4.cloned.1.call-start = ((), (), s32[]{:S(2)}) async-start(), calls=%async_computation.5 | async-start | bytes 4718592 | tf_op jit(solution)/shard_map/reduce_scatter | solution.py:178
  352.0 172.7 %copy-start.24 = (bf16[1,256,1024]{2,1,0:T(8,128)(2,1)S(1)}, bf16[1,256,1024]{2,1,0:T(8,128)(2,1)}, u32[]{:S(2)}) copy-start(bf16[1,256,1024]{2,1,0:T(8,128)(2,1)} %param.23) | copy-start | bytes 1572868
  352.0 520.9 %reduce-scatter.8.cloned.1.call-start = ((), (), s32[]{:S(2)}) async-start(), calls=%async_computation.7 | async-start | bytes 1474560 | tf_op jit(solution)/shard_map/reduce_scatter | solution.py:256
  531.7 275.9 %copy-start.32 = (f32[256,32]{0,1:T(8,128)S(1)}, f32[256,32]{0,1:T(8,128)}, u32[]{:S(2)}) copy-start(f32[256,32]{0,1:T(8,128)} %get-tuple-element.598) | copy-start | bytes 98308
  580.8 10.5 copy-start.5
  614.0 7.2 copy-start.4
  634.0 7.4 copy-start.2
  657.2 7.4 copy-start.3
  702.8 10.5 copy-start.5
  736.0 7.4 copy-start.4
  756.2 7.4 copy-start.2
  779.4 7.4 copy-start.3
  807.5 120.6 %all-reduce.8.cloned.1.call-start = ((), (), s32[]{:S(2)}) async-start(), calls=%async_computation.10 | async-start | bytes 4325376 | tf_op jit(solution)/shard_map/psum | solution.py:201
  807.7 7.6 copy-start.39
  807.7 7.6 copy-start.41
  817.8 287.3 %all-reduce.6.cloned.1.call-start = ((), (), s32[]{:S(2)}) async-start(), calls=%async_computation.9 | async-start | bytes 14942208 | tf_op jit(solution)/shard_map/psum | solution.py:284
  820.3 8.5 copy-start.25
  830.3 44.3 %copy-start.30 = (f32[256,32]{0,1:T(8,128)S(1)}, f32[256,32]{0,1:T(8,128)}, u32[]{:S(2)}) copy-start(f32[256,32]{0,1:T(8,128)} %copy-done.29) | copy-start | bytes 98308
  830.3 44.4 %copy-start.14 = (bf16[1,256,1024]{2,1,0:T(8,128)(2,1)S(1)}, bf16[1,256,1024]{2,1,0:T(8,128)(2,1)}, u32[]{:S(2)}) copy-start(bf16[1,256,1024]{2,1,0:T(8,128)(2,1)} %param.22) | copy-start | bytes 1572868
  830.3 44.4 %copy-start.35 = (f32[1024]{0:T(1024)S(1)}, f32[1024]{0:T(1024)}, u32[]{:S(2)}) copy-start(f32[1024]{0:T(1024)} %param.26) | copy-start | bytes 12292
  830.3 44.4 %copy-start.38 = (f32[256]{0:T(256)S(1)}, f32[256]{0:T(256)}, u32[]{:S(2)}) copy-start(f32[256]{0:T(256)} %copy-done.37) | copy-start | bytes 3076
  (27 other events, 94.8 us)
Sparse Core Ops, SparseCore 0:
  21.5 44.2 all-gather.4
  185.6 71.1 all-gather.6
  258.9 71.3 all-gather.8
  346.3 86.8 reduce-scatter.5
  436.7 87.9 reduce-scatter.3
  807.6 65.2 reduce-scatter.7
  876.6 51.4 all-reduce.7
  934.7 170.3 all-reduce.5
where the time goes:
time: 1140 us; the launch traced here: 1130 us
  waiting for transfers between devices  549 us (48%)
  matrix products  279 us (24%)
  local copies, waits for them, and re-layouts  149 us (13%)
  other arithmetic  50.6 us (4%)
  loops' own time  41.6 us (4%)
  blocking collectives  41.3 us (4%)
  between operations  14.9 us (1%)
    psum x1, waiting for transfers between devices, body(): lax.psum((proj_part, outproj_part, attngain_part, ffngain_part), ('dp', '...  127 us
    reduce_scatter x1, waiting for transfers between devices, body(): lax.psum_scatter(jnp.dot(inner, downproj, preferred_element_type=jnp.floa...  89 us
    reduce_scatter x1, waiting for transfers between devices, body(): lax.psum_scatter(contract(d_paired, paired, 1, 1).astype(jnp.bfloat16), '...  81.2 us
    all_gather x1, waiting for transfers between devices, body(): whole_two = lax.all_gather(input_two, 'tensor', axis=0, tiled=True)  67.6 us
    all_gather x1, waiting for transfers between devices, body(): piece = lax.all_gather(upstream, 'tensor', axis=0, tiled=True)  65.2 us
    psum x1, waiting for transfers between devices, body(): lax.psum(gate_part.astype(jnp.bfloat16), 'dp').astype(jnp.float32)  50.8 us
    psum x1, blocking collectives, body(): lax.psum((proj_part, outproj_part, attngain_part, ffngain_part), ('dp', '...  41.3 us
    reduce_scatter x1, waiting for transfers between devices, body(): lax.psum_scatter(key_terms.astype(jnp.bfloat16), 'tensor', scatter_dimens...  37.1 us
  transfers between devices with their start and end apart: 8, of which 8 were waited for; matrix products, arithmetic and copies ran while one was open for 6% of the time, Pallas kernels for 0%

commit v1 on v0

v1 whole, which is shorter than its diff:
```python
import functools
import jax
import jax.numpy as jnp
from jax import lax
from jax.experimental import pallas as pl
from jax.experimental.pallas import tpu as pltpu

from jax.sharding import PartitionSpec as P

HEADS = 16
HEAD_DIM = 64
QRANK = 6
KRANK = 2
PAIRS = HEADS // 2
QHW = HEADS * QRANK
QDW = QRANK * HEAD_DIM
KDW = KRANK * HEAD_DIM
KHW = HEADS * KRANK
FACW = 2 * KDW + 2 * KHW
QFW = QHW + QDW
LOG2E = 1.4426950408889634
EPS = 1e-06
BF = jnp.bfloat16
F32 = jnp.float32


def mm(a, b, ca=1, cb=0):
    return lax.dot_general(a, b, (((ca,), (cb,)), ((), ())), preferred_element_type=F32)


def expand_pair(bk0, bk1, rows):
    first = rows[0] * bk0 + rows[1] * bk1
    second = rows[2] * bk0 + rows[3] * bk1
    return jnp.concatenate([first, second], axis=0) * (1.0 / KRANK)


def query_pair(qfac_ref, aq_s, pair):
    halves = []
    for h in range(2):
        acc = None
        for r in range(QRANK):
            row = aq_s[pl.ds(pair * (2 * QRANK) + h * QRANK + r, 1), :]
            term = row * qfac_ref[QHW + r * HEAD_DIM : QHW + (r + 1) * HEAD_DIM, :].astype(F32)
            acc = term if acc is None else acc + term
        halves.append(acc * (1.0 / QRANK))
    return jnp.concatenate(halves, axis=0).astype(BF)


def fill_tables(scal_ref, qfac_ref, fac_ref, start_ref, aq_s, kv_s, bias_s):
    length = qfac_ref.shape[1]
    me = scal_ref[1]
    aq_s[...] = qfac_ref[0:QHW, :].astype(F32)
    row = lax.broadcasted_iota(jnp.int32, (length, length), 0) + me * length
    column = lax.broadcasted_iota(jnp.int32, (length, length), 1)
    begin = start_ref[...]

    def fill(c, carry):
        kv_s[c] = fac_ref[c, 2 * KDW :, :].astype(F32)
        key = column + c * length
        keep = (key >= begin) & (key <= row)
        bias_s[c] = jnp.where(keep, 0.0, -1e30)
        return carry

    lax.fori_loop(scal_ref[0], me + 1, fill, 0)


def key_pair(fac_ref, kv_s, c, pair, which):
    base = which * KDW
    b0 = fac_ref[c, base : base + HEAD_DIM, :].astype(F32)
    b1 = fac_ref[c, base + HEAD_DIM : base + 2 * HEAD_DIM, :].astype(F32)
    rows = [kv_s[c, pl.ds(which * KHW + pair * 4 + j, 1), :] for j in range(4)]
    return expand_pair(b0, b1, rows), b0, b1, rows


def forward_kernel(scal_ref, qfac_ref, fac_ref, start_ref, o_ref, lse_ref, aq_s, kv_s, bias_s, s_s):
    pair = pl.program_id(0)
    length = qfac_ref.shape[1]
    lo, me = scal_ref[0], scal_ref[1]

    @pl.when(pair == 0)
    def _():
        fill_tables(scal_ref, qfac_ref, fac_ref, start_ref, aq_s, kv_s, bias_s)

    query = jnp.transpose(query_pair(qfac_ref, aq_s, pair).astype(F32)) * (HEAD_DIM**-0.5)
    low_half = lax.broadcasted_iota(jnp.int32, (length, 2 * HEAD_DIM), 1) < HEAD_DIM
    queries = [
        jnp.where(low_half, query, 0.0).astype(BF),
        jnp.where(low_half, 0.0, query).astype(BF),
    ]
    lanes = 128
    pieces = length // lanes

    def score(c, tops):
        keys = key_pair(fac_ref, kv_s, c, pair, 0)[0].astype(BF)
        bias = bias_s[c]
        new = []
        for h in range(2):
            s = mm(queries[h], keys) * LOG2E + bias
            s_s[h, c] = s
            top = tops[h]
            for i in range(pieces):
                top = jnp.maximum(top, s[:, i * lanes : (i + 1) * lanes])
            new.append(top)
        return tuple(new)

    start = jnp.full((length, lanes), -1e30, F32)
    tops = lax.fori_loop(lo, me + 1, score, (start, start))
    tops = [jnp.max(top, axis=1, keepdims=True) for top in tops]

    def value(c, carry):
        values = key_pair(fac_ref, kv_s, c, pair, 1)[0].astype(BF)
        new = []
        for h in range(2):
            p = jnp.exp2(s_s[h, c] - tops[h])
            total = carry[2 * h]
            for i in range(pieces):
                total = total + p[:, i * lanes : (i + 1) * lanes]
            new += [total, carry[2 * h + 1] + mm(p.astype(BF), values, 1, 1)]
        return tuple(new)

    zero = jnp.zeros((length, lanes), F32)
    wide = jnp.zeros((length, 2 * HEAD_DIM), F32)
    done = lax.fori_loop(lo, me + 1, value, (zero, wide, zero, wide))
    outs = []
    for h in range(2):
        total = jnp.sum(done[2 * h], axis=1, keepdims=True)
        outs.append(done[2 * h + 1] / total)
        lse_ref[h] = jnp.broadcast_to(tops[h] + jnp.log2(total), (length, lanes))
    o_ref[...] = jnp.where(low_half, outs[0], outs[1]).astype(BF)


def full(shape):
    return pl.BlockSpec(shape, lambda p, s: (0,) * len(shape))


def attention_forward(scal, qfac, fac, start):
    n, unused, length = fac.shape
    return pl.pallas_call(
        forward_kernel,
        out_shape=(
            jax.ShapeDtypeStruct((length, HEADS * HEAD_DIM), BF),
            jax.ShapeDtypeStruct((HEADS, length, 128), F32),
        ),
        grid_spec=pltpu.PrefetchScalarGridSpec(
            num_scalar_prefetch=1,
            grid=(PAIRS,),
            in_specs=[full(qfac.shape), full(fac.shape), full(start.shape)],
            out_specs=[
                pl.BlockSpec((length, 2 * HEAD_DIM), lambda p, s: (0, p)),
                pl.BlockSpec((2, length, 128), lambda p, s: (p, 0, 0)),
            ],
            scratch_shapes=[
                pltpu.VMEM((QHW, length), F32),
                pltpu.VMEM((n, 2 * KHW, length), F32),
                pltpu.VMEM((n, length, length), F32),
                pltpu.VMEM((2, n, length, length), F32),
            ],
        ),
        compiler_params=pltpu.CompilerParams(
            dimension_semantics=("arbitrary",), vmem_limit_bytes=58 << 20
        ),
        name="attention_forward",
    )(scal, qfac, fac, start)


def backward_kernel(
    scal_ref,
    qfac_ref,
    fac_ref,
    start_ref,
    o_ref,
    do_ref,
    lse_ref,
    cos_ref,
    sin_ref,
    terms_ref,
    dq_ref,
    aq_s,
    kv_s,
    bias_s,
    acc_s,
    heads_s,
    dbq_s,
    daq_s,
):
    pair = pl.program_id(0)
    length = qfac_ref.shape[1]
    n = fac_ref.shape[0]
    lo, me = scal_ref[0], scal_ref[1]
    pieces = length // 128

    @pl.when(pair == 0)
    def _():
        fill_tables(scal_ref, qfac_ref, fac_ref, start_ref, aq_s, kv_s, bias_s)
        dbq_s[...] = jnp.zeros_like(dbq_s)

        def clear(c, carry):
            acc_s[c] = jnp.zeros((2 * KDW, length), F32)
            return carry

        lax.fori_loop(lo, me + 1, clear, 0)

    query_t = query_pair(qfac_ref, aq_s, pair).astype(F32) * (HEAD_DIM**-0.5)
    query = jnp.transpose(query_t)
    query_t = query_t.astype(BF)
    do = do_ref[...].astype(F32)
    do_t = jnp.transpose(do).astype(BF)
    low_half = lax.broadcasted_iota(jnp.int32, (length, 2 * HEAD_DIM), 1) < HEAD_DIM
    product = do * o_ref[...].astype(F32)
    queries, grads, deltas, stats = [], [], [], []
    for h in range(2):
        keep = low_half if h == 0 else jnp.logical_not(low_half)
        queries.append(jnp.where(keep, query, 0.0).astype(BF))
        grads.append(jnp.where(keep, do, 0.0).astype(BF))
        deltas.append(jnp.sum(jnp.where(keep, product, 0.0), axis=1, keepdims=True))
        stats.append(lse_ref[h])

    def step(c, dqs):
        keys, kb0, kb1, krows = key_pair(fac_ref, kv_s, c, pair, 0)
        values, vb0, vb1, vrows = key_pair(fac_ref, kv_s, c, pair, 1)
        keys, values = keys.astype(BF), values.astype(BF)
        bias = bias_s[c]
        new, sums, rows = [], [None] * 4, []
        for h in range(2):
            s = mm(queries[h], keys) * LOG2E + bias
            lse = jnp.concatenate([stats[h]] * pieces, axis=1)
            p = jnp.exp2(s - lse)
            dp = mm(grads[h], values)
            ds = (p * (dp - deltas[h])).astype(BF)
            pb = p.astype(BF)
            new.append(dqs[h] + mm(ds, keys, 1, 1))
            half = slice(h * HEAD_DIM, (h + 1) * HEAD_DIM)
            dk = mm(query_t[half, :], ds)
            dv = mm(do_t[half, :], pb)
            for which, d, b0, b1, a in ((0, dk, kb0, kb1, krows), (1, dv, vb0, vb1, vrows)):
                for r, b in ((0, b0), (1, b1)):
                    term = d * a[2 * h + r]
                    k = 2 * which + r
                    sums[k] = term if sums[k] is None else sums[k] + term
                    rows.append((which * 4 + 2 * h + r, jnp.sum(d * b, axis=0, keepdims=True)))
        for k in range(4):
            part = slice(k * HEAD_DIM, (k + 1) * HEAD_DIM)
            acc_s[c, part, :] = acc_s[c, part, :] + sums[k]
        for k, row in rows:
            where = (k // 4) * KHW + pair * 4 + k % 4
            heads_s[c, pl.ds(where, 1), :] = row
        return tuple(new)

    zero = jnp.zeros((length, 2 * HEAD_DIM), F32)
    dqs = lax.fori_loop(lo, me + 1, step, (zero, zero))
    dq_t = jnp.transpose(jnp.where(low_half, dqs[0], dqs[1])) * (HEAD_DIM**-0.5 / QRANK)
    for h in range(2):
        d = dq_t[h * HEAD_DIM : (h + 1) * HEAD_DIM, :]
        for r in range(QRANK):
            part = slice(r * HEAD_DIM, (r + 1) * HEAD_DIM)
            b = qfac_ref[QHW + r * HEAD_DIM : QHW + (r + 1) * HEAD_DIM, :].astype(F32)
            k = pl.ds(pair * (2 * QRANK) + h * QRANK + r, 1)
            daq_s[k, :] = jnp.sum(d * b, axis=0, keepdims=True)
            dbq_s[part, :] = dbq_s[part, :] + d * aq_s[k, :]

    @pl.when(pair == PAIRS - 1)
    def _():
        cosine, sine = cos_ref[...], sin_ref[...]
        half = HEAD_DIM // 2
        dq_ref[0:QHW, :] = daq_s[...].astype(BF)
        for r in range(QRANK):
            first = dbq_s[r * HEAD_DIM : r * HEAD_DIM + half, :]
            second = dbq_s[r * HEAD_DIM + half : (r + 1) * HEAD_DIM, :]
            turned = jnp.concatenate(
                [first * cosine + second * sine, second * cosine - first * sine], axis=0
            )
            dq_ref[QHW + r * HEAD_DIM : QHW + (r + 1) * HEAD_DIM, :] = turned.astype(BF)

        def flush(c, carry):
            inside = (c >= lo) & (c <= me)

            @pl.when(inside)
            def _():
                terms_ref[c, 0 : 2 * KDW, :] = (acc_s[c] * (1.0 / KRANK)).astype(BF)
                terms_ref[c, 2 * KDW :, :] = (heads_s[c] * (1.0 / KRANK)).astype(BF)

            @pl.when(jnp.logical_not(inside))
            def _():
                terms_ref[c] = jnp.zeros((FACW, length), BF)

            return carry

        lax.fori_loop(0, n, flush, 0)


def attention_backward(scal, qfac, fac, start, o, do, lse, cosine, sine):
    n, unused, length = fac.shape
    return pl.pallas_call(
        backward_kernel,
        out_shape=(
            jax.ShapeDtypeStruct((n, FACW, length), BF),
            jax.ShapeDtypeStruct((QFW, length), BF),
        ),
        grid_spec=pltpu.PrefetchScalarGridSpec(
            num_scalar_prefetch=1,
            grid=(PAIRS,),
            in_specs=[
                full(qfac.shape),
                full(fac.shape),
                full(start.shape),
                pl.BlockSpec((length, 2 * HEAD_DIM), lambda p, s: (0, p)),
                pl.BlockSpec((length, 2 * HEAD_DIM), lambda p, s: (0, p)),
                pl.BlockSpec((2, length, 128), lambda p, s: (p, 0, 0)),
                full(cosine.shape),
                full(sine.shape),
            ],
            out_specs=[full((n, FACW, length)), full((QFW, length))],
            scratch_shapes=[
                pltpu.VMEM((QHW, length), F32),
                pltpu.VMEM((n, 2 * KHW, length), F32),
                pltpu.VMEM((n, length, length), F32),
                pltpu.VMEM((n, 2 * KDW, length), F32),
                pltpu.VMEM((n, 2 * KHW, length), F32),
                pltpu.VMEM((QDW, length), F32),
                pltpu.VMEM((QHW, length), F32),
            ],
        ),
        compiler_params=pltpu.CompilerParams(
            dimension_semantics=("arbitrary",), vmem_limit_bytes=58 << 20
        ),
        name="attention_backward",
    )(scal, qfac, fac, start, o, do, lse, cosine, sine)


def norm_of(values):
    inverse = lax.rsqrt(jnp.mean(values * values, axis=-1, keepdims=True) + EPS)
    return values * inverse, inverse


def turn(values, cosine, sine, sign):
    half = HEAD_DIM // 2
    parts = []
    for r in range(values.shape[0] // HEAD_DIM):
        first = values[r * HEAD_DIM : r * HEAD_DIM + half, :]
        second = values[r * HEAD_DIM + half : (r + 1) * HEAD_DIM, :]
        parts.append(first * cosine - sign * second * sine)
        parts.append(second * cosine + sign * first * sine)
    return jnp.concatenate(parts, axis=0)


def enter_kernel(x_ref, gain_ref, qh, qd, kh, kd, vh, vd, cos_ref, sin_ref, xa_ref, qfac_ref, fac_ref):
    normed = norm_of(x_ref[...].astype(F32))[0]
    xa = (normed * gain_ref[...]).astype(BF)
    xa_ref[...] = xa
    cosine, sine = cos_ref[...], sin_ref[...]
    kdims = turn(jnp.transpose(mm(xa, kd[...])), cosine, sine, 1.0)
    fac_ref[0:KDW, :] = kdims.astype(BF)
    fac_ref[KDW : 2 * KDW, :] = jnp.transpose(mm(xa, vd[...])).astype(BF)
    fac_ref[2 * KDW : 2 * KDW + KHW, :] = jnp.transpose(mm(xa, kh[...])).astype(BF)
    fac_ref[2 * KDW + KHW :, :] = jnp.transpose(mm(xa, vh[...])).astype(BF)
    qfac_ref[0:QHW, :] = jnp.transpose(mm(xa, qh[...])).astype(BF)
    qdims = turn(jnp.transpose(mm(xa, qd[...])), cosine, sine, 1.0)
    qfac_ref[QHW:, :] = qdims.astype(BF)


def enter(x, gain, weights, cosine, sine):
    length, width = x.shape
    return pl.pallas_call(
        enter_kernel,
        out_shape=(
            jax.ShapeDtypeStruct((length, width), BF),
            jax.ShapeDtypeStruct((QFW, length), BF),
            jax.ShapeDtypeStruct((FACW, length), BF),
        ),
        compiler_params=pltpu.CompilerParams(vmem_limit_bytes=40 << 20),
        name="enter",
    )(x, gain, *weights, cosine, sine)


def leave_query_kernel(xa_ref, dq_ref, fgain_ref, out_ref):
    xa_t = jnp.transpose(xa_ref[...].astype(F32)).astype(BF)
    d = dq_ref[...].astype(F32)
    out_ref[:, 0:QHW] = mm(xa_t, d[0:QHW, :].astype(BF), 1, 1).astype(BF)
    out_ref[:, QHW:QFW] = mm(xa_t, d[QHW:, :].astype(BF), 1, 1).astype(BF)
    out_ref[:, QFW:] = jnp.transpose(jnp.concatenate([fgain_ref[...]] * (512 - QFW), axis=0)).astype(BF)


def leave_key_kernel(
    x_ref, xa_ref, gain_ref, dres_ref, dq_ref, kg_ref, cos_ref, sin_ref, qh, qd, kh, kd, vh, vd, tg_ref, out_ref
):
    normed, inverse = norm_of(x_ref[...].astype(F32))
    g = kg_ref[...]
    dkd = turn(g[0:KDW, :], cos_ref[...], sin_ref[...], -1.0)
    d_kd = jnp.transpose(dkd).astype(BF)
    d_vd = jnp.transpose(g[KDW : 2 * KDW, :]).astype(BF)
    d_kh = jnp.transpose(g[2 * KDW : 2 * KDW + KHW, :]).astype(BF)
    d_vh = jnp.transpose(g[2 * KDW + KHW :, :]).astype(BF)
    dq = dq_ref[...].astype(F32)
    d_qh = jnp.transpose(dq[0:QHW, :]).astype(BF)
    d_qd = jnp.transpose(dq[QHW:, :]).astype(BF)
    xa_t = jnp.transpose(xa_ref[...].astype(F32)).astype(BF)
    dxa = mm(d_qd, qd[...], 1, 1) + mm(d_qh, qh[...], 1, 1)
    dxa = dxa + mm(d_kd, kd[...], 1, 1) + mm(d_vd, vd[...], 1, 1)
    dxa = dxa + mm(d_kh, kh[...], 1, 1) + mm(d_vh, vh[...], 1, 1)
    scaled = dxa * gain_ref[...]
    product = dxa * normed
    mean = jnp.mean(scaled * normed, axis=-1, keepdims=True)
    tg_ref[...] = (dres_ref[...] + inverse * (scaled - normed * mean)).astype(BF)
    gain_part = jnp.sum(product, axis=0, keepdims=True)
    out_ref[:, 0:KDW] = mm(xa_t, d_kd).astype(BF)
    out_ref[:, KDW : 2 * KDW] = mm(xa_t, d_vd).astype(BF)
    out_ref[:, 2 * KDW : 2 * KDW + KHW] = mm(xa_t, d_kh).astype(BF)
    out_ref[:, 2 * KDW + KHW : FACW] = mm(xa_t, d_vh).astype(BF)
    out_ref[:, FACW:] = jnp.transpose(jnp.concatenate([gain_part] * (384 - FACW), axis=0)).astype(BF)


def leave_query(xa, dq, fgain):
    width = xa.shape[1]
    return pl.pallas_call(
        leave_query_kernel,
        out_shape=jax.ShapeDtypeStruct((width, 512), BF),
        compiler_params=pltpu.CompilerParams(vmem_limit_bytes=40 << 20),
        name="leave_query",
    )(xa, dq, fgain)


def leave_key(x, xa, gain, dres, dq, kg, cosine, sine, weights):
    length, width = x.shape
    return pl.pallas_call(
        leave_key_kernel,
        out_shape=(
            jax.ShapeDtypeStruct((length, width), BF),
            jax.ShapeDtypeStruct((width, 384), BF),
        ),
        compiler_params=pltpu.CompilerParams(vmem_limit_bytes=40 << 20),
        name="leave_key",
    )(x, xa, gain, dres, dq, kg, cosine, sine, *weights)


class Grid:
    def __init__(self, dp, tensor):
        self.c = 2 if dp % 2 == 0 else 1
        self.y = dp // self.c
        self.x = self.y if tensor % self.y == 0 else 1
        self.z = tensor // self.x
        self.dp, self.tensor = dp, tensor
        self.axes = {
            "c": ("dp", 1, self.c),
            "y": ("dp", self.c, self.y),
            "x": ("tensor", 1, self.x),
            "z": ("tensor", self.x, self.z),
        }

    def size(self, g):
        return self.axes[g][2]

    def place(self, g):
        axis, stride, size = self.axes[g]
        return (lax.axis_index(axis) // stride) % size

    def swap(self, v, g, r):
        axis, stride, size = self.axes[g]
        total = self.dp if axis == "dp" else self.tensor
        return lax.ppermute(v, axis, [(i, i ^ (r * stride)) for i in range(total)])

    def scatter_sum(self, v, g, last=BF):
        size = self.size(g)
        if size == 1:
            return v.astype(last)
        me = self.place(g)
        rows = v.shape[0] // size
        got = []
        for r in range(1, size):
            got.append(self.swap(lax.dynamic_slice_in_dim(v, (me ^ r) * rows, rows, 0), g, r))
        total = lax.dynamic_slice_in_dim(v, me * rows, rows, 0).astype(F32)
        for piece in got:
            total = total + piece.astype(F32)
        return total.astype(last)

    def gather(self, v, g):
        size = self.size(g)
        if size == 1:
            return v
        me = self.place(g)
        rows = v.shape[0]
        got = [v] + [self.swap(v, g, r) for r in range(1, size)]
        if size == 2:
            return jnp.concatenate(
                [jnp.where(me == 0, got[0], got[1]), jnp.where(me == 0, got[1], got[0])], axis=0
            )
        out = jnp.zeros((rows * size,) + v.shape[1:], v.dtype)
        for r in range(size):
            out = lax.dynamic_update_slice_in_dim(out, got[r], (me ^ r) * rows, 0)
        return out

    def sum_all(self, v, order):
        for g in order:
            v = self.scatter_sum(v, g)
        for g in reversed(order):
            v = self.gather(v, g)
        return v


def contract(left, right, left_dim, right_dim):
    return lax.dot_general(
        left, right, (((left_dim,), (right_dim,)), ((), ())), preferred_element_type=jnp.float32
    )


def norm_back(grad_out, normed, inverse, gain):
    scaled = grad_out * gain
    gain_part = jnp.sum(grad_out * normed, axis=0)
    grad_in = inverse * (scaled - normed * jnp.mean(scaled * normed, axis=-1, keepdims=True))
    return (grad_in, gain_part)


def body(
    grid,
    tokens,
    cotangent,
    segments,
    positions,
    attngain,
    ffngain,
    queryheads,
    querydims,
    keyheads,
    keydims,
    valueheads,
    valuedims,
    outproj,
    gateproj,
    upproj,
    downproj,
):
    x = tokens[0]
    upstream = cotangent[0]
    length = x.shape[0]
    me = lax.axis_index("tensor")
    offset = me * length
    places = lax.dynamic_slice_in_dim(positions[0], offset, length)
    half = HEAD_DIM // 2
    freqs = 10000.0 ** (-jnp.arange(half, dtype=F32) * 2.0 / HEAD_DIM)
    angles = freqs[:, None] * places.astype(F32)[None, :]
    cosine, sine = jnp.cos(angles), jnp.sin(angles)
    start = (offset + jnp.arange(length, dtype=jnp.int32) - places)[:, None]
    scal = jnp.stack([jnp.maximum(offset - places[0], 0) // length, me]).astype(jnp.int32)
    weights = (queryheads, querydims, keyheads, keydims, valueheads, valuedims)
    xa, qfac, fac = enter(x, attngain[None, :], weights, cosine, sine)

    fac_z = grid.gather(fac[None, None], "z")
    fac_x = [fac_z] + [grid.swap(fac_z, "x", r) for r in range(1, grid.x)]
    mine = grid.place("x")
    facs = jnp.zeros((grid.z, grid.x) + fac.shape, BF)
    for r in range(grid.x):
        facs = lax.dynamic_update_slice_in_dim(facs, fac_x[r], mine ^ r, 1)
    facs = facs.reshape((grid.tensor,) + fac.shape)

    attn_out, lse = attention_forward(scal, qfac, facs, start)

    local = x.astype(F32)
    residual = local + jnp.dot(attn_out, outproj, preferred_element_type=jnp.float32)
    inverse_two = lax.rsqrt(jnp.mean(residual * residual, axis=-1, keepdims=True) + EPS)
    normed_two = residual * inverse_two
    input_two = (normed_two * ffngain).astype(jnp.bfloat16)
    shard = gateproj.shape[1]
    whole_two = lax.all_gather(input_two, "tensor", axis=0, tiled=True)
    paired = jnp.concatenate([gateproj, upproj], axis=1)
    joined = jnp.dot(whole_two, paired, preferred_element_type=jnp.float32)
    gate = joined[:, :shard]
    upper = joined[:, shard:]
    sigma = jax.nn.sigmoid(gate)
    active = gate * sigma
    inner = (active * upper).astype(jnp.bfloat16)
    ffn_out = lax.psum_scatter(
        jnp.dot(inner, downproj, preferred_element_type=jnp.float32).astype(jnp.bfloat16),
        "tensor",
        scatter_dimension=0,
        tiled=True,
    ).astype(jnp.float32)
    piece = lax.all_gather(upstream, "tensor", axis=0, tiled=True)
    down_part = contract(inner, piece, 0, 0)
    held = contract(piece, downproj, 1, 1)
    d_gate = (held * upper * sigma * (1.0 + gate * (1.0 - sigma))).astype(jnp.bfloat16)
    d_upper = (held * active).astype(jnp.bfloat16)
    d_paired = jnp.concatenate([d_gate, d_upper], axis=1)
    pair_part = contract(whole_two, d_paired, 0, 0)
    gate_part = pair_part[:, :shard]
    up_part = pair_part[:, shard:]
    d_norm_two = lax.psum_scatter(
        contract(d_paired, paired, 1, 1).astype(jnp.bfloat16),
        "tensor",
        scatter_dimension=0,
        tiled=True,
    ).astype(jnp.float32)
    gate_part, up_part, down_part = (
        lax.psum(gate_part.astype(jnp.bfloat16), "dp").astype(jnp.float32),
        lax.psum(up_part.astype(jnp.bfloat16), "dp").astype(jnp.float32),
        lax.psum(down_part.astype(jnp.bfloat16), "dp").astype(jnp.float32),
    )
    mixed = (residual + ffn_out).astype(jnp.bfloat16)
    grad_through, ffngain_part = norm_back(d_norm_two, normed_two, inverse_two, ffngain)
    d_residual = upstream.astype(jnp.float32) + grad_through
    d_res_low = d_residual.astype(jnp.bfloat16)
    outproj_part = contract(attn_out, d_res_low, 0, 0).astype(BF)
    d_attended = contract(d_res_low, outproj, 1, 1).astype(jnp.bfloat16)

    terms, dq = attention_backward(
        scal, qfac, facs, start, attn_out, d_attended, lse, cosine, sine
    )
    terms = terms.reshape((grid.z, grid.x) + fac.shape)
    near = lax.dynamic_slice_in_dim(terms, mine, 1, 1).astype(F32)
    for r in range(1, grid.x):
        near = near + grid.swap(lax.dynamic_slice_in_dim(terms, mine ^ r, 1, 1), "x", r).astype(F32)
    key_grads = grid.scatter_sum(near[:, 0].astype(BF), "z", F32)[0]

    query_part = leave_query(xa, dq, ffngain_part[None, :])
    tokens_grad, key_part = leave_key(
        x, xa, attngain[None, :], d_residual, dq, key_grads, cosine, sine, weights
    )
    order = ("c", "x", "y", "z")
    outproj_sum = grid.sum_all(outproj_part, order).astype(F32)
    query_sum = grid.sum_all(query_part, order).astype(F32)
    key_sum = grid.sum_all(key_part, order).astype(F32)
    return (
        mixed[None],
        tokens_grad[None],
        key_sum[:, FACW],
        query_sum[:, QFW],
        query_sum[:, :QHW],
        query_sum[:, QHW:QFW],
        key_sum[:, 2 * KDW : 2 * KDW + KHW],
        key_sum[:, :KDW],
        key_sum[:, 2 * KDW + KHW : FACW],
        key_sum[:, KDW : 2 * KDW],
        outproj_sum,
        gate_part,
        up_part,
        down_part,
    )


def solution(mesh):
    grid = Grid(mesh.shape["dp"], mesh.shape["tensor"])
    rows = P("dp", "tensor", None)
    placed = (rows, rows, P("dp", None), P("dp", None)) + (P(),) * 9
    halves = (P(None, "tensor"), P(None, "tensor"), P("tensor", None))
    return jax.shard_map(
        functools.partial(body, grid),
        mesh=mesh,
        in_specs=placed + halves,
        out_specs=(rows, rows) + (P(),) * 9 + halves,
        check_vma=False,
    )
```

time: 1140 us -> 656 us (0.58); the launches traced: 1130 us -> 655 us
  matrix products: 279 us -> 41.5 us
  local copies, waits for them, and re-layouts: 149 us -> 41 us
  waiting for transfers between devices: 549 us -> 445 us
  starting transfers between devices: 0.33 us -> 53.5 us
  loops' own time: 41.6 us -> 0 us
  blocking collectives: 41.3 us -> 0 us
  Pallas kernels: 0 us -> 30.5 us
  other arithmetic: 50.6 us -> 28.3 us
    dot_general x36 -> x0, matrix products: 233 us -> none  [the longest x4 35.7 us: key_block(): jnp.einsum('qhd,khd->hqk', query, keys, preferred_element_type=jnp.float32)]
    psum x1 -> x0, waiting for transfers between devices: 127 us -> none  [body(): lax.psum((proj_part, outproj_part, attngain_part, ffngain_part), ('dp', '...]
    ppermute x0 -> x44, waiting for transfers between devices: none -> 92.9 us  [swap(): return lax.ppermute(v, axis, [(i, i ^ r * stride) for i in range(total)])]
    ppermute x0 -> x44, starting transfers between devices: none -> 53.1 us  [swap(): return lax.ppermute(v, axis, [(i, i ^ r * stride) for i in range(total)])]
    another operation x3 -> x0, loops' own time: 41.6 us -> none  [the longest x1 33.3 us: body(): lax.scan(back_step, jnp.zeros((length, HEADS, HEAD_DIM), jnp.float32), be...]
    psum x1 -> x0, blocking collectives: 41.3 us -> none  [body(): lax.psum((proj_part, outproj_part, attngain_part, ffngain_part), ('dp', '...]
    reduce_scatter x1 -> x0, waiting for transfers between devices: 37.1 us -> none  [body(): lax.psum_scatter(key_terms.astype(jnp.bfloat16), 'tensor', scatter_dimens...]
    pallas_call x0 -> x5, Pallas kernels: none -> 30.5 us  [the longest x1 14.2 us: attention_backward(): pl.pallas_call(backward_kernel, out_shape=(jax.ShapeDtypeStruct((n, FACW,...]
  transfers between devices with their start and end apart: 8 -> 49, of which waited for: 8 -> 28; matrix products, arithmetic and copies ran while one was open for 6% -> 11% of each run, Pallas kernels for 0% -> 3%
where the time goes in v1:
time: 656 us; the launch traced here: 655 us
  waiting for transfers between devices  445 us (68%)
  starting transfers between devices  53.5 us (8%)
  matrix products  41.5 us (6%)
  local copies, waits for them, and re-layouts  41 us (6%)
  Pallas kernels  30.5 us (5%)
  other arithmetic  28.3 us (4%)
  between operations  15.4 us (2%)
    all_gather x1, waiting for transfers between devices, body(): whole_two = lax.all_gather(input_two, 'tensor', axis=0, tiled=True)  93 us
    ppermute x44, waiting for transfers between devices, swap(): return lax.ppermute(v, axis, [(i, i ^ r * stride) for i in range(total)])  92.9 us
    reduce_scatter x1, waiting for transfers between devices, body(): lax.psum_scatter(jnp.dot(inner, downproj, preferred_element_type=jnp.floa...  89.9 us
    reduce_scatter x1, waiting for transfers between devices, body(): lax.psum_scatter(contract(d_paired, paired, 1, 1).astype(jnp.bfloat16), '...  69.9 us
    all_gather x1, waiting for transfers between devices, body(): piece = lax.all_gather(upstream, 'tensor', axis=0, tiled=True)  65.2 us
    ppermute x44, starting transfers between devices, swap(): return lax.ppermute(v, axis, [(i, i ^ r * stride) for i in range(total)])  53.1 us
    psum x1, waiting for transfers between devices, body(): lax.psum(gate_part.astype(jnp.bfloat16), 'dp').astype(jnp.float32)  33 us
    dot_general x6, matrix products, contract(): lax.dot_general(left, right, (((left_dim,), (right_dim,)), ((), ())), pre...  25.5 us
  transfers between devices with their start and end apart: 49, of which 28 were waited for; matrix products, arithmetic and copies ran while one was open for 11% of the time, Pallas kernels for 3%

profile of v1, /device:TPU:0, one launch (start us, length us, event | category | flops | bytes accessed | tf_op | source)
XLA Modules:
  0.0 654.9 jit_solution(10777750409634851621)
XLA Ops:
  19.2 3.1 collective-permute-start
  26.4 2.7 collective-permute-done
  30.6 6.6 %collective-permute-done.1 = bf16[1,1,320,256]{3,2,1,0:T(8,128)(2,1)S(1)} collective-permute-done((bf16[1,1,320,256]{3,2,1,0:T(8,128)(2,1)S(1)}, bf16[1,1,320,256]{3,2,1,0:T(8,128)(2,1)S(1)}, u32[]{:S(2)}, u32[]{:S(2)}) %collective-permute-start.1) | collective-permute-done | bytes 163872 | tf_op jit(solution)/shard_map/ppermute | solution.py:459
  44.7 7.5 %collective-permute-done.3 = bf16[4,1,320,256]{3,2,1,0:T(8,128)(2,1)S(1)} collective-permute-done((bf16[4,1,320,256]{3,2,1,0:T(8,128)(2,1)}, bf16[4,1,320,256]{3,2,1,0:T(8,128)(2,1)S(1)}, u32[]{:S(2)}, u32[]{:S(2)}) %collective-permute-start.3) | collective-permute-done | bytes 655392 | tf_op jit(solution)/shard_map/ppermute | solution.py:459
  53.3 11.6 %attention_forward.1 = (bf16[256,1024]{1,0:T(8,128)(2,1)}, f32[16,256,128]{2,1,0:T(8,128)}) custom-call(s32[2]{0:T(128)} %pad_add_fusion.scal_ref, bf16[480,256]{1,0:T(8,128)(2,1)} %copy-done.19, bf16[8,320,256]{2,1,0:T(8,128)(2,1)} %bitcast.60, s32[256,1]{1,0:T(8,128)} %add_subtract_fusion.start_ref), custom_call_target="tpu_custom_call" | custom-call | tf_op jit(solution)/shard_map/attention_forward/pallas_call | solution.py:138
  72.7 93.0 %all-gather.4.cloned.1.call-done = bf16[2048,1024]{1,0:T(8,128)(2,1)} async-done(((bf16[256,1024]{1,0:T(8,128)(2,1)}), bf16[2048,1024]{1,0:T(8,128)(2,1)}) %all-gather.4.cloned.1.call-update) | async-done | bytes 4194320 | tf_op jit(solution)/shard_map/all_gather | solution.py:562
  165.8 8.3 %fusion.30 = f32[2048,704]{0,1:T(8,128)} fusion(bf16[2048,1024]{1,0:T(8,128)(2,1)} %all-gather.4.cloned.1.call-done, bf16[1024,704]{0,1:T(8,128)(2,1)} %constant_dynamic-update-slice_fusion.18), kind=kOutput, calls=%fused_computation.138 | convolution fusion | flops 2952790016 | bytes 11403264 | tf_op jit(solution)/shard_map/dot_general | solution.py:564
  174.0 65.2 %all-gather.6.cloned.1.call-done = bf16[1,2048,1024]{2,1,0:T(8,128)(2,1)} async-done(((bf16[1,256,1024]{2,1,0:T(8,128)(2,1)}), bf16[1,2048,1024]{2,1,0:T(8,128)(2,1)}) %all-gather.6.cloned.1.call-update) | async-done | bytes 4194320 | tf_op jit(solution)/shard_map/all_gather | solution.py:576
  239.2 7.9 %multiply_convert_fusion.1 = (bf16[2048,352]{0,1:T(8,128)(2,1)S(1)}, bf16[2048,352]{0,1:T(8,128)(2,1)S(1)}, bf16[2048,352]{0,1:T(8,128)(2,1)}) fusion(f32[2048,704]{0,1:T(8,128)} %fusion.30, bf16[352,1024]{1,0:T(8,128)(2,1)} %param.30, bf16[1,2048,1024]{2,1,0:T(8,128)(2,1)} %all-gather.6.cloned.1.call-done), kind=kOutput, calls=%fused_computation.8 | convolution fusion | flops 1487208448 | bytes 15007744 | tf_op jit(solution)/shard_map/dot_general | solution.py:500
  248.7 6.4 convolution_convert_fusion
  255.4 6.0 convolution_convert_fusion.1
  261.4 6.3 fusion.6
  272.2 69.9 %reduce-scatter.5.cloned.1.call-done = bf16[256,1024]{1,0:T(8,128)(2,1)} async-done(((bf16[2048,1024]{1,0:T(8,128)(2,1)}), bf16[256,1024]{1,0:T(8,128)(2,1)}) %reduce-scatter.5.cloned.1.call-update) | async-done | bytes 524304 | tf_op jit(solution)/shard_map/reduce_scatter | solution.py:585
  343.6 89.9 %reduce-scatter.3.cloned.1.call-done = bf16[256,1024]{1,0:T(8,128)(2,1)} async-done(((bf16[2048,1024]{1,0:T(8,128)(2,1)}), bf16[256,1024]{1,0:T(8,128)(2,1)}) %reduce-scatter.3.cloned.1.call-update) | async-done | bytes 524304 | tf_op jit(solution)/shard_map/reduce_scatter | solution.py:570
  433.6 2.8 fusion.14
  438.0 14.2 %attention_backward.1 = (bf16[8,320,256]{2,1,0:T(8,128)(2,1)}, bf16[480,256]{1,0:T(8,128)(2,1)}) custom-call(s32[2]{0:T(128)} %pad_add_fusion.scal_ref, bf16[480,256]{1,0:T(8,128)(2,1)} %copy-done.19, bf16[8,320,256]{2,1,0:T(8,128)(2,1)} %bitcast.61, s32[256,1]{1,0:T(8,128)} %add_subtract_fusion.start_ref, bf16[256,1024]{1,0:T(8,128)(2,1)} %get-tuple-element.25.o_ref, ...), custom_call_target="tpu_custom_call" | custom-call | tf_op jit(solution)/shard_map/attention_backward/pallas_call | solution.py:293
  455.7 33.0 %all-reduce.3.cloned.1.call-done = (bf16[1024,352]{0,1:T(8,128)(2,1)}, bf16[1024,352]{0,1:T(8,128)(2,1)}, bf16[352,1024]{1,0:T(8,128)(2,1)}) async-done(((bf16[1024,352]{0,1:T(8,128)(2,1)}, bf16[1024,352]{0,1:T(8,128)(2,1)}, bf16[352,1024]{1,0:T(8,128)(2,1)}), (bf16[1024,352]{0,1:T(8,128)(2,1)}, bf16[1024,352]{0,1:T(8,128)(2,1)}, bf16[352,1024]{1,0:T(8,128)(2,1)})) %all-reduce.3.cloned.1.call-update) | async-done | bytes 2162704 | tf_op jit(solution)/shard_map/psum | solution.py:592
  498.1 17.6 %collective-permute-done.21 = bf16[256,512]{1,0:T(8,128)(2,1)S(1)} collective-permute-done((bf16[256,512]{1,0:T(8,128)(2,1)S(1)}, bf16[256,512]{1,0:T(8,128)(2,1)S(1)}, u32[]{:S(2)}, u32[]{:S(2)}) %collective-permute-start.21) | collective-permute-done | bytes 262176 | tf_op jit(solution)/shard_map/ppermute | solution.py:459
  526.6 7.2 %collective-permute-done.6 = bf16[1,320,256]{2,1,0:T(8,128)(2,1)S(1)} collective-permute-done((bf16[1,320,256]{2,1,0:T(8,128)(2,1)S(1)}, bf16[1,320,256]{2,1,0:T(8,128)(2,1)S(1)}, u32[]{:S(2)}, u32[]{:S(2)}) %collective-permute-start.6) | collective-permute-done | bytes 163872 | tf_op jit(solution)/shard_map/ppermute | solution.py:459
  539.7 3.2 collective-permute-start.27
  544.9 3.7 collective-permute-done.28
  555.2 14.0 %collective-permute-done.9 = bf16[256,384]{1,0:T(8,128)(2,1)S(1)} collective-permute-done((bf16[256,384]{1,0:T(8,128)(2,1)S(1)}, bf16[256,384]{1,0:T(8,128)(2,1)S(1)}, u32[]{:S(2)}, u32[]{:S(2)}) %collective-permute-start.9) | collective-permute-done | bytes 196640 | tf_op jit(solution)/shard_map/ppermute | solution.py:459
  575.9 2.6 collective-permute-start.13
  578.9 2.8 collective-permute-done.13
  581.9 3.2 collective-permute-start.15
  587.6 3.2 collective-permute-done.16
  593.1 3.2 collective-permute-start.36
  598.6 3.7 collective-permute-done.37
  602.5 3.1 collective-permute-start.18
  608.7 2.8 collective-permute-done.39
  614.7 4.4 collective-permute-done.41
  625.6 4.7 collective-permute-done.42
  (276 shorter events, 125.9 us)
Async XLA Ops:
  7.2 158.6 %all-gather.4.cloned.1.call-start = ((), (), s32[]{:S(2)}) async-start(), calls=%async_computation.2 | async-start | bytes 4718592 | tf_op jit(solution)/shard_map/all_gather | solution.py:562
  19.2 9.9 %collective-permute-start = (bf16[1,1,320,256]{3,2,1,0:T(8,128)(2,1)S(1)}, bf16[1,1,320,256]{3,2,1,0:T(8,128)(2,1)}, u32[]{:S(2)}, u32[]{:S(2)}) collective-permute-start(bf16[1,1,320,256]{3,2,1,0:T(8,128)(2,1)S(1)} %bitcast.54), channel_id=1, source_target_pairs={{0,2},{1,3},{2,0},{3,1},{4,6},{5,7},{6,4},{7,5},{8,10},{9,11},{10,... | collective-permute-start | bytes 491528 | tf_op jit(solution)/shard_map/ppermute | solution.py:459
  22.2 15.0 %collective-permute-start.1 = (bf16[1,1,320,256]{3,2,1,0:T(8,128)(2,1)S(1)}, bf16[1,1,320,256]{3,2,1,0:T(8,128)(2,1)S(1)}, u32[]{:S(2)}, u32[]{:S(2)}) collective-permute-start(bf16[1,1,320,256]{3,2,1,0:T(8,128)(2,1)S(1)} %bitcast.55), channel_id=1, source_target_pairs={{0,4},{1,5},{2,6},{3,7},{4,0},{5,1},{6,2},{7,3},{8,12},{9,13},{10,... | collective-permute-start | bytes 491528 | tf_op jit(solution)/shard_map/ppermute | solution.py:459
  24.8 13.1 %collective-permute-start.2 = (bf16[1,1,320,256]{3,2,1,0:T(8,128)(2,1)S(1)}, bf16[1,1,320,256]{3,2,1,0:T(8,128)(2,1)S(1)}, u32[]{:S(2)}, u32[]{:S(2)}) collective-permute-start(bf16[1,1,320,256]{3,2,1,0:T(8,128)(2,1)S(1)} %bitcast.56), channel_id=1, source_target_pairs={{0,6},{1,7},{2,4},{3,5},{4,2},{5,3},{6,0},{7,1},{8,14},{9,15},{10,... | collective-permute-start | bytes 491528 | tf_op jit(solution)/shard_map/ppermute | solution.py:459
  38.6 13.6 %collective-permute-start.3 = (bf16[4,1,320,256]{3,2,1,0:T(8,128)(2,1)}, bf16[4,1,320,256]{3,2,1,0:T(8,128)(2,1)S(1)}, u32[]{:S(2)}, u32[]{:S(2)}) collective-permute-start(bf16[4,1,320,256]{3,2,1,0:T(8,128)(2,1)} %constant_dynamic-update-slice_fusion.14), channel_id=1, source_target_pairs={{0,1},{1,0},{2,3},{3,2},{4,5},{5,4},{6,7},{7,6},{8,9},{9,8},{10,11... | collective-permute-start | bytes 1966088 | tf_op jit(solution)/shard_map/ppermute | solution.py:459
  67.9 171.3 %all-gather.6.cloned.1.call-start = ((), (), s32[]{:S(2)}) async-start(), calls=%async_computation.5 | async-start | bytes 4718592 | tf_op jit(solution)/shard_map/all_gather | solution.py:576
  68.7 273.5 %reduce-scatter.5.cloned.1.call-start = ((), (), s32[]{:S(2)}) async-start(), calls=%async_computation.4 | async-start | bytes 4718592 | tf_op jit(solution)/shard_map/reduce_scatter | solution.py:585
  255.1 178.4 %reduce-scatter.3.cloned.1.call-start = ((), (), s32[]{:S(2)}) async-start(), calls=%async_computation.3 | async-start | bytes 4718592 | tf_op jit(solution)/shard_map/reduce_scatter | solution.py:570
  261.3 227.4 %all-reduce.3.cloned.1.call-start = ((), (), s32[]{:S(2)}) async-start(), calls=%async_computation.6 | async-start | bytes 4325376 | tf_op jit(solution)/shard_map/psum | solution.py:592
  455.7 39.6 %collective-permute-start.20 = (bf16[512,512]{1,0:T(8,128)(2,1)}, bf16[512,512]{1,0:T(8,128)(2,1)}, u32[]{:S(2)}, u32[]{:S(2)}) collective-permute-start(bf16[512,512]{1,0:T(8,128)(2,1)} %constant_dynamic-slice_fusion.12), channel_id=1, source_target_pairs={{0,8},{8,0},{16,24},{24,16},{1,9},{9,1},{17,25},{25,17},{2,10},{10... | collective-permute-start | bytes 1572872 | tf_op jit(solution)/shard_map/ppermute | solution.py:459
  493.8 23.0 %collective-permute-start.4 = (bf16[4,1,320,256]{3,2,1,0:T(8,128)(2,1)S(1)}, bf16[4,1,320,256]{3,2,1,0:T(8,128)(2,1)S(1)}, u32[]{:S(2)}, u32[]{:S(2)}) collective-permute-start(bf16[4,1,320,256]{3,2,1,0:T(8,128)(2,1)S(1)} %constant_dynamic-slice_fusion.19), channel_id=1, source_target_pairs={{0,1},{1,0},{2,3},{3,2},{4,5},{5,4},{6,7},{7,6},{8,9},{9,8},{10,11... | collective-permute-start | bytes 1966088 | tf_op jit(solution)/shard_map/ppermute | solution.py:459
  496.5 19.2 %collective-permute-start.21 = (bf16[256,512]{1,0:T(8,128)(2,1)S(1)}, bf16[256,512]{1,0:T(8,128)(2,1)S(1)}, u32[]{:S(2)}, u32[]{:S(2)}) collective-permute-start(bf16[256,512]{1,0:T(8,128)(2,1)S(1)} %constant_dynamic-slice_fusion.11), channel_id=1, source_target_pairs={{0,1},{1,0},{2,3},{3,2},{4,5},{5,4},{6,7},{7,6},{8,9},{9,8},{10,11... | collective-permute-start | bytes 786440 | tf_op jit(solution)/shard_map/ppermute | solution.py:459
  498.0 51.7 %collective-permute-start.32 = (bf16[512,1024]{1,0:T(8,128)(2,1)S(1)}, bf16[512,1024]{1,0:T(8,128)(2,1)S(1)}, u32[]{:S(2)}, u32[]{:S(2)}) collective-permute-start(bf16[512,1024]{1,0:T(8,128)(2,1)S(1)} %constant_dynamic-slice_fusion.6), channel_id=1, source_target_pairs={{0,8},{8,0},{16,24},{24,16},{1,9},{9,1},{17,25},{25,17},{2,10},{10... | collective-permute-start | bytes 3145736 | tf_op jit(solution)/shard_map/ppermute | solution.py:459
  517.0 7.7 %collective-permute-start.5 = (bf16[1,320,256]{2,1,0:T(8,128)(2,1)S(1)}, bf16[1,320,256]{2,1,0:T(8,128)(2,1)S(1)}, u32[]{:S(2)}, u32[]{:S(2)}) collective-permute-start(bf16[1,320,256]{2,1,0:T(8,128)(2,1)S(1)} %get-tuple-element.90), channel_id=1, source_target_pairs={{0,2},{1,3},{2,0},{3,1},{4,6},{5,7},{6,4},{7,5},{8,10},{9,11},{10,... | collective-permute-start | bytes 491528 | tf_op jit(solution)/shard_map/ppermute | solution.py:459
  518.6 15.2 %collective-permute-start.6 = (bf16[1,320,256]{2,1,0:T(8,128)(2,1)S(1)}, bf16[1,320,256]{2,1,0:T(8,128)(2,1)S(1)}, u32[]{:S(2)}, u32[]{:S(2)}) collective-permute-start(bf16[1,320,256]{2,1,0:T(8,128)(2,1)S(1)} %get-tuple-element.92), channel_id=1, source_target_pairs={{0,4},{1,5},{2,6},{3,7},{4,0},{5,1},{6,2},{7,3},{8,12},{9,13},{10,... | collective-permute-start | bytes 491528 | tf_op jit(solution)/shard_map/ppermute | solution.py:459
  521.0 15.1 %collective-permute-start.7 = (bf16[1,320,256]{2,1,0:T(8,128)(2,1)S(1)}, bf16[1,320,256]{2,1,0:T(8,128)(2,1)S(1)}, u32[]{:S(2)}, u32[]{:S(2)}) collective-permute-start(bf16[1,320,256]{2,1,0:T(8,128)(2,1)S(1)} %get-tuple-element.91), channel_id=1, source_target_pairs={{0,6},{1,7},{2,4},{3,5},{4,2},{5,3},{6,0},{7,1},{8,14},{9,15},{10,... | collective-permute-start | bytes 491528 | tf_op jit(solution)/shard_map/ppermute | solution.py:459
  521.5 17.3 %collective-permute-start.23 = (bf16[32,512]{1,0:T(8,128)(2,1)S(1)}, bf16[32,512]{1,0:T(8,128)(2,1)S(1)}, u32[]{:S(2)}, u32[]{:S(2)}) collective-permute-start(bf16[32,512]{1,0:T(8,128)(2,1)S(1)} %get-tuple-element.106), channel_id=1, source_target_pairs={{0,2},{1,3},{2,0},{3,1},{4,6},{5,7},{6,4},{7,5},{8,10},{9,11},{10,... | collective-permute-start | bytes 98312 | tf_op jit(solution)/shard_map/ppermute | solution.py:459
  524.7 14.1 %collective-permute-start.24 = (bf16[32,512]{1,0:T(8,128)(2,1)S(1)}, bf16[32,512]{1,0:T(8,128)(2,1)S(1)}, u32[]{:S(2)}, u32[]{:S(2)}) collective-permute-start(bf16[32,512]{1,0:T(8,128)(2,1)S(1)} %get-tuple-element.108), channel_id=1, source_target_pairs={{0,4},{1,5},{2,6},{3,7},{4,0},{5,1},{6,2},{7,3},{8,12},{9,13},{10,... | collective-permute-start | bytes 98312 | tf_op jit(solution)/shard_map/ppermute | solution.py:459
  539.7 12.0 %collective-permute-start.8 = (bf16[512,384]{1,0:T(8,128)(2,1)S(1)}, bf16[512,384]{1,0:T(8,128)(2,1)S(1)}, u32[]{:S(2)}, u32[]{:S(2)}) collective-permute-start(bf16[512,384]{1,0:T(8,128)(2,1)S(1)} %constant_dynamic-slice_fusion.18), channel_id=1, source_target_pairs={{0,8},{8,0},{16,24},{24,16},{1,9},{9,1},{17,25},{25,17},{2,10},{10... | collective-permute-start | bytes 1179656 | tf_op jit(solution)/shard_map/ppermute | solution.py:459
  550.2 36.1 %collective-permute-start.33 = (bf16[256,1024]{1,0:T(8,128)(2,1)S(1)}, bf16[256,1024]{1,0:T(8,128)(2,1)S(1)}, u32[]{:S(2)}, u32[]{:S(2)}) collective-permute-start(bf16[256,1024]{1,0:T(8,128)(2,1)S(1)} %constant_dynamic-slice_fusion.5), channel_id=1, source_target_pairs={{0,1},{1,0},{2,3},{3,2},{4,5},{5,4},{6,7},{7,6},{8,9},{9,8},{10,11... | collective-permute-start | bytes 1572872 | tf_op jit(solution)/shard_map/ppermute | solution.py:459
  551.9 17.4 %collective-permute-start.9 = (bf16[256,384]{1,0:T(8,128)(2,1)S(1)}, bf16[256,384]{1,0:T(8,128)(2,1)S(1)}, u32[]{:S(2)}, u32[]{:S(2)}) collective-permute-start(bf16[256,384]{1,0:T(8,128)(2,1)S(1)} %constant_dynamic-slice_fusion.17), channel_id=1, source_target_pairs={{0,1},{1,0},{2,3},{3,2},{4,5},{5,4},{6,7},{7,6},{8,9},{9,8},{10,11... | collective-permute-start | bytes 589832 | tf_op jit(solution)/shard_map/ppermute | solution.py:459
  553.7 18.9 %collective-permute-start.30 = (bf16[256,512]{1,0:T(8,128)(2,1)S(1)}, bf16[256,512]{1,0:T(8,128)(2,1)S(1)}, u32[]{:S(2)}, u32[]{:S(2)}) collective-permute-start(bf16[256,512]{1,0:T(8,128)(2,1)S(1)} %pad_maximum_fusion.10), channel_id=1, source_target_pairs={{0,1},{1,0},{2,3},{3,2},{4,5},{5,4},{6,7},{7,6},{8,9},{9,8},{10,11... | collective-permute-start | bytes 786440 | tf_op jit(solution)/shard_map/ppermute | solution.py:459
  578.6 41.6 %collective-permute-start.31 = (bf16[512,512]{1,0:T(8,128)(2,1)S(1)}, bf16[512,512]{1,0:T(8,128)(2,1)S(1)}, u32[]{:S(2)}, u32[]{:S(2)}) collective-permute-start(bf16[512,512]{1,0:T(8,128)(2,1)S(1)} %pad_maximum_fusion.7), channel_id=1, source_target_pairs={{0,8},{8,0},{16,24},{24,16},{1,9},{9,1},{17,25},{25,17},{2,10},{10... | collective-permute-start | bytes 1572872 | tf_op jit(solution)/shard_map/ppermute | solution.py:459
  586.5 6.4 collective-permute-start.34
  590.7 6.7 %collective-permute-start.17 = (bf16[128,384]{1,0:T(8,128)(2,1)S(1)}, bf16[128,384]{1,0:T(8,128)(2,1)S(1)}, u32[]{:S(2)}, u32[]{:S(2)}) collective-permute-start(bf16[128,384]{1,0:T(8,128)(2,1)S(1)} %constant_dynamic-update-slice_fusion.8), channel_id=1, source_target_pairs={{0,16},{8,24},{16,0},{24,8},{1,17},{9,25},{17,1},{25,9},{2,18},{10... | collective-permute-start | bytes 294920 | tf_op jit(solution)/shard_map/ppermute | solution.py:459
  602.4 6.3 collective-permute-start.38
  602.5 11.2 %collective-permute-start.18 = (bf16[256,384]{1,0:T(8,128)(2,1)S(1)}, bf16[256,384]{1,0:T(8,128)(2,1)S(1)}, u32[]{:S(2)}, u32[]{:S(2)}) collective-permute-start(bf16[256,384]{1,0:T(8,128)(2,1)S(1)} %pad_maximum_fusion.11), channel_id=1, source_target_pairs={{0,1},{1,0},{2,3},{3,2},{4,5},{5,4},{6,7},{7,6},{8,9},{9,8},{10,11... | collective-permute-start | bytes 589832 | tf_op jit(solution)/shard_map/ppermute | solution.py:459
  606.5 6.2 collective-permute-start.40
  612.7 6.4 collective-permute-start.41
  614.7 18.0 %collective-permute-start.19 = (bf16[512,384]{1,0:T(8,128)(2,1)}, bf16[512,384]{1,0:T(8,128)(2,1)}, u32[]{:S(2)}, u32[]{:S(2)}) collective-permute-start(bf16[512,384]{1,0:T(8,128)(2,1)} %pad_maximum_fusion.9), channel_id=1, source_target_pairs={{0,8},{8,0},{16,24},{24,16},{1,9},{9,1},{17,25},{25,17},{2,10},{10... | collective-permute-start | bytes 1179656 | tf_op jit(solution)/shard_map/ppermute | solution.py:459
  620.1 10.2 %collective-permute-start.42 = (bf16[256,1024]{1,0:T(8,128)(2,1)}, bf16[256,1024]{1,0:T(8,128)(2,1)}, u32[]{:S(2)}, u32[]{:S(2)}) collective-permute-start(bf16[256,1024]{1,0:T(8,128)(2,1)} %pad_maximum_fusion.8), channel_id=1, source_target_pairs={{0,1},{1,0},{2,3},{3,2},{4,5},{5,4},{6,7},{7,6},{8,9},{9,8},{10,11... | collective-permute-start | bytes 1572872 | tf_op jit(solution)/shard_map/ppermute | solution.py:459
  632.7 11.5 %collective-permute-start.43 = (bf16[512,1024]{1,0:T(8,128)(2,1)}, bf16[512,1024]{1,0:T(8,128)(2,1)}, u32[]{:S(2)}, u32[]{:S(2)}) collective-permute-start(bf16[512,1024]{1,0:T(8,128)(2,1)} %pad_maximum_fusion.5), channel_id=1, source_target_pairs={{0,8},{8,0},{16,24},{24,16},{1,9},{9,1},{17,25},{25,17},{2,10},{10... | collective-permute-start | bytes 3145736 | tf_op jit(solution)/shard_map/ppermute | solution.py:459
  (65 other events, 862.6 us)
Sparse Core Ops, SparseCore 0:
  68.0 97.6 all-gather.3
  167.9 71.3 all-gather.5
  255.2 86.8 reduce-scatter.4
  345.6 87.9 reduce-scatter.2
  436.5 52.1 all-reduce.2

commit v2 on v1

v2 whole, which is shorter than its diff:
```python
import functools
import math

import jax
import jax.numpy as jnp
from jax import lax
from jax.experimental import pallas as pl
from jax.experimental.pallas import tpu as pltpu

from jax.sharding import PartitionSpec as P

HEADS = 16
HEAD_DIM = 64
QRANK = 6
KRANK = 2
PAIRS = HEADS // 2
QHW = HEADS * QRANK
QDW = QRANK * HEAD_DIM
KDW = KRANK * HEAD_DIM
KHW = HEADS * KRANK
FACW = 2 * KDW + 2 * KHW
QFW = QHW + QDW
LOG2E = 1.4426950408889634
EPS = 1e-06
BF = jnp.bfloat16
F32 = jnp.float32


def mm(a, b, ca=1, cb=0):
    return lax.dot_general(a, b, (((ca,), (cb,)), ((), ())), preferred_element_type=F32)


def expand_pair(bk0, bk1, rows):
    first = rows[0] * bk0 + rows[1] * bk1
    second = rows[2] * bk0 + rows[3] * bk1
    return jnp.concatenate([first, second], axis=0) * (1.0 / KRANK)


def query_pair(qfac_ref, aq_s, pair):
    halves = []
    for h in range(2):
        acc = None
        for r in range(QRANK):
            row = aq_s[pl.ds(pair * (2 * QRANK) + h * QRANK + r, 1), :]
            term = row * qfac_ref[QHW + r * HEAD_DIM : QHW + (r + 1) * HEAD_DIM, :].astype(F32)
            acc = term if acc is None else acc + term
        halves.append(acc * (1.0 / QRANK))
    return jnp.concatenate(halves, axis=0).astype(BF)


def reverse_bits(r, size):
    total, bits = 0, size.bit_length() - 1
    for k in range(bits):
        total = total + (((r >> k) & 1) << (bits - 1 - k))
    return total


def fill_tables(scal_ref, qfac_ref, fac_refs, start_ref, fac_s, aq_s, kv_s, bias_s):
    length = qfac_ref.shape[1]
    me = scal_ref[1]
    across = len(fac_refs)
    aq_s[...] = qfac_ref[0:QHW, :].astype(F32)
    row = lax.broadcasted_iota(jnp.int32, (length, length), 0) + me * length
    column = lax.broadcasted_iota(jnp.int32, (length, length), 1)
    begin = start_ref[...]

    def fill(c, carry):
        for k, ref in enumerate(fac_refs):

            @pl.when(((c ^ me) % across) == k)
            def _(ref=ref):
                piece = ref[reverse_bits((c ^ me) // across, ref.shape[0])]
                fac_s[c] = piece[0 : 2 * KDW, :]
                kv_s[c] = piece[2 * KDW :, :].astype(F32)

        key = column + c * length
        keep = (key >= begin) & (key <= row)
        bias_s[c] = jnp.where(keep, 0.0, -1e30)
        return carry

    lax.fori_loop(scal_ref[0], me + 1, fill, 0)


def key_pair(fac_ref, kv_s, c, pair, which):
    base = which * KDW
    b0 = fac_ref[c, base : base + HEAD_DIM, :].astype(F32)
    b1 = fac_ref[c, base + HEAD_DIM : base + 2 * HEAD_DIM, :].astype(F32)
    rows = [kv_s[c, pl.ds(which * KHW + pair * 4 + j, 1), :] for j in range(4)]
    return expand_pair(b0, b1, rows), b0, b1, rows


def forward_kernel(across, scal_ref, qfac_ref, *refs):
    fac_refs, start_ref = refs[:across], refs[across]
    o_ref, lse_ref, fac_ref, aq_s, kv_s, bias_s, s_s = refs[across + 1 :]
    pair = pl.program_id(0)
    length = qfac_ref.shape[1]
    lo, me = scal_ref[0], scal_ref[1]

    @pl.when(pair == 0)
    def _():
        fill_tables(scal_ref, qfac_ref, fac_refs, start_ref, fac_ref, aq_s, kv_s, bias_s)

    query = jnp.transpose(query_pair(qfac_ref, aq_s, pair).astype(F32)) * (HEAD_DIM**-0.5)
    low_half = lax.broadcasted_iota(jnp.int32, (length, 2 * HEAD_DIM), 1) < HEAD_DIM
    queries = [
        jnp.where(low_half, query, 0.0).astype(BF),
        jnp.where(low_half, 0.0, query).astype(BF),
    ]
    lanes = 128
    pieces = length // lanes

    def score(c, tops):
        keys = key_pair(fac_ref, kv_s, c, pair, 0)[0].astype(BF)
        bias = bias_s[c]
        new = []
        for h in range(2):
            s = mm(queries[h], keys) * LOG2E + bias
            s_s[h, c] = s
            top = tops[h]
            for i in range(pieces):
                top = jnp.maximum(top, s[:, i * lanes : (i + 1) * lanes])
            new.append(top)
        return tuple(new)

    start = jnp.full((length, lanes), -1e30, F32)
    tops = lax.fori_loop(lo, me + 1, score, (start, start))
    tops = [jnp.max(top, axis=1, keepdims=True) for top in tops]

    def value(c, carry):
        values = key_pair(fac_ref, kv_s, c, pair, 1)[0].astype(BF)
        new = []
        for h in range(2):
            p = jnp.exp2(s_s[h, c] - tops[h])
            total = carry[2 * h]
            for i in range(pieces):
                total = total + p[:, i * lanes : (i + 1) * lanes]
            new += [total, carry[2 * h + 1] + mm(p.astype(BF), values, 1, 1)]
        return tuple(new)

    zero = jnp.zeros((length, lanes), F32)
    wide = jnp.zeros((length, 2 * HEAD_DIM), F32)
    done = lax.fori_loop(lo, me + 1, value, (zero, wide, zero, wide))
    outs = []
    for h in range(2):
        total = jnp.sum(done[2 * h], axis=1, keepdims=True)
        outs.append(done[2 * h + 1] / total)
        lse_ref[h] = jnp.broadcast_to(tops[h] + jnp.log2(total), (length, lanes))
    o_ref[...] = jnp.where(low_half, outs[0], outs[1]).astype(BF)


def full(shape):
    return pl.BlockSpec(shape, lambda p, s: (0,) * len(shape))


def attention_forward(scal, qfac, facs, start):
    length = qfac.shape[1]
    n = facs[0].shape[0] * len(facs)
    return pl.pallas_call(
        functools.partial(forward_kernel, len(facs)),
        out_shape=(
            jax.ShapeDtypeStruct((length, HEADS * HEAD_DIM), BF),
            jax.ShapeDtypeStruct((HEADS, length, 128), F32),
        ),
        grid_spec=pltpu.PrefetchScalarGridSpec(
            num_scalar_prefetch=1,
            grid=(PAIRS,),
            in_specs=[full(qfac.shape)] + [full(v.shape) for v in facs] + [full(start.shape)],
            out_specs=[
                pl.BlockSpec((length, 2 * HEAD_DIM), lambda p, s: (0, p)),
                pl.BlockSpec((2, length, 128), lambda p, s: (p, 0, 0)),
            ],
            scratch_shapes=[
                pltpu.VMEM((n, 2 * KDW, length), BF),
                pltpu.VMEM((QHW, length), F32),
                pltpu.VMEM((n, 2 * KHW, length), F32),
                pltpu.VMEM((n, length, length), F32),
                pltpu.VMEM((2, n, length, length), F32),
            ],
        ),
        compiler_params=pltpu.CompilerParams(
            dimension_semantics=("arbitrary",), vmem_limit_bytes=58 << 20
        ),
        cost_estimate=SMALL,
        name="attention_forward",
    )(scal, qfac, *facs, start)


def backward_kernel(across, scal_ref, qfac_ref, *refs):
    fac_refs = refs[:across]
    start_ref, o_ref, do_ref, lse_ref, cos_ref, sin_ref = refs[across : across + 6]
    terms_refs = refs[across + 6 : 2 * across + 6]
    dq_ref, fac_ref, aq_s, kv_s, bias_s, acc_s, heads_s, dbq_s, daq_s = refs[2 * across + 6 :]
    pair = pl.program_id(0)
    length = qfac_ref.shape[1]
    n = fac_ref.shape[0]
    lo, me = scal_ref[0], scal_ref[1]
    pieces = length // 128

    @pl.when(pair == 0)
    def _():
        fill_tables(scal_ref, qfac_ref, fac_refs, start_ref, fac_ref, aq_s, kv_s, bias_s)
        dbq_s[...] = jnp.zeros_like(dbq_s)

        def clear(c, carry):
            acc_s[c] = jnp.zeros((2 * KDW, length), F32)
            return carry

        lax.fori_loop(lo, me + 1, clear, 0)

    query_t = query_pair(qfac_ref, aq_s, pair).astype(F32) * (HEAD_DIM**-0.5)
    query = jnp.transpose(query_t)
    query_t = query_t.astype(BF)
    do = do_ref[...].astype(F32)
    do_t = jnp.transpose(do).astype(BF)
    low_half = lax.broadcasted_iota(jnp.int32, (length, 2 * HEAD_DIM), 1) < HEAD_DIM
    product = do * o_ref[...].astype(F32)
    queries, grads, deltas, stats = [], [], [], []
    for h in range(2):
        keep = low_half if h == 0 else jnp.logical_not(low_half)
        queries.append(jnp.where(keep, query, 0.0).astype(BF))
        grads.append(jnp.where(keep, do, 0.0).astype(BF))
        deltas.append(jnp.sum(jnp.where(keep, product, 0.0), axis=1, keepdims=True))
        stats.append(lse_ref[h])

    def step(c, dqs):
        keys, kb0, kb1, krows = key_pair(fac_ref, kv_s, c, pair, 0)
        values, vb0, vb1, vrows = key_pair(fac_ref, kv_s, c, pair, 1)
        keys, values = keys.astype(BF), values.astype(BF)
        bias = bias_s[c]
        new, sums, rows = [], [None] * 4, []
        for h in range(2):
            s = mm(queries[h], keys) * LOG2E + bias
            lse = jnp.concatenate([stats[h]] * pieces, axis=1)
            p = jnp.exp2(s - lse)
            dp = mm(grads[h], values)
            ds = (p * (dp - deltas[h])).astype(BF)
            pb = p.astype(BF)
            new.append(dqs[h] + mm(ds, keys, 1, 1))
            half = slice(h * HEAD_DIM, (h + 1) * HEAD_DIM)
            dk = mm(query_t[half, :], ds)
            dv = mm(do_t[half, :], pb)
            for which, d, b0, b1, a in ((0, dk, kb0, kb1, krows), (1, dv, vb0, vb1, vrows)):
                for r, b in ((0, b0), (1, b1)):
                    term = d * a[2 * h + r]
                    k = 2 * which + r
                    sums[k] = term if sums[k] is None else sums[k] + term
                    rows.append((which * 4 + 2 * h + r, jnp.sum(d * b, axis=0, keepdims=True)))
        for k in range(4):
            part = slice(k * HEAD_DIM, (k + 1) * HEAD_DIM)
            acc_s[c, part, :] = acc_s[c, part, :] + sums[k]
        for k, row in rows:
            where = (k // 4) * KHW + pair * 4 + k % 4
            heads_s[c, pl.ds(where, 1), :] = row
        return tuple(new)

    zero = jnp.zeros((length, 2 * HEAD_DIM), F32)
    dqs = lax.fori_loop(lo, me + 1, step, (zero, zero))
    dq_t = jnp.transpose(jnp.where(low_half, dqs[0], dqs[1])) * (HEAD_DIM**-0.5 / QRANK)
    for h in range(2):
        d = dq_t[h * HEAD_DIM : (h + 1) * HEAD_DIM, :]
        for r in range(QRANK):
            part = slice(r * HEAD_DIM, (r + 1) * HEAD_DIM)
            b = qfac_ref[QHW + r * HEAD_DIM : QHW + (r + 1) * HEAD_DIM, :].astype(F32)
            k = pl.ds(pair * (2 * QRANK) + h * QRANK + r, 1)
            daq_s[k, :] = jnp.sum(d * b, axis=0, keepdims=True)
            dbq_s[part, :] = dbq_s[part, :] + d * aq_s[k, :]

    @pl.when(pair == PAIRS - 1)
    def _():
        cosine, sine = cos_ref[...], sin_ref[...]
        half = HEAD_DIM // 2
        dq_ref[0:QHW, :] = daq_s[...].astype(BF)
        for r in range(QRANK):
            first = dbq_s[r * HEAD_DIM : r * HEAD_DIM + half, :]
            second = dbq_s[r * HEAD_DIM + half : (r + 1) * HEAD_DIM, :]
            turned = jnp.concatenate(
                [first * cosine + second * sine, second * cosine - first * sine], axis=0
            )
            dq_ref[QHW + r * HEAD_DIM : QHW + (r + 1) * HEAD_DIM, :] = turned.astype(BF)

        def flush(c, carry):
            inside = (c >= lo) & (c <= me)
            for k, ref in enumerate(terms_refs):

                @pl.when(inside & (((c ^ me) % across) == k))
                def _(ref=ref):
                    place = reverse_bits((c ^ me) // across, ref.shape[0])
                    ref[place, 0 : 2 * KDW, :] = (acc_s[c] * (1.0 / KRANK)).astype(BF)
                    ref[place, 2 * KDW :, :] = (heads_s[c] * (1.0 / KRANK)).astype(BF)

                @pl.when(jnp.logical_not(inside) & (((c ^ me) % across) == k))
                def _(ref=ref):
                    ref[reverse_bits((c ^ me) // across, ref.shape[0])] = jnp.zeros((FACW, length), BF)

            return carry

        lax.fori_loop(0, n, flush, 0)


def attention_backward(scal, qfac, facs, start, o, do, lse, cosine, sine):
    length = qfac.shape[1]
    across, along = len(facs), facs[0].shape[0]
    n = across * along
    return pl.pallas_call(
        functools.partial(backward_kernel, across),
        out_shape=(jax.ShapeDtypeStruct((along, FACW, length), BF),) * across
        + (jax.ShapeDtypeStruct((QFW, length), BF),),
        grid_spec=pltpu.PrefetchScalarGridSpec(
            num_scalar_prefetch=1,
            grid=(PAIRS,),
            in_specs=[
                full(qfac.shape),
            ]
            + [full(v.shape) for v in facs]
            + [
                full(start.shape),
                pl.BlockSpec((length, 2 * HEAD_DIM), lambda p, s: (0, p)),
                pl.BlockSpec((length, 2 * HEAD_DIM), lambda p, s: (0, p)),
                pl.BlockSpec((2, length, 128), lambda p, s: (p, 0, 0)),
                full(cosine.shape),
                full(sine.shape),
            ],
            out_specs=[full((along, FACW, length))] * across + [full((QFW, length))],
            scratch_shapes=[
                pltpu.VMEM((n, 2 * KDW, length), BF),
                pltpu.VMEM((QHW, length), F32),
                pltpu.VMEM((n, 2 * KHW, length), F32),
                pltpu.VMEM((n, length, length), F32),
                pltpu.VMEM((n, 2 * KDW, length), F32),
                pltpu.VMEM((n, 2 * KHW, length), F32),
                pltpu.VMEM((QDW, length), F32),
                pltpu.VMEM((QHW, length), F32),
            ],
        ),
        compiler_params=pltpu.CompilerParams(
            dimension_semantics=("arbitrary",), vmem_limit_bytes=58 << 20
        ),
        cost_estimate=SMALL,
        name="attention_backward",
    )(scal, qfac, *facs, start, o, do, lse, cosine, sine)


def norm_of(values):
    inverse = lax.rsqrt(jnp.mean(values * values, axis=-1, keepdims=True) + EPS)
    return values * inverse, inverse


def turn(values, cosine, sine, sign):
    half = HEAD_DIM // 2
    parts = []
    for r in range(values.shape[0] // HEAD_DIM):
        first = values[r * HEAD_DIM : r * HEAD_DIM + half, :]
        second = values[r * HEAD_DIM + half : (r + 1) * HEAD_DIM, :]
        parts.append(first * cosine - sign * second * sine)
        parts.append(second * cosine + sign * first * sine)
    return jnp.concatenate(parts, axis=0)


def enter_kernel(gain_ref, cos_ref, sin_ref, *refs):
    sources, (xa_ref, qfac_ref, fac_ref) = refs[:7], refs[7:10]
    x_ref, qh, qd, kh, kd, vh, vd, sem = refs[10:]
    copies = [
        pltpu.make_async_copy(source, target, sem.at[k])
        for k, (source, target) in enumerate(zip(sources, (x_ref, qh, qd, kh, kd, vh, vd)))
    ]
    for copy in copies:
        copy.start()
    for copy in copies:
        copy.wait()
    normed = norm_of(x_ref[...].astype(F32))[0]
    xa = (normed * gain_ref[...]).astype(BF)
    xa_ref[...] = xa
    cosine, sine = cos_ref[...], sin_ref[...]
    kdims = turn(jnp.transpose(mm(xa, kd[...])), cosine, sine, 1.0)
    fac_ref[0:KDW, :] = kdims.astype(BF)
    fac_ref[KDW : 2 * KDW, :] = jnp.transpose(mm(xa, vd[...])).astype(BF)
    fac_ref[2 * KDW : 2 * KDW + KHW, :] = mm(kh[...], xa, 1, 1).astype(BF)
    fac_ref[2 * KDW + KHW :, :] = mm(vh[...], xa, 1, 1).astype(BF)
    qfac_ref[0:QHW, :] = mm(qh[...], xa, 1, 1).astype(BF)
    qdims = turn(jnp.transpose(mm(xa, qd[...])), cosine, sine, 1.0)
    qfac_ref[QHW:, :] = qdims.astype(BF)


WHOLE = pl.BlockSpec(memory_space=pltpu.VMEM)
RAW = pl.BlockSpec(memory_space=pl.ANY)
SCALAR = pl.BlockSpec(memory_space=pltpu.SMEM)
SMALL = pl.CostEstimate(flops=1000, transcendentals=0, bytes_accessed=1000)


def enter(x, gain, weights, cosine, sine):
    length, width = x.shape
    moved = (x,) + tuple(weights)
    return pl.pallas_call(
        enter_kernel,
        out_shape=(
            jax.ShapeDtypeStruct((length, width), BF),
            jax.ShapeDtypeStruct((QFW, length), BF),
            jax.ShapeDtypeStruct((FACW, length), BF),
        ),
        in_specs=[WHOLE] * 3 + [RAW] * 7,
        out_specs=[WHOLE] * 3,
        scratch_shapes=[pltpu.VMEM(v.shape, BF) for v in moved] + [pltpu.SemaphoreType.DMA((7,))],
        compiler_params=pltpu.CompilerParams(vmem_limit_bytes=40 << 20),
        name="enter",
    )(gain, cosine, sine, *moved)


def block_place(ids_ref, sizes, index, rows):
    place, scale = 0, 1
    for k in reversed(range(len(sizes))):
        place = place + ((index % sizes[k]) ^ ids_ref[k]) * scale
        index, scale = index // sizes[k], scale * sizes[k]
    return pl.multiple_of(place * rows, rows)


def deal(ids_ref, sizes, t_s, outs):
    blocks, rows = outs[0].shape[:2]
    for side in range(2):

        def one(i, carry, side=side):
            place = block_place(ids_ref, sizes, side * blocks + i, rows)
            outs[side][i] = t_s[pl.ds(place, rows), :].astype(BF)
            return carry

        lax.fori_loop(0, blocks, one, 0)


def collect(ids_ref, sizes, sources, write):
    blocks, rows = sources[0].shape[:2]
    for side in range(2):

        def one(i, carry, side=side):
            place = block_place(ids_ref, sizes, side * blocks + i, rows)
            write(pl.ds(place, rows), sources[side][i].astype(F32))
            return carry

        lax.fori_loop(0, blocks, one, 0)


def leave_query_kernel(sizes, ids_ref, xa_ref, dq_ref, fgain_ref, o_ref, dhb_ref, kept_ref, sent_ref, t_s):
    xa_t = jnp.transpose(xa_ref[...])
    depth = o_ref.shape[1]
    t_s[:, 0:depth] = mm(jnp.transpose(o_ref[...]), dhb_ref[...])
    t_s[:, depth : depth + QHW] = mm(xa_t, dq_ref[0:QHW, :], 1, 1)
    t_s[:, depth + QHW : depth + QFW] = mm(xa_t, dq_ref[QHW:, :], 1, 1)
    gain = jnp.concatenate([fgain_ref[...]] * (512 - QFW), axis=0)
    t_s[:, depth + QFW :] = jnp.transpose(gain)
    deal(ids_ref, sizes, t_s, (kept_ref, sent_ref))


def leave_key_kernel(
    sizes, ids_ref, x_ref, xa_ref, gain_ref, dres_ref, dq_ref, kg_ref, cos_ref, sin_ref,
    qh, qd, kh, kd, vh, vd, tg_ref, kept_ref, sent_ref, out_ref
):
    normed, inverse = norm_of(x_ref[...].astype(F32))
    g = kg_ref[...]
    dkd = turn(g[0:KDW, :], cos_ref[...], sin_ref[...], -1.0)
    d_kd = jnp.transpose(dkd).astype(BF)
    d_vd = jnp.transpose(g[KDW : 2 * KDW, :]).astype(BF)
    d_kh = jnp.transpose(g[2 * KDW : 2 * KDW + KHW, :]).astype(BF)
    d_vh = jnp.transpose(g[2 * KDW + KHW :, :]).astype(BF)
    dq = dq_ref[...].astype(F32)
    d_qh = jnp.transpose(dq[0:QHW, :]).astype(BF)
    d_qd = jnp.transpose(dq[QHW:, :]).astype(BF)
    xa_t = jnp.transpose(xa_ref[...])
    out_ref[:, 0:KDW] = mm(xa_t, d_kd)
    out_ref[:, KDW : 2 * KDW] = mm(xa_t, d_vd)
    out_ref[:, 2 * KDW : 2 * KDW + KHW] = mm(xa_t, d_kh)
    out_ref[:, 2 * KDW + KHW : FACW] = mm(xa_t, d_vh)
    dxa = mm(d_qd, qd[...], 1, 1) + mm(d_qh, qh[...])
    dxa = dxa + mm(d_kd, kd[...], 1, 1) + mm(d_vd, vd[...], 1, 1)
    dxa = dxa + mm(d_kh, kh[...]) + mm(d_vh, vh[...])
    scaled = dxa * gain_ref[...]
    mean = jnp.mean(scaled * normed, axis=-1, keepdims=True)
    tg_ref[...] = (dres_ref[...] + inverse * (scaled - normed * mean)).astype(BF)
    gain_part = jnp.sum(dxa * normed, axis=0, keepdims=True)
    gain = jnp.concatenate([gain_part] * (384 - FACW), axis=0)
    out_ref[:, FACW:] = jnp.transpose(gain)
    deal(ids_ref, sizes, out_ref, (kept_ref, sent_ref))


def leave_query(sizes, ids, xa, dq, fgain, o, dhb):
    depth = xa.shape[1]
    blocks = math.prod(sizes) // 2
    columns = depth + 512
    return pl.pallas_call(
        functools.partial(leave_query_kernel, sizes),
        out_shape=(jax.ShapeDtypeStruct((blocks, depth // (2 * blocks), columns), BF),) * 2,
        in_specs=[SCALAR] + [WHOLE] * 5,
        out_specs=[WHOLE] * 2,
        scratch_shapes=[pltpu.VMEM((depth, columns), F32)],
        compiler_params=pltpu.CompilerParams(vmem_limit_bytes=40 << 20),
        cost_estimate=SMALL,
        name="leave_query",
    )(ids, xa, dq, fgain, o, dhb)


def leave_key(sizes, ids, x, xa, gain, dres, dq, kg, cosine, sine, weights):
    length, depth = x.shape
    blocks = math.prod(sizes) // 2
    return pl.pallas_call(
        functools.partial(leave_key_kernel, sizes),
        out_shape=(jax.ShapeDtypeStruct((length, depth), BF),)
        + (jax.ShapeDtypeStruct((blocks, depth // (2 * blocks), 384), BF),) * 2,
        in_specs=[SCALAR] + [WHOLE] * (8 + len(weights)),
        out_specs=[WHOLE] * 3,
        scratch_shapes=[pltpu.VMEM((depth, 384), F32)],
        compiler_params=pltpu.CompilerParams(vmem_limit_bytes=40 << 20),
        cost_estimate=SMALL,
        name="leave_key",
    )(ids, x, xa, gain, dres, dq, kg, cosine, sine, *weights)


def end_query_kernel(sizes, ids_ref, own_ref, got_ref, proj_ref, qh_ref, qd_ref, gain_ref, t_s):
    depth = proj_ref.shape[1]

    def write(rows, v):
        proj_ref[rows, :] = v[:, 0:depth]
        qd_ref[rows, :] = v[:, depth + QHW : depth + QFW]
        t_s[rows, 0:128] = v[:, depth : depth + 128]
        t_s[rows, 128:] = v[:, depth + 384 :]

    collect(ids_ref, sizes, (own_ref, got_ref), write)
    turned = jnp.transpose(t_s[...])
    qh_ref[...] = turned[0:QHW, :]
    gain_ref[...] = turned[128 + QFW - 384 : 128 + QFW - 384 + 1, :]


def end_query(sizes, ids, own, got):
    depth = own.shape[0] * own.shape[1] * 2
    return pl.pallas_call(
        functools.partial(end_query_kernel, sizes),
        out_shape=(
            jax.ShapeDtypeStruct((depth, depth), F32),
            jax.ShapeDtypeStruct((QHW, depth), F32),
            jax.ShapeDtypeStruct((depth, QDW), F32),
            jax.ShapeDtypeStruct((1, depth), F32),
        ),
        in_specs=[SCALAR] + [WHOLE] * 2,
        out_specs=[WHOLE] * 4,
        scratch_shapes=[pltpu.VMEM((depth, 256), F32)],
        compiler_params=pltpu.CompilerParams(vmem_limit_bytes=40 << 20),
        name="end_query",
    )(ids, own, got)


def end_key_kernel(sizes, ids_ref, own_ref, got_ref, kd_ref, vd_ref, kh_ref, vh_ref, gain_ref, t_s):
    def write(rows, v):
        kd_ref[rows, :] = v[:, 0:KDW]
        vd_ref[rows, :] = v[:, KDW : 2 * KDW]
        t_s[rows, :] = v[:, 2 * KDW :]

    collect(ids_ref, sizes, (own_ref, got_ref), write)
    turned = jnp.transpose(t_s[...])
    kh_ref[...] = turned[0:KHW, :]
    vh_ref[...] = turned[KHW : 2 * KHW, :]
    gain_ref[...] = turned[2 * KHW : 2 * KHW + 1, :]


def end_key(sizes, ids, own, got):
    depth = own.shape[0] * own.shape[1] * 2
    return pl.pallas_call(
        functools.partial(end_key_kernel, sizes),
        out_shape=(
            jax.ShapeDtypeStruct((depth, KDW), F32),
            jax.ShapeDtypeStruct((depth, KDW), F32),
            jax.ShapeDtypeStruct((KHW, depth), F32),
            jax.ShapeDtypeStruct((KHW, depth), F32),
            jax.ShapeDtypeStruct((1, depth), F32),
        ),
        in_specs=[SCALAR] + [WHOLE] * 2,
        out_specs=[WHOLE] * 5,
        scratch_shapes=[pltpu.VMEM((depth, 128), F32)],
        name="end_key",
    )(ids, own, got)


def after(v, *others):
    return lax.optimization_barrier((v,) + others)[0]


class Grid:
    def __init__(self, dp, tensor):
        self.c = 2
        self.y = dp // 2
        self.x = self.y if tensor % self.y == 0 else 1
        self.z = tensor // self.x
        self.dp, self.tensor = dp, tensor
        self.axes = {
            "c": ("dp", 1, self.c),
            "y": ("dp", self.c, self.y),
            "x": ("tensor", 1, self.x),
            "z": ("tensor", self.x, self.z),
        }

    def size(self, g):
        return self.axes[g][2]

    def place(self, g):
        axis, stride, size = self.axes[g]
        return ((lax.axis_index(axis) // stride) % size).astype(jnp.int32)

    def swap(self, v, g, r):
        axis, stride, size = self.axes[g]
        total = self.dp if axis == "dp" else self.tensor
        return lax.ppermute(v, axis, [(i, i ^ (r * stride)) for i in range(total)])

    def bits(self, g):
        return [1 << k for k in range(self.size(g).bit_length() - 1)]

    def rels(self, g):
        order = [0]
        for bit in reversed(self.bits(g)):
            order = order + [r ^ bit for r in order]
        return order

    def stack(self, v, g):
        v = v[None]
        for bit in reversed(self.bits(g)):
            v = jnp.concatenate([v, self.swap(v, g, bit)], axis=0)
        return v

    def unstack(self, v, g, last=BF):
        bits = self.bits(g)
        for k, bit in enumerate(bits):
            rows = v.shape[0] // 2
            got = self.swap(v[rows:].astype(BF), g, bit)
            v = v[:rows].astype(F32) + got.astype(F32)
        return v[0].astype(last)

    def direct(self, v, g):
        return [v] + [self.swap(v, g, r) for r in self.rels(g)[1:]]

    def swap_masks(self, v, dp_mask, tensor_mask):
        if not tensor_mask:
            return lax.ppermute(v, "dp", [(i, i ^ dp_mask) for i in range(self.dp)])
        if not dp_mask:
            return lax.ppermute(v, "tensor", [(i, i ^ tensor_mask) for i in range(self.tensor)])
        mask = dp_mask * self.tensor + tensor_mask
        pairs = [(i, i ^ mask) for i in range(self.dp * self.tensor)]
        return lax.ppermute(v, ("dp", "tensor"), pairs)

    def levels(self, plan):
        out = []
        for letters in plan:
            masks = [(0, 0)]
            for g in letters:
                axis, stride, size = self.axes[g]
                masks = [
                    (d + r * stride, t) if axis == "dp" else (d, t + r * stride)
                    for d, t in masks
                    for r in range(size)
                ]
            out.append(masks)
        return out

    def numbers(self, plan):
        out = []
        for letters in plan:
            number = jnp.int32(0)
            for g in letters:
                number = number * self.size(g) + self.place(g)
            out.append(number)
        return jnp.stack(out)

    def sum_all(self, kept, sent, plan, shared):
        levels = self.levels(plan)
        v = kept.astype(F32) + self.swap_masks(sent, *levels[0][1]).astype(F32)
        for masks in levels[1:]:
            low = v.astype(BF)
            total = v[0]
            for m in range(1, len(masks)):
                total = total + self.swap_masks(low[m], *masks[m]).astype(F32)
            v = total
        for masks in self.levels(shared):
            low = v.astype(BF)
            for m in masks[1:]:
                v = v + self.swap_masks(low, *m).astype(F32)
        v = v.astype(BF)
        for masks in reversed(levels[1:]):
            v = jnp.stack([v] + [self.swap_masks(v, *m) for m in masks[1:]])
        return v, self.swap_masks(v, *levels[0][1])


def ffn_kernel(parts, plan, shards, blend, scal_ref, xf_ref, dy_ref, *refs):
    own, arrays = plan
    count = (3 if own else 0) + len(arrays)
    sources, refs = refs[:count], refs[count:]
    if blend:
        mixed_in, dxf_in = refs[:2]
        refs = refs[2:]
    mixed_ref, dxf_ref, inner_ref, dgate_ref, dup_ref, w_s, sem = refs
    width = w_s.shape[2]
    rows = w_s.shape[3] // parts
    copies = []

    def move(source, target):
        copies.append(pltpu.make_async_copy(source, target, sem.at[len(copies)]))

    if own:
        for k in range(3):
            move(sources[k], w_s.at[k, 0])
    for (slots, q), source in zip(arrays, sources[3 if own else 0 :]):
        place = pl.multiple_of((scal_ref[0] ^ q) * rows, rows)
        for i, slot in enumerate(slots):
            move(source.at[i], w_s.at[:, slot, :, pl.ds(place, rows)])
    for copy in copies:
        copy.start()
    for copy in copies:
        copy.wait()
    xf, dy = xf_ref[...], dy_ref[...]
    units, unused, hidden = inner_ref.shape
    for s in range(units):
        wg, wu, wd = ((w_s[k] if units == 1 else w_s[k, s]).reshape(hidden, -1) for k in range(3))
        gate = mm(xf, wg, 1, 1)
        up = mm(xf, wu, 1, 1)
        d_inner = mm(dy, wd, 1, 1)
        sig = 1.0 / (1.0 + jnp.exp(-gate))
        act = gate * sig
        inner = (act * up).astype(BF)
        d_gate = (d_inner * up * sig * (1.0 + gate * (1.0 - sig))).astype(BF)
        d_up = (d_inner * act).astype(BF)
        inner_ref[s] = inner
        dgate_ref[s] = d_gate
        dup_ref[s] = d_up
        dxf = mm(d_gate, wg) + mm(d_up, wu)
        mixed = mm(inner, wd)
        if s == 0 and blend:
            dxf, mixed = dxf + dxf_in[...], mixed + mixed_in[...]
        if s > 0:
            dxf, mixed = dxf + total[0], mixed + total[1]
        total = (dxf, mixed)
    dxf_ref[...] = total[0].astype(dxf_ref.dtype)
    mixed_ref[...] = total[1].astype(mixed_ref.dtype)


def ffn(mine, xf, dy, own, arrays, parts, width, before, out_type, name):
    length, depth = xf.shape
    shards = (1 if own else 0) + sum(len(slots) for slots, q, v in arrays if q == 0)
    hidden = (1, length, shards * width) if width % 16 == 0 else (shards, length, width)
    plan = (bool(own), [(slots, q) for slots, q, v in arrays])
    sources = list(own) + [v for slots, q, v in arrays]
    moves = (3 if own else 0) + sum(len(slots) for slots, q, v in arrays)
    return pl.pallas_call(
        functools.partial(ffn_kernel, parts, plan, shards, bool(before)),
        out_shape=(jax.ShapeDtypeStruct((length, depth), out_type),) * 2
        + (jax.ShapeDtypeStruct(hidden, BF),) * 3,
        in_specs=[SCALAR, WHOLE, WHOLE] + [RAW] * len(sources) + [WHOLE] * len(before),
        out_specs=[WHOLE] * 5,
        scratch_shapes=[
            pltpu.VMEM((3, shards, width, depth), BF),
            pltpu.SemaphoreType.DMA((moves,)),
        ],
        compiler_params=pltpu.CompilerParams(vmem_limit_bytes=58 << 20),
        cost_estimate=SMALL,
        name=name,
    )(mine, xf, dy, *sources, *before)


def products(lefts, rights, width, write):
    slot = 0
    for group in range(len(lefts[0])):
        units, unused, hidden = lefts[0][group].shape
        for s in range(units):
            total = None
            for b in range(len(rights)):
                term = mm(jnp.transpose(lefts[b][group][s]), rights[b][...])
                total = term if total is None else total + term
            for i in range(hidden // width):
                write(slot, total[i * width : (i + 1) * width, :])
                slot += 1


def divide(refs, blocks):
    each = len(refs) // blocks
    return [refs[b * each : (b + 1) * each] for b in range(blocks)]


def store(outs, scal_ref, t_s, slot, first, value):
    rows, lanes = value.shape[0], outs[0].shape[3]
    t_s[0:rows, :] = value
    for q in range(2 * outs[0].shape[0]):
        place = pl.multiple_of((scal_ref[0] ^ q) * lanes, lanes)
        part = t_s[0:rows, pl.ds(place, lanes)]
        outs[q % 2][q // 2, slot, first : first + rows, :] = part.astype(BF)


def gate_up_kernel(blocks, scal_ref, *refs):
    xfs, outs, t_s = refs[:blocks], refs[-3:-1], refs[-1]
    rest = refs[blocks:-3]
    width = outs[0].shape[2] // 2
    for k in range(2):
        lefts = divide(rest[k * len(rest) // 2 : (k + 1) * len(rest) // 2], blocks)

        def write(slot, value, k=k):
            store(outs, scal_ref, t_s, slot, k * width, value)

        products(lefts, xfs, width, write)


def down_kernel(blocks, scal_ref, *refs):
    dys, outs, t_s = refs[:blocks], refs[-3:-1], refs[-1]
    width = outs[0].shape[2]

    def write(slot, value):
        store(outs, scal_ref, t_s, slot, 0, value)

    products(divide(refs[blocks:-3], blocks), dys, width, write)


def grads(kernel, mine, wholes, parts, zs, rows, depth, scratch, name):
    return pl.pallas_call(
        kernel,
        out_shape=(jax.ShapeDtypeStruct((parts // 2, zs, rows, depth // parts), BF),) * 2,
        in_specs=[SCALAR] + [WHOLE] * len(wholes),
        out_specs=[WHOLE] * 2,
        scratch_shapes=scratch,
        compiler_params=pltpu.CompilerParams(vmem_limit_bytes=58 << 20),
        cost_estimate=SMALL,
        name=name,
    )(mine, *wholes)


def unpack_kernel(scal_ref, first_ref, second_ref, gate_ref, up_ref, down_ref):
    width = gate_ref.shape[0]
    gate_ref[...] = first_ref[0, 0:width, :].astype(F32)
    up_ref[...] = first_ref[0, width:, :].astype(F32)
    down_ref[...] = second_ref[0].astype(F32)


def unpack(mine, first, second):
    parts, width, lanes = second.shape
    column = pl.BlockSpec((width, lanes), lambda q, s: (0, s[0] ^ q))
    return pl.pallas_call(
        unpack_kernel,
        out_shape=(jax.ShapeDtypeStruct((width, parts * lanes), F32),) * 3,
        grid_spec=pltpu.PrefetchScalarGridSpec(
            num_scalar_prefetch=1,
            grid=(parts,),
            in_specs=[
                pl.BlockSpec((1, 2 * width, lanes), lambda q, s: (q, 0, 0)),
                pl.BlockSpec((1, width, lanes), lambda q, s: (q, 0, 0)),
            ],
            out_specs=[column] * 3,
        ),
        compiler_params=pltpu.CompilerParams(dimension_semantics=("arbitrary",)),
        name="unpack",
    )(mine, first, second)


def spread_pieces(grid, got, tie):
    entries = []
    for k in range(grid.y):
        piece = got if k == 0 else grid.swap(got, "y", k)
        entries.append((2 * k, piece))
    return [
        pair
        for q, piece in entries
        for pair in ((q, piece), (q + 1, grid.swap(after(piece, tie), "c", 1)))
    ]


def reduce_core(grid, even, odd):
    held = even.astype(F32) + grid.swap(odd, "c", 1).astype(F32)
    return [held[0]] + [held[k].astype(BF) for k in range(1, grid.y)]


def reduce_part(grid, held):
    total = held[0]
    for k in range(1, grid.y):
        total = total + grid.swap(held[k], "y", k).astype(F32)
    return grid.unstack(total.astype(BF), "z")


def spread_part(grid, mine):
    column = [mine] + [grid.swap(mine, "y", k) for k in range(1, grid.y)]
    pieces = []
    for piece in column:
        pieces += [piece, grid.swap(piece, "c", 1)]
    return jnp.stack(pieces)


def contract(left, right, left_dim, right_dim):
    return lax.dot_general(
        left, right, (((left_dim,), (right_dim,)), ((), ())), preferred_element_type=jnp.float32
    )


def norm_back(grad_out, normed, inverse, gain):
    scaled = grad_out * gain
    gain_part = jnp.sum(grad_out * normed, axis=0)
    grad_in = inverse * (scaled - normed * jnp.mean(scaled * normed, axis=-1, keepdims=True))
    return (grad_in, gain_part)


def body(
    grid,
    tokens,
    cotangent,
    segments,
    positions,
    attngain,
    ffngain,
    queryheads,
    querydims,
    keyheads,
    keydims,
    valueheads,
    valuedims,
    outproj,
    gateproj,
    upproj,
    downproj,
):
    x = tokens[0]
    upstream = cotangent[0]
    length, depth = x.shape
    parts = grid.dp
    lanes = depth // parts
    me = lax.axis_index("tensor").astype(jnp.int32)
    spot = jnp.stack([lax.axis_index("dp").astype(jnp.int32), grid.place("z")])
    offset = me * length
    places = lax.dynamic_slice_in_dim(positions[0], offset, length)
    half = HEAD_DIM // 2
    freqs = 10000.0 ** (-jnp.arange(half, dtype=F32) * 2.0 / HEAD_DIM)
    angles = freqs[:, None] * places.astype(F32)[None, :]
    cosine, sine = jnp.cos(angles), jnp.sin(angles)
    start = (offset + jnp.arange(length, dtype=jnp.int32) - places)[:, None]
    scal = jnp.stack([jnp.maximum(offset - places[0], 0) // length, me]).astype(jnp.int32)
    weights = (queryheads.T, querydims, keyheads.T, keydims, valueheads.T, valuedims)

    own = (gateproj.T, upproj.T, downproj)
    width = downproj.shape[0]
    payload = jnp.stack(
        [lax.dynamic_slice_in_dim(v, spot[0] * lanes, lanes, 1) for v in own]
    )
    dys = [upstream] + [grid.swap(upstream, "x", r) for r in range(1, grid.x)]
    far = grid.bits("z")[::-1]
    held, rels = payload[None], [0]

    xa, qfac, fac = enter(x, attngain[None, :], weights, cosine, sine)
    near = jnp.stack(grid.direct(fac, "z"))
    held = after(held, near)
    arrived = [grid.swap(held, "z", far[0])] if far else []
    facs = [near] + [grid.swap(near, "x", r) for r in range(1, grid.x)]
    stages = []
    for k, bit in enumerate(far):
        got = arrived[k]
        new = [r ^ bit for r in rels]
        if k + 1 < len(far):
            held = jnp.concatenate([held, got], axis=0)
            arrived.append(grid.swap(held, "z", far[k + 1]))
        rels = rels + new
        stages.append((new, got))
    qfac = after(qfac, held, *dys[1:])
    attn_out, lse = attention_forward(scal, qfac, facs, start)
    stages = [
        [
            (new, q, v)
            for q, v in spread_pieces(
                grid, after(got, attn_out) if k == len(stages) - 1 else got, attn_out
            )
        ]
        for k, (new, got) in enumerate(stages)
    ]

    local = x.astype(F32)
    residual = local + jnp.dot(attn_out, outproj, preferred_element_type=jnp.float32)
    inverse_two = lax.rsqrt(jnp.mean(residual * residual, axis=-1, keepdims=True) + EPS)
    normed_two = residual * inverse_two
    input_two = (normed_two * ffngain).astype(jnp.bfloat16)
    xfs = [input_two] + [grid.swap(input_two, "x", r) for r in range(1, grid.x)]

    early, late, filled = [], [], 1
    for entries in stages[:-1]:
        for rels, q, v in entries:
            early.append(([filled + i for i in range(len(rels))], q, v))
        filled += len(entries[0][0])
    for rels, q, v in stages[-1] if stages else []:
        late.append((list(range(len(rels))), q, v))


    results = [None] * grid.x
    firsts = []
    for k in range(grid.x):
        kind = BF if k and not late else F32
        if k:
            xfs[k] = after(xfs[k], firsts[0][0])
        firsts.append(
            ffn(spot, xfs[k], dys[k], own, early, parts, width, (), kind, "ffn_early")
        )
    for k in reversed(range(grid.x)):
        first = firsts[k]
        if late:
            second = ffn(
                spot, xfs[k], dys[k], (), late, parts, width, first[:2], BF if k else F32, "ffn_late"
            )
            results[k] = (second[0], second[1]) + tuple(
                [first[i], second[i]] for i in range(2, 5)
            )
        else:
            results[k] = (first[0], first[1]) + tuple([first[i]] for i in range(2, 5))
    d_norm_two, ffn_out = results[0][1], results[0][0]
    inners, dgates, dups = (
        [v for k in range(grid.x) for v in results[k][i]] for i in range(2, 5)
    )
    first_parts = grads(
        functools.partial(gate_up_kernel, grid.x),
        spot, xfs + dgates + dups, parts, grid.z, 2 * width, depth,
        [pltpu.VMEM((width, depth), F32)], "gate_up_grads",
    )
    second_parts = grads(
        functools.partial(down_kernel, grid.x),
        spot, dys + inners, parts, grid.z, width, depth,
        [pltpu.VMEM((width, depth), F32)], "down_grads",
    )
    first_held = reduce_core(grid, *first_parts)
    for r in range(1, grid.x):
        got = grid.swap(results[r][1], "x", r)
        d_norm_two = d_norm_two + after(got, second_parts[0], first_held[0]).astype(F32)
    grad_through, ffngain_part = norm_back(d_norm_two, normed_two, inverse_two, ffngain)
    d_residual = upstream.astype(jnp.float32) + grad_through
    d_res_low = d_residual.astype(jnp.bfloat16)
    d_attended = contract(d_res_low, outproj, 1, 1).astype(jnp.bfloat16)
    d_attended = after(d_attended, first_held[-1])
    back = attention_backward(
        scal, qfac, facs, start, attn_out, d_attended, lse, cosine, sine
    )
    terms, dq = back[:-1], back[-1]
    near = terms[0].astype(F32)
    for r in range(1, grid.x):
        near = near + grid.swap(terms[r], "x", r).astype(F32)
    low = near.astype(BF)
    key_grads = near[0]
    for k, r in enumerate(grid.rels("z")):
        if k:
            key_grads = key_grads + grid.swap(low[k], "z", r).astype(F32)

    for r in range(1, grid.x):
        ffn_out = ffn_out + grid.swap(after(results[r][0], d_res_low), "x", r).astype(F32)
    mixed = (residual + ffn_out).astype(jnp.bfloat16)

    first_mine = reduce_part(grid, first_held)
    second_mine = reduce_part(grid, reduce_core(grid, *second_parts))
    gate_part, up_part, down_part = unpack(
        spot, spread_part(grid, first_mine), spread_part(grid, second_mine)
    )

    plan, shared = ("c", "xy", "z"), ()
    if depth // (parts * grid.tensor) < 16:
        plan, shared = ("c", "xy"), ("z",)
    sizes = tuple(len(masks) for masks in grid.levels(plan))
    ids = grid.numbers(plan)
    shape = sizes[1:] + (depth // math.prod(sizes), -1)
    tokens_grad, kept, sent = leave_key(
        sizes, ids, x, xa, attngain[None, :], d_residual, dq, key_grads, cosine, sine, weights
    )
    sums = grid.sum_all(kept.reshape(shape), sent.reshape(shape), plan, shared)
    flat = [v.reshape(kept.shape) for v in sums]
    kd_grad, vd_grad, kh_grad, vh_grad, again_grad = end_key(sizes, ids, *flat)
    kept, sent = leave_query(sizes, ids, xa, dq, ffngain_part[None, :], attn_out, d_res_low)
    sums = grid.sum_all(kept.reshape(shape), sent.reshape(shape), plan, shared)
    flat = [v.reshape(kept.shape) for v in sums]
    out_part, qh_grad, qd_grad, fgain_grad = end_query(sizes, ids, *flat)
    return (
        mixed[None],
        tokens_grad[None],
        again_grad[0],
        fgain_grad[0],
        qh_grad.T,
        qd_grad,
        kh_grad.T,
        kd_grad,
        vh_grad.T,
        vd_grad,
        out_part,
        gate_part.T,
        up_part.T,
        down_part,
    )


def solution(mesh):
    grid = Grid(mesh.shape["dp"], mesh.shape["tensor"])
    rows = P("dp", "tensor", None)
    placed = (rows, rows, P("dp", None), P("dp", None)) + (P(),) * 9
    halves = (P(None, "tensor"), P(None, "tensor"), P("tensor", None))
    return jax.shard_map(
        functools.partial(body, grid),
        mesh=mesh,
        in_specs=placed + halves,
        out_specs=(rows, rows) + (P(),) * 9 + halves,
        check_vma=False,
    )
```

time: 656 us -> 461 us (0.70)
  waiting for transfers between devices: 445 us -> 176 us
  starting transfers between devices: 53.5 us -> 129 us
  Pallas kernels: 30.5 us -> 96 us
  matrix products: 41.5 us -> 3.39 us
  local copies, waits for them, and re-layouts: 41 us -> 25.9 us
  between operations: 15.4 us -> 2.55 us
    reduce_scatter x2 -> x0, waiting for transfers between devices: 160 us -> none  [the longest x1 89.9 us: body(): lax.psum_scatter(jnp.dot(inner, downproj, preferred_element_type=jnp.floa...]
    all_gather x2 -> x0, waiting for transfers between devices: 158 us -> none  [the longest x1 93 us: body(): whole_two = lax.all_gather(input_two, 'tensor', axis=0, tiled=True)]
    ppermute x0 -> x28, waiting for transfers between devices: none -> 66.7 us  [the longest x8 37.8 us: swap_masks(): return lax.ppermute(v, 'dp', [(i, i ^ dp_mask) for i in range(self.dp)])]
    pallas_call x4 -> x13, Pallas kernels: 29.1 us -> 94.1 us  [the longest x4 32.3 us: ffn(): pl.pallas_call(functools.partial(ffn_kernel, parts, plan, shards, bool(be...]
    ppermute x0 -> x28, starting transfers between devices: none -> 43.3 us  [the longest x16 27.2 us: swap_masks(): lax.ppermute(v, 'tensor', [(i, i ^ tensor_mask) for i in range(self.tenso...]
    ppermute x44 -> x34, starting transfers between devices: 53.1 us -> 86.2 us  [swap(): return lax.ppermute(v, axis, [(i, i ^ r * stride) for i in range(total)])]
    psum x1 -> x0, waiting for transfers between devices: 33 us -> none  [body(): lax.psum(gate_part.astype(jnp.bfloat16), 'dp').astype(jnp.float32)]
    dot_general x6 -> x1, matrix products: 25.5 us -> 1.54 us  [contract(): lax.dot_general(left, right, (((left_dim,), (right_dim,)), ((), ())), pre...]
  transfers between devices with their start and end apart: 49 -> 62, of which waited for: 28 -> 25; matrix products, arithmetic and copies ran while one was open for 11% -> 7% of each run, Pallas kernels for 3% -> 14%
where the time goes in v2:
time: 461 us; the launch traced here: 456 us
  waiting for transfers between devices  176 us (38%)
  starting transfers between devices  129 us (28%)
  Pallas kernels  96 us (21%)
  local copies, waits for them, and re-layouts  25.9 us (6%)
  other arithmetic  23.3 us (5%)
    ppermute x34, waiting for transfers between devices, swap(): return lax.ppermute(v, axis, [(i, i ^ r * stride) for i in range(total)])  109 us
    ppermute x34, starting transfers between devices, swap(): return lax.ppermute(v, axis, [(i, i ^ r * stride) for i in range(total)])  86.2 us
    ppermute x8, waiting for transfers between devices, swap_masks(): return lax.ppermute(v, 'dp', [(i, i ^ dp_mask) for i in range(self.dp)])  37.8 us
    pallas_call x4, Pallas kernels, ffn(): pl.pallas_call(functools.partial(ffn_kernel, parts, plan, shards, bool(be...  32.3 us
    ppermute x16, starting transfers between devices, swap_masks(): lax.ppermute(v, 'tensor', [(i, i ^ tensor_mask) for i in range(self.tenso...  27.2 us
    ppermute x16, waiting for transfers between devices, swap_masks(): lax.ppermute(v, 'tensor', [(i, i ^ tensor_mask) for i in range(self.tenso...  26 us
    unnamed x107, local copies, waits for them, and re-layouts  17.5 us
    pallas_call x1, Pallas kernels, attention_backward(): pl.pallas_call(functools.partial(backward_kernel, across), out_shape=(jax...  14.4 us
  transfers between devices with their start and end apart: 62, of which 25 were waited for; matrix products, arithmetic and copies ran while one was open for 7% of the time, Pallas kernels for 14%

profile of v2, /device:TPU:0, one launch (start us, length us, event | category | flops | bytes accessed | tf_op | source)
XLA Modules:
  0.0 456.2 jit_solution(2970906895970926593)
XLA Ops:
  12.6 5.1 %collective-permute-start.2 = (bf16[320,256]{1,0:T(8,128)(2,1)S(1)}, bf16[320,256]{1,0:T(8,128)(2,1)S(1)}, u32[]{:S(2)}, u32[]{:S(2)}) collective-permute-start(bf16[320,256]{1,0:T(8,128)(2,1)S(1)} %get-tuple-element.75), channel_id=1, source_target_pairs={{0,6},{1,7},{2,4},{3,5},{4,2},{5,3},{6,0},{7,1},{8,14},{9,15},{10,... | collective-permute-start | bytes 491528 | tf_op jit(solution)/shard_map/ppermute | solution.py:606
  22.8 3.7 collective-permute-done.1
  26.5 5.2 %collective-permute-done = bf16[320,256]{1,0:T(8,128)(2,1)} collective-permute-done((bf16[320,256]{1,0:T(8,128)(2,1)S(1)}, bf16[320,256]{1,0:T(8,128)(2,1)}, u32[]{:S(2)}, u32[]{:S(2)}) %collective-permute-start) | collective-permute-done | bytes 163872 | tf_op jit(solution)/shard_map/ppermute | solution.py:606
  34.5 24.6 %collective-permute-done.3.refs_3_ = bf16[1,3,352,256]{3,2,1,0:T(8,128)(2,1)} collective-permute-done((bf16[1,3,352,256]{3,2,1,0:T(8,128)(2,1)S(1)}, bf16[1,3,352,256]{3,2,1,0:T(8,128)(2,1)}, u32[]{:S(2)}, u32[]{:S(2)}) %collective-permute-start.3) | collective-permute-done | bytes 540704 | tf_op jit(solution)/shard_map/ppermute | solution.py:606
  66.5 22.8 %collective-permute-done.4.dy_ref.refs_1_ = bf16[256,1024]{1,0:T(8,128)(2,1)} collective-permute-done((bf16[256,1024]{1,0:T(8,128)(2,1)S(1)}, bf16[256,1024]{1,0:T(8,128)(2,1)}, u32[]{:S(2)}, u32[]{:S(2)}) %collective-permute-start.4) | collective-permute-done | bytes 524320 | tf_op jit(solution)/shard_map/ppermute | solution.py:606
  89.3 11.8 %attention_forward.1 = (bf16[256,1024]{1,0:T(8,128)(2,1)}, f32[16,256,128]{2,1,0:T(8,128)}) custom-call(s32[2]{0:T(128)} %pad_add_fusion.scal_ref, bf16[480,256]{1,0:T(8,128)(2,1)} %copy-done.18, bf16[4,320,256]{2,1,0:T(8,128)(2,1)} %pad_maximum_fusion.3.refs_0_, bf16[4,320,256]{2,1,0:T(8,128)(2,1)} %collective-permute-done.5.refs_1_, ...), custom_call_target="tpu_custom_call" | custom-call | flops 1000 | bytes 1000 | tf_op jit(solution)/shard_map/attention_forward/pallas_call | solution.py:158
  103.7 24.5 %collective-permute-done.8.refs_2_ = bf16[2,3,352,256]{3,2,1,0:T(8,128)(2,1)} collective-permute-done((bf16[2,3,352,256]{3,2,1,0:T(8,128)(2,1)}, bf16[2,3,352,256]{3,2,1,0:T(8,128)(2,1)}, u32[]{:S(2)}, u32[]{:S(2)}) %collective-permute-start.8) | collective-permute-done | bytes 1081376 | tf_op jit(solution)/shard_map/ppermute | solution.py:606
  130.1 7.9 %collective-permute-done.11.refs_5_ = bf16[1,3,352,256]{3,2,1,0:T(8,128)(2,1)} collective-permute-done((bf16[1,3,352,256]{3,2,1,0:T(8,128)(2,1)}, bf16[1,3,352,256]{3,2,1,0:T(8,128)(2,1)}, u32[]{:S(2)}, u32[]{:S(2)}) %collective-permute-start.11) | collective-permute-done | bytes 540704 | tf_op jit(solution)/shard_map/ppermute | solution.py:606
  138.2 6.0 %collective-permute-start.13 = (bf16[256,1024]{1,0:T(8,128)(2,1)S(1)}, bf16[256,1024]{1,0:T(8,128)(2,1)}, u32[]{:S(2)}, u32[]{:S(2)}) collective-permute-start(bf16[256,1024]{1,0:T(8,128)(2,1)S(1)} %multiply_convert_fusion.xf_ref.refs_0_), channel_id=1, source_target_pairs={{0,1},{1,0},{2,3},{3,2},{4,5},{5,4},{6,7},{7,6},{8,9},{9,8},{10,11... | collective-permute-start | bytes 1572872 | tf_op jit(solution)/shard_map/ppermute | solution.py:606
  144.8 7.9 %ffn_early.2 = (f32[256,1024]{1,0:T(8,128)}, f32[256,1024]{1,0:T(8,128)}, bf16[1,256,704]{2,1,0:T(8,128)(2,1)}, bf16[1,256,704]{2,1,0:T(8,128)(2,1)}, bf16[1,256,704]{2,1,0:T(8,128)(2,1)}) custom-call(s32[2]{0:T(128)} %pad_add_fusion.1.scal_ref, bf16[256,1024]{1,0:T(8,128)(2,1)} %copy-done.40, bf16[256,1024]{1,0:T(8,128)(2,1)} %bitcast.198, ...), custom_call_target="tpu_custom_call" | custom-call | flops 1000 | bytes 1000 | tf_op jit(solution)/shard_map/ffn_early/pallas_call | solution.py:744
  152.7 4.2 collective-permute-done.13.xf_ref.refs_1_
  156.9 7.9 %ffn_early.3 = (f32[256,1024]{1,0:T(8,128)}, f32[256,1024]{1,0:T(8,128)}, bf16[1,256,704]{2,1,0:T(8,128)(2,1)}, bf16[1,256,704]{2,1,0:T(8,128)(2,1)}, bf16[1,256,704]{2,1,0:T(8,128)(2,1)}) custom-call(s32[2]{0:T(128)} %pad_add_fusion.1.scal_ref, bf16[256,1024]{1,0:T(8,128)(2,1)} %collective-permute-done.13.xf_ref.refs_1_, ...), custom_call_target="tpu_custom_call" | custom-call | flops 1000 | bytes 1000 | tf_op jit(solution)/shard_map/ffn_early/pallas_call | solution.py:744
  164.8 8.5 %ffn_late.2 = (f32[256,1024]{1,0:T(8,128)}, f32[256,1024]{1,0:T(8,128)}, bf16[1,256,704]{2,1,0:T(8,128)(2,1)}, bf16[1,256,704]{2,1,0:T(8,128)(2,1)}, bf16[1,256,704]{2,1,0:T(8,128)(2,1)}) custom-call(s32[2]{0:T(128)} %pad_add_fusion.1.scal_ref, bf16[256,1024]{1,0:T(8,128)(2,1)} %copy-done.40, bf16[256,1024]{1,0:T(8,128)(2,1)} %bitcast.199, ...), custom_call_target="tpu_custom_call" | custom-call | flops 1000 | bytes 1000 | tf_op jit(solution)/shard_map/ffn_late/pallas_call | solution.py:744
  173.2 8.1 %ffn_late.3 = (bf16[256,1024]{1,0:T(8,128)(2,1)}, bf16[256,1024]{1,0:T(8,128)(2,1)}, bf16[1,256,704]{2,1,0:T(8,128)(2,1)}, bf16[1,256,704]{2,1,0:T(8,128)(2,1)}, bf16[1,256,704]{2,1,0:T(8,128)(2,1)}) custom-call(s32[2]{0:T(128)} %pad_add_fusion.1.scal_ref, bf16[256,1024]{1,0:T(8,128)(2,1)} %collective-permute-done.13.xf_ref.refs_1_, ...), custom_call_target="tpu_custom_call" | custom-call | flops 1000 | bytes 1000 | tf_op jit(solution)/shard_map/ffn_late/pallas_call | solution.py:744
  181.3 9.0 %gate_up_grads.1 = (bf16[2,4,704,256]{3,2,1,0:T(8,128)(2,1)}, bf16[2,4,704,256]{3,2,1,0:T(8,128)(2,1)}) custom-call(s32[2]{0:T(128)} %pad_add_fusion.1.scal_ref, bf16[256,1024]{1,0:T(8,128)(2,1)} %copy-done.40, bf16[256,1024]{1,0:T(8,128)(2,1)} %collective-permute-done.13.xf_ref.refs_1_, bf16[1,256,704]{2,1,0:T(8,128)(2,1)} %get-tuple-element.98.refs_2_, ...), custom_call_target="tpu_custom_call" | custom-call | flops 1000 | bytes 1000 | tf_op jit(solution)/shard_map/gate_up_grads/pallas_call | solution.py:812
  192.2 5.3 %down_grads.1 = (bf16[2,4,352,256]{3,2,1,0:T(8,128)(2,1)}, bf16[2,4,352,256]{3,2,1,0:T(8,128)(2,1)}) custom-call(s32[2]{0:T(128)} %pad_add_fusion.1.scal_ref, bf16[256,1024]{1,0:T(8,128)(2,1)} %bitcast.200, bf16[256,1024]{1,0:T(8,128)(2,1)} %collective-permute-done.4.dy_ref.refs_1_, bf16[1,256,704]{2,1,0:T(8,128)(2,1)} %get-tuple-element.93.refs_2_, ...), custom_call_target="tpu_custom_call" | custom-call | flops 1000 | bytes 1000 | tf_op jit(solution)/shard_map/down_grads/pallas_call | solution.py:812
  197.6 7.3 %collective-permute-done.14 = bf16[256,1024]{1,0:T(8,128)(2,1)S(1)} collective-permute-done((bf16[256,1024]{1,0:T(8,128)(2,1)}, bf16[256,1024]{1,0:T(8,128)(2,1)S(1)}, u32[]{:S(2)}, u32[]{:S(2)}) %collective-permute-start.14) | collective-permute-done | bytes 524320 | tf_op jit(solution)/shard_map/ppermute | solution.py:606
  219.9 14.4 %attention_backward.1 = (bf16[4,320,256]{2,1,0:T(8,128)(2,1)}, bf16[4,320,256]{2,1,0:T(8,128)(2,1)}, bf16[480,256]{1,0:T(8,128)(2,1)}) custom-call(s32[2]{0:T(128)} %pad_add_fusion.scal_ref, bf16[480,256]{1,0:T(8,128)(2,1)} %copy-done.18, bf16[4,320,256]{2,1,0:T(8,128)(2,1)} %pad_maximum_fusion.3.refs_0_, ...), custom_call_target="tpu_custom_call" | custom-call | flops 1000 | bytes 1000 | tf_op jit(solution)/shard_map/attention_backward/pallas_call | solution.py:304
  234.3 7.6 %collective-permute-start.17 = (bf16[4,320,256]{2,1,0:T(8,128)(2,1)}, bf16[4,320,256]{2,1,0:T(8,128)(2,1)}, u32[]{:S(2)}, u32[]{:S(2)}) collective-permute-start(bf16[4,320,256]{2,1,0:T(8,128)(2,1)} %get-tuple-element.115), channel_id=1, source_target_pairs={{0,1},{1,0},{2,3},{3,2},{4,5},{5,4},{6,7},{7,6},{8,9},{9,8},{10,11... | collective-permute-start | bytes 1966088 | tf_op jit(solution)/shard_map/ppermute | solution.py:606
  248.1 13.2 %collective-permute-start.57 = (bf16[2,352,256]{2,1,0:T(8,128)(2,1)S(1)}, bf16[2,352,256]{2,1,0:T(8,128)(2,1)S(1)}, u32[]{:S(2)}, u32[]{:S(2)}) collective-permute-start(bf16[2,352,256]{2,1,0:T(8,128)(2,1)S(1)} %slice.166), channel_id=1, source_target_pairs={{0,2},{1,3},{2,0},{3,1},{4,6},{5,7},{6,4},{7,5},{8,10},{9,11},{10,... | collective-permute-start | bytes 1081352 | tf_op jit(solution)/shard_map/ppermute | solution.py:606
  262.8 29.1 %collective-permute-start.18 = (bf16[320,256]{1,0:T(8,128)(2,1)S(1)}, bf16[320,256]{1,0:T(8,128)(2,1)S(1)}, u32[]{:S(2)}, u32[]{:S(2)}) collective-permute-start(bf16[320,256]{1,0:T(8,128)(2,1)S(1)} %get-tuple-element.151), channel_id=1, source_target_pairs={{0,4},{1,5},{2,6},{3,7},{4,0},{5,1},{6,2},{7,3},{8,12},{9,13},{10,... | collective-permute-start | bytes 491528 | tf_op jit(solution)/shard_map/ppermute | solution.py:606
  296.0 7.2 %collective-permute-start.49 = (bf16[4,704,256]{2,1,0:T(8,128)(2,1)S(1)}, bf16[4,704,256]{2,1,0:T(8,128)(2,1)S(1)}, u32[]{:S(2)}, u32[]{:S(2)}) collective-permute-start(bf16[4,704,256]{2,1,0:T(8,128)(2,1)S(1)} %copy-done.45), channel_id=1, source_target_pairs={{0,16},{8,24},{16,0},{24,8},{1,17},{9,25},{17,1},{25,9},{2,18},{10... | collective-permute-start | bytes 4325384 | tf_op jit(solution)/shard_map/ppermute | solution.py:606
  306.3 4.6 %leave_key.1 = (bf16[256,1024]{1,0:T(8,128)(2,1)}, bf16[16,32,384]{2,1,0:T(8,128)(2,1)S(1)}, bf16[16,32,384]{2,1,0:T(8,128)(2,1)S(1)}) custom-call(s32[3]{0:T(128)S(1)} %pad_add_fusion.2.ids_ref, bf16[256,1024]{1,0:T(8,128)(2,1)S(1)} %bitcast.180, bf16[256,1024]{1,0:T(8,128)(2,1)S(1)} %copy-done.11, f32[1,1024]{1,0:T(1,128)S(1)} %bitcast.193, ...), custom_call_target="tpu_custom_call" | custom-call | flops 1000 | bytes 1000 | tf_op jit(solution)/shard_map/leave_key/pallas_call | solution.py:501
  311.7 3.5 collective-permute-start.36
  317.3 32.2 %collective-permute-done.36 = bf16[4,32,1536]{2,1,0:T(8,128)(2,1)S(1)} collective-permute-done((bf16[4,32,1536]{2,1,0:T(8,128)(2,1)S(1)}, bf16[4,32,1536]{2,1,0:T(8,128)(2,1)S(1)}, u32[]{:S(2)}, u32[]{:S(2)}) %collective-permute-start.36) | collective-permute-done | bytes 393248 | tf_op jit(solution)/shard_map/ppermute | solution.py:636
  351.6 4.4 collective-permute-start.39
  370.9 12.3 %collective-permute-done.44 = bf16[32,1536]{1,0:T(8,128)(2,1)S(1)} collective-permute-done((bf16[32,1536]{1,0:T(8,128)(2,1)S(1)}, bf16[32,1536]{1,0:T(8,128)(2,1)S(1)}, u32[]{:S(2)}, u32[]{:S(2)}) %collective-permute-start.44) | collective-permute-done | bytes 98336 | tf_op jit(solution)/shard_map/ppermute | solution.py:638
  390.0 3.6 collective-permute-done.46
  394.3 5.2 %collective-permute-done.45 = bf16[4,32,1536]{2,1,0:T(8,128)(2,1)S(1)} collective-permute-done((bf16[4,32,1536]{2,1,0:T(8,128)(2,1)S(1)}, bf16[4,32,1536]{2,1,0:T(8,128)(2,1)S(1)}, u32[]{:S(2)}, u32[]{:S(2)}) %collective-permute-start.45) | collective-permute-done | bytes 393248 | tf_op jit(solution)/shard_map/ppermute | solution.py:636
  412.5 4.5 collective-permute-start.29
  441.0 4.9 %unpack.1 = (f32[352,1024]{1,0:T(8,128)}, f32[352,1024]{1,0:T(8,128)}, f32[352,1024]{1,0:T(8,128)}) custom-call(s32[2]{0:T(128)} %pad_add_fusion.1.scal_ref, bf16[4,704,256]{2,1,0:T(8,128)(2,1)} %pad_maximum_fusion.1.first_ref, bf16[4,352,256]{2,1,0:T(8,128)(2,1)} %pad_maximum_fusion.2.second_ref), custom_call_target="tpu_custom_call" | custom-call | tf_op jit(solution)/shard_map/unpack/pallas_call | solution.py:834
  450.1 5.7 %end_query.1 = (f32[1024,1024]{1,0:T(8,128)}, f32[96,1024]{1,0:T(8,128)}, f32[1024,384]{1,0:T(8,128)}, f32[1,1024]{1,0:T(1,128)}) custom-call(s32[3]{0:T(128)S(1)} %copy-done.33, bf16[16,32,1536]{2,1,0:T(8,128)(2,1)S(1)} %bitcast.178, bf16[16,32,1536]{2,1,0:T(8,128)(2,1)S(1)} %bitcast.181), custom_call_target="tpu_custom_call" | custom-call | tf_op jit(solution)/shard_map/end_query/pallas_call | solution.py:531
  (269 shorter events, 131.7 us)
Async XLA Ops:
  17.7 14.0 %collective-permute-start = (bf16[320,256]{1,0:T(8,128)(2,1)S(1)}, bf16[320,256]{1,0:T(8,128)(2,1)}, u32[]{:S(2)}, u32[]{:S(2)}) collective-permute-start(bf16[320,256]{1,0:T(8,128)(2,1)S(1)} %get-tuple-element.75), channel_id=1, source_target_pairs={{0,4},{1,5},{2,6},{3,7},{4,0},{5,1},{6,2},{7,3},{8,12},{9,13},{10,... | collective-permute-start | bytes 491528 | tf_op jit(solution)/shard_map/ppermute | solution.py:606
  33.6 25.6 %collective-permute-start.3 = (bf16[1,3,352,256]{3,2,1,0:T(8,128)(2,1)S(1)}, bf16[1,3,352,256]{3,2,1,0:T(8,128)(2,1)}, u32[]{:S(2)}, u32[]{:S(2)}) collective-permute-start(bf16[1,3,352,256]{3,2,1,0:T(8,128)(2,1)S(1)} %maximum_bitcast_fusion), channel_id=1, source_target_pairs={{0,4},{1,5},{2,6},{3,7},{4,0},{5,1},{6,2},{7,3},{8,12},{9,13},{10,... | collective-permute-start | bytes 1622024 | tf_op jit(solution)/shard_map/ppermute | solution.py:606
  61.0 40.1 %collective-permute-start.6 = (bf16[2,3,352,256]{3,2,1,0:T(8,128)(2,1)}, bf16[2,3,352,256]{3,2,1,0:T(8,128)(2,1)}, u32[]{:S(2)}, u32[]{:S(2)}) collective-permute-start(bf16[2,3,352,256]{3,2,1,0:T(8,128)(2,1)} %constant_dynamic-update-slice_fusion), channel_id=1, source_target_pairs={{0,2},{1,3},{2,0},{3,1},{4,6},{5,7},{6,4},{7,5},{8,10},{9,11},{10,... | collective-permute-start | bytes 3244040 | tf_op jit(solution)/shard_map/ppermute | solution.py:606
  61.0 28.2 %collective-permute-start.5 = (bf16[4,320,256]{2,1,0:T(8,128)(2,1)}, bf16[4,320,256]{2,1,0:T(8,128)(2,1)}, u32[]{:S(2)}, u32[]{:S(2)}) collective-permute-start(bf16[4,320,256]{2,1,0:T(8,128)(2,1)} %pad_maximum_fusion.3.refs_0_), channel_id=1, source_target_pairs={{0,1},{1,0},{2,3},{3,2},{4,5},{5,4},{6,7},{7,6},{8,9},{9,8},{10,11... | collective-permute-start | bytes 1966088 | tf_op jit(solution)/shard_map/ppermute | solution.py:606
  62.5 26.7 %collective-permute-start.4 = (bf16[256,1024]{1,0:T(8,128)(2,1)S(1)}, bf16[256,1024]{1,0:T(8,128)(2,1)}, u32[]{:S(2)}, u32[]{:S(2)}) collective-permute-start(bf16[256,1024]{1,0:T(8,128)(2,1)S(1)} %bitcast.201), channel_id=1, source_target_pairs={{0,1},{1,0},{2,3},{3,2},{4,5},{5,4},{6,7},{7,6},{8,9},{9,8},{10,11... | collective-permute-start | bytes 1572872 | tf_op jit(solution)/shard_map/ppermute | solution.py:606
  101.1 27.1 %collective-permute-start.8 = (bf16[2,3,352,256]{3,2,1,0:T(8,128)(2,1)}, bf16[2,3,352,256]{3,2,1,0:T(8,128)(2,1)}, u32[]{:S(2)}, u32[]{:S(2)}) collective-permute-start(bf16[2,3,352,256]{3,2,1,0:T(8,128)(2,1)} %collective-permute-done.6.refs_0_), channel_id=1, source_target_pairs={{0,16},{8,24},{16,0},{24,8},{1,17},{9,25},{17,1},{25,9},{2,18},{10... | collective-permute-start | bytes 3244040 | tf_op jit(solution)/shard_map/ppermute | solution.py:606
  102.7 35.3 %collective-permute-start.11 = (bf16[1,3,352,256]{3,2,1,0:T(8,128)(2,1)}, bf16[1,3,352,256]{3,2,1,0:T(8,128)(2,1)}, u32[]{:S(2)}, u32[]{:S(2)}) collective-permute-start(bf16[1,3,352,256]{3,2,1,0:T(8,128)(2,1)} %collective-permute-done.3.refs_3_), channel_id=1, source_target_pairs={{0,16},{8,24},{16,0},{24,8},{1,17},{9,25},{17,1},{25,9},{2,18},{10... | collective-permute-start | bytes 1622024 | tf_op jit(solution)/shard_map/ppermute | solution.py:606
  103.2 41.6 %collective-permute-start.10 = (bf16[1,3,352,256]{3,2,1,0:T(8,128)(2,1)}, bf16[1,3,352,256]{3,2,1,0:T(8,128)(2,1)}, u32[]{:S(2)}, u32[]{:S(2)}) collective-permute-start(bf16[1,3,352,256]{3,2,1,0:T(8,128)(2,1)} %collective-permute-done.3.refs_3_), channel_id=1, source_target_pairs={{0,8},{8,0},{16,24},{24,16},{1,9},{9,1},{17,25},{25,17},{2,10},{10... | collective-permute-start | bytes 1622024 | tf_op jit(solution)/shard_map/ppermute | solution.py:606
  103.2 61.5 %collective-permute-start.7 = (bf16[2,3,352,256]{3,2,1,0:T(8,128)(2,1)}, bf16[2,3,352,256]{3,2,1,0:T(8,128)(2,1)}, u32[]{:S(2)}, u32[]{:S(2)}) collective-permute-start(bf16[2,3,352,256]{3,2,1,0:T(8,128)(2,1)} %collective-permute-done.6.refs_0_), channel_id=1, source_target_pairs={{0,8},{8,0},{16,24},{24,16},{1,9},{9,1},{17,25},{25,17},{2,10},{10... | collective-permute-start | bytes 3244040 | tf_op jit(solution)/shard_map/ppermute | solution.py:606
  128.2 36.5 %collective-permute-start.9 = (bf16[2,3,352,256]{3,2,1,0:T(8,128)(2,1)}, bf16[2,3,352,256]{3,2,1,0:T(8,128)(2,1)}, u32[]{:S(2)}, u32[]{:S(2)}) collective-permute-start(bf16[2,3,352,256]{3,2,1,0:T(8,128)(2,1)} %collective-permute-done.8.refs_2_), channel_id=1, source_target_pairs={{0,8},{8,0},{16,24},{24,16},{1,9},{9,1},{17,25},{25,17},{2,10},{10... | collective-permute-start | bytes 3244040 | tf_op jit(solution)/shard_map/ppermute | solution.py:606
  138.2 18.7 %collective-permute-start.13 = (bf16[256,1024]{1,0:T(8,128)(2,1)S(1)}, bf16[256,1024]{1,0:T(8,128)(2,1)}, u32[]{:S(2)}, u32[]{:S(2)}) collective-permute-start(bf16[256,1024]{1,0:T(8,128)(2,1)S(1)} %multiply_convert_fusion.xf_ref.refs_0_), channel_id=1, source_target_pairs={{0,1},{1,0},{2,3},{3,2},{4,5},{5,4},{6,7},{7,6},{8,9},{9,8},{10,11... | collective-permute-start | bytes 1572872 | tf_op jit(solution)/shard_map/ppermute | solution.py:606
  190.3 24.3 %collective-permute-start.15 = (bf16[2,4,704,256]{3,2,1,0:T(8,128)(2,1)}, bf16[2,4,704,256]{3,2,1,0:T(8,128)(2,1)}, u32[]{:S(2)}, u32[]{:S(2)}) collective-permute-start(bf16[2,4,704,256]{3,2,1,0:T(8,128)(2,1)} %get-tuple-element.107), channel_id=1, source_target_pairs={{0,8},{8,0},{16,24},{24,16},{1,9},{9,1},{17,25},{25,17},{2,10},{10... | collective-permute-start | bytes 8650760 | tf_op jit(solution)/shard_map/ppermute | solution.py:606
  190.4 14.5 %collective-permute-start.14 = (bf16[256,1024]{1,0:T(8,128)(2,1)}, bf16[256,1024]{1,0:T(8,128)(2,1)S(1)}, u32[]{:S(2)}, u32[]{:S(2)}) collective-permute-start(bf16[256,1024]{1,0:T(8,128)(2,1)} %get-tuple-element.92), channel_id=1, source_target_pairs={{0,1},{1,0},{2,3},{3,2},{4,5},{5,4},{6,7},{7,6},{8,9},{9,8},{10,11... | collective-permute-start | bytes 1572872 | tf_op jit(solution)/shard_map/ppermute | solution.py:606
  213.0 33.3 %collective-permute-start.56 = (bf16[4,352,256]{2,1,0:T(8,128)(2,1)S(1)}, bf16[4,352,256]{2,1,0:T(8,128)(2,1)}, u32[]{:S(2)}, u32[]{:S(2)}) collective-permute-start(bf16[4,352,256]{2,1,0:T(8,128)(2,1)S(1)} %fusion.6), channel_id=1, source_target_pairs={{0,16},{8,24},{16,0},{24,8},{1,17},{9,25},{17,1},{25,9},{2,18},{10... | collective-permute-start | bytes 2162696 | tf_op jit(solution)/shard_map/ppermute | solution.py:606
  234.3 27.0 %collective-permute-start.17 = (bf16[4,320,256]{2,1,0:T(8,128)(2,1)}, bf16[4,320,256]{2,1,0:T(8,128)(2,1)}, u32[]{:S(2)}, u32[]{:S(2)}) collective-permute-start(bf16[4,320,256]{2,1,0:T(8,128)(2,1)} %get-tuple-element.115), channel_id=1, source_target_pairs={{0,1},{1,0},{2,3},{3,2},{4,5},{5,4},{6,7},{7,6},{8,9},{9,8},{10,11... | collective-permute-start | bytes 1966088 | tf_op jit(solution)/shard_map/ppermute | solution.py:606
  246.1 64.9 %collective-permute-start.35 = (bf16[4,4,32,1536]{3,2,1,0:T(8,128)(2,1)S(1)}, bf16[4,4,32,1536]{3,2,1,0:T(8,128)(2,1)S(1)}, u32[]{:S(2)}, u32[]{:S(2)}) collective-permute-start(bf16[4,4,32,1536]{3,2,1,0:T(8,128)(2,1)S(1)} %bitcast.194), channel_id=1, source_target_pairs={{0,8},{8,0},{16,24},{24,16},{1,9},{9,1},{17,25},{25,17},{2,10},{10... | collective-permute-start | bytes 4718600 | tf_op jit(solution)/shard_map/ppermute | solution.py:636
  246.2 185.4 %collective-permute-start.16 = (bf16[256,1024]{1,0:T(8,128)(2,1)}, bf16[256,1024]{1,0:T(8,128)(2,1)S(1)}, u32[]{:S(2)}, u32[]{:S(2)}) collective-permute-start(bf16[256,1024]{1,0:T(8,128)(2,1)} %get-tuple-element.109), channel_id=1, source_target_pairs={{0,1},{1,0},{2,3},{3,2},{4,5},{5,4},{6,7},{7,6},{8,9},{9,8},{10,11... | collective-permute-start | bytes 1572872 | tf_op jit(solution)/shard_map/ppermute | solution.py:606
  248.1 43.9 %collective-permute-start.57 = (bf16[2,352,256]{2,1,0:T(8,128)(2,1)S(1)}, bf16[2,352,256]{2,1,0:T(8,128)(2,1)S(1)}, u32[]{:S(2)}, u32[]{:S(2)}) collective-permute-start(bf16[2,352,256]{2,1,0:T(8,128)(2,1)S(1)} %slice.166), channel_id=1, source_target_pairs={{0,2},{1,3},{2,0},{3,1},{4,6},{5,7},{6,4},{7,5},{8,10},{9,11},{10,... | collective-permute-start | bytes 1081352 | tf_op jit(solution)/shard_map/ppermute | solution.py:606
  262.8 33.1 %collective-permute-start.18 = (bf16[320,256]{1,0:T(8,128)(2,1)S(1)}, bf16[320,256]{1,0:T(8,128)(2,1)S(1)}, u32[]{:S(2)}, u32[]{:S(2)}) collective-permute-start(bf16[320,256]{1,0:T(8,128)(2,1)S(1)} %get-tuple-element.151), channel_id=1, source_target_pairs={{0,4},{1,5},{2,6},{3,7},{4,0},{5,1},{6,2},{7,3},{8,12},{9,13},{10,... | collective-permute-start | bytes 491528 | tf_op jit(solution)/shard_map/ppermute | solution.py:606
  292.0 14.1 %collective-permute-start.20 = (bf16[320,256]{1,0:T(8,128)(2,1)S(1)}, bf16[320,256]{1,0:T(8,128)(2,1)S(1)}, u32[]{:S(2)}, u32[]{:S(2)}) collective-permute-start(bf16[320,256]{1,0:T(8,128)(2,1)S(1)} %get-tuple-element.152), channel_id=1, source_target_pairs={{0,6},{1,7},{2,4},{3,5},{4,2},{5,3},{6,0},{7,1},{8,14},{9,15},{10,... | collective-permute-start | bytes 491528 | tf_op jit(solution)/shard_map/ppermute | solution.py:606
  292.0 14.1 %collective-permute-start.19 = (bf16[320,256]{1,0:T(8,128)(2,1)S(1)}, bf16[320,256]{1,0:T(8,128)(2,1)S(1)}, u32[]{:S(2)}, u32[]{:S(2)}) collective-permute-start(bf16[320,256]{1,0:T(8,128)(2,1)S(1)} %get-tuple-element.153), channel_id=1, source_target_pairs={{0,2},{1,3},{2,0},{3,1},{4,6},{5,7},{6,4},{7,5},{8,10},{9,11},{10,... | collective-permute-start | bytes 491528 | tf_op jit(solution)/shard_map/ppermute | solution.py:606
  296.0 62.6 %collective-permute-start.49 = (bf16[4,704,256]{2,1,0:T(8,128)(2,1)S(1)}, bf16[4,704,256]{2,1,0:T(8,128)(2,1)S(1)}, u32[]{:S(2)}, u32[]{:S(2)}) collective-permute-start(bf16[4,704,256]{2,1,0:T(8,128)(2,1)S(1)} %copy-done.45), channel_id=1, source_target_pairs={{0,16},{8,24},{16,0},{24,8},{1,17},{9,25},{17,1},{25,9},{2,18},{10... | collective-permute-start | bytes 4325384 | tf_op jit(solution)/shard_map/ppermute | solution.py:606
  311.7 37.9 %collective-permute-start.36 = (bf16[4,32,1536]{2,1,0:T(8,128)(2,1)S(1)}, bf16[4,32,1536]{2,1,0:T(8,128)(2,1)S(1)}, u32[]{:S(2)}, u32[]{:S(2)}) collective-permute-start(bf16[4,32,1536]{2,1,0:T(8,128)(2,1)S(1)} %get-tuple-element.144), channel_id=1, source_target_pairs={{0,16},{8,24},{16,0},{24,8},{1,17},{9,25},{17,1},{25,9},{2,18},{10... | collective-permute-start | bytes 1179656 | tf_op jit(solution)/shard_map/ppermute | solution.py:636
  315.1 36.2 %collective-permute-start.38 = (bf16[4,32,1536]{2,1,0:T(8,128)(2,1)S(1)}, bf16[4,32,1536]{2,1,0:T(8,128)(2,1)S(1)}, u32[]{:S(2)}, u32[]{:S(2)}) collective-permute-start(bf16[4,32,1536]{2,1,0:T(8,128)(2,1)S(1)} %get-tuple-element.145), channel_id=1, source_target_pairs={{0,17},{1,16},{2,19},{3,18},{4,21},{5,20},{6,23},{7,22},{8,25},{9,... | collective-permute-start | bytes 1179656 | tf_op jit(solution)/shard_map/ppermute | solution.py:641
  316.7 34.6 %collective-permute-start.37 = (bf16[4,32,1536]{2,1,0:T(8,128)(2,1)S(1)}, bf16[4,32,1536]{2,1,0:T(8,128)(2,1)S(1)}, u32[]{:S(2)}, u32[]{:S(2)}) collective-permute-start(bf16[4,32,1536]{2,1,0:T(8,128)(2,1)S(1)} %get-tuple-element.146), channel_id=1, source_target_pairs={{0,1},{1,0},{2,3},{3,2},{4,5},{5,4},{6,7},{7,6},{8,9},{9,8},{10,11... | collective-permute-start | bytes 1179656 | tf_op jit(solution)/shard_map/ppermute | solution.py:638
  349.6 16.8 %collective-permute-start.22 = (bf16[4,32,384]{2,1,0:T(8,128)(2,1)S(1)}, bf16[4,32,384]{2,1,0:T(8,128)(2,1)S(1)}, u32[]{:S(2)}, u32[]{:S(2)}) collective-permute-start(bf16[4,32,384]{2,1,0:T(8,128)(2,1)S(1)} %get-tuple-element.159), channel_id=1, source_target_pairs={{0,16},{8,24},{16,0},{24,8},{1,17},{9,25},{17,1},{25,9},{2,18},{10... | collective-permute-start | bytes 294920 | tf_op jit(solution)/shard_map/ppermute | solution.py:636
  366.3 22.4 %collective-permute-start.50 = (bf16[2,704,256]{2,1,0:T(8,128)(2,1)S(1)}, bf16[2,704,256]{2,1,0:T(8,128)(2,1)S(1)}, u32[]{:S(2)}, u32[]{:S(2)}) collective-permute-start(bf16[2,704,256]{2,1,0:T(8,128)(2,1)S(1)} %slice.160), channel_id=1, source_target_pairs={{0,2},{1,3},{2,0},{3,1},{4,6},{5,7},{6,4},{7,5},{8,10},{9,11},{10,... | collective-permute-start | bytes 2162696 | tf_op jit(solution)/shard_map/ppermute | solution.py:606
  366.3 16.9 %collective-permute-start.44 = (bf16[32,1536]{1,0:T(8,128)(2,1)S(1)}, bf16[32,1536]{1,0:T(8,128)(2,1)S(1)}, u32[]{:S(2)}, u32[]{:S(2)}) collective-permute-start(bf16[32,1536]{1,0:T(8,128)(2,1)S(1)} %fusion.16), channel_id=1, source_target_pairs={{0,6},{1,7},{2,4},{3,5},{4,2},{5,3},{6,0},{7,1},{8,14},{9,15},{10,... | collective-permute-start | bytes 294920 | tf_op jit(solution)/shard_map/ppermute | solution.py:638
  369.9 14.6 %collective-permute-start.42 = (bf16[32,1536]{1,0:T(8,128)(2,1)S(1)}, bf16[32,1536]{1,0:T(8,128)(2,1)S(1)}, u32[]{:S(2)}, u32[]{:S(2)}) collective-permute-start(bf16[32,1536]{1,0:T(8,128)(2,1)S(1)} %fusion.16), channel_id=1, source_target_pairs={{0,2},{1,3},{2,0},{3,1},{4,6},{5,7},{6,4},{7,5},{8,10},{9,11},{10,... | collective-permute-start | bytes 294920 | tf_op jit(solution)/shard_map/ppermute | solution.py:638
  388.7 19.7 %collective-permute-start.58 = (bf16[1,352,256]{2,1,0:T(8,128)(2,1)S(1)}, bf16[1,352,256]{2,1,0:T(8,128)(2,1)S(1)}, u32[]{:S(2)}, u32[]{:S(2)}) collective-permute-start(bf16[1,352,256]{2,1,0:T(8,128)(2,1)S(1)} %slice.248), channel_id=1, source_target_pairs={{0,4},{1,5},{2,6},{3,7},{4,0},{5,1},{6,2},{7,3},{8,12},{9,13},{10,... | collective-permute-start | bytes 540680 | tf_op jit(solution)/shard_map/ppermute | solution.py:606
  401.9 15.1 %collective-permute-start.51 = (bf16[1,704,256]{2,1,0:T(8,128)(2,1)S(1)}, bf16[1,704,256]{2,1,0:T(8,128)(2,1)S(1)}, u32[]{:S(2)}, u32[]{:S(2)}) collective-permute-start(bf16[1,704,256]{2,1,0:T(8,128)(2,1)S(1)} %slice.247), channel_id=1, source_target_pairs={{0,4},{1,5},{2,6},{3,7},{4,0},{5,1},{6,2},{7,3},{8,12},{9,13},{10,... | collective-permute-start | bytes 1081352 | tf_op jit(solution)/shard_map/ppermute | solution.py:606
  405.2 40.7 %collective-permute-start.48 = (bf16[4,4,32,1536]{3,2,1,0:T(8,128)(2,1)S(1)}, bf16[4,4,32,1536]{3,2,1,0:T(8,128)(2,1)S(1)}, u32[]{:S(2)}, u32[]{:S(2)}) collective-permute-start(bf16[4,4,32,1536]{3,2,1,0:T(8,128)(2,1)S(1)} %pad_maximum_fusion), channel_id=1, source_target_pairs={{0,8},{8,0},{16,24},{24,16},{1,9},{9,1},{17,25},{25,17},{2,10},{10... | collective-permute-start | bytes 4718600 | tf_op jit(solution)/shard_map/ppermute | solution.py:636
  (83 other events, 1422.4 us)

commit v3 on v2

--- a/solution.py
+++ b/solution.py
@@ -437,22 +437,23 @@
         lax.fori_loop(0, blocks, one, 0)
 
 
-def leave_query_kernel(sizes, ids_ref, xa_ref, dq_ref, fgain_ref, o_ref, dhb_ref, kept_ref, sent_ref, t_s):
-    xa_t = jnp.transpose(xa_ref[...])
-    depth = o_ref.shape[1]
-    t_s[:, 0:depth] = mm(jnp.transpose(o_ref[...]), dhb_ref[...])
-    t_s[:, depth : depth + QHW] = mm(xa_t, dq_ref[0:QHW, :], 1, 1)
-    t_s[:, depth + QHW : depth + QFW] = mm(xa_t, dq_ref[QHW:, :], 1, 1)
-    gain = jnp.concatenate([fgain_ref[...]] * (512 - QFW), axis=0)
-    t_s[:, depth + QFW :] = jnp.transpose(gain)
+def leave_out_kernel(sizes, ids_ref, o_ref, dhb_ref, kept_ref, sent_ref, t_s):
+    t_s[...] = mm(jnp.transpose(o_ref[...]), dhb_ref[...])
     deal(ids_ref, sizes, t_s, (kept_ref, sent_ref))
 
 
-def leave_key_kernel(
-    sizes, ids_ref, x_ref, xa_ref, gain_ref, dres_ref, dq_ref, kg_ref, cos_ref, sin_ref,
+SMALLS = 256
+RESTW = 2 * KDW + QDW + SMALLS
+GAINS = QHW + 2 * KHW
+GAIN_COPIES = (SMALLS - GAINS) // 2
+
+
+def leave_rest_kernel(
+    sizes, ids_ref, x_ref, xa_ref, gain_ref, dres_ref, dq_ref, kg_ref, fgain_ref, cos_ref, sin_ref,
     qh, qd, kh, kd, vh, vd, tg_ref, kept_ref, sent_ref, out_ref
 ):
     normed, inverse = norm_of(x_ref[...].astype(F32))
+    xa = xa_ref[...]
     g = kg_ref[...]
     dkd = turn(g[0:KDW, :], cos_ref[...], sin_ref[...], -1.0)
     d_kd = jnp.transpose(dkd).astype(BF)
@@ -462,11 +463,10 @@
     dq = dq_ref[...].astype(F32)
     d_qh = jnp.transpose(dq[0:QHW, :]).astype(BF)
     d_qd = jnp.transpose(dq[QHW:, :]).astype(BF)
-    xa_t = jnp.transpose(xa_ref[...])
+    xa_t = jnp.transpose(xa)
     out_ref[:, 0:KDW] = mm(xa_t, d_kd)
     out_ref[:, KDW : 2 * KDW] = mm(xa_t, d_vd)
-    out_ref[:, 2 * KDW : 2 * KDW + KHW] = mm(xa_t, d_kh)
-    out_ref[:, 2 * KDW + KHW : FACW] = mm(xa_t, d_vh)
+    out_ref[:, 2 * KDW : 2 * KDW + QDW] = mm(xa_t, d_qd)
     dxa = mm(d_qd, qd[...], 1, 1) + mm(d_qh, qh[...])
     dxa = dxa + mm(d_kd, kd[...], 1, 1) + mm(d_vd, vd[...], 1, 1)
     dxa = dxa + mm(d_kh, kh[...]) + mm(d_vh, vh[...])
@@ -474,104 +474,94 @@
     mean = jnp.mean(scaled * normed, axis=-1, keepdims=True)
     tg_ref[...] = (dres_ref[...] + inverse * (scaled - normed * mean)).astype(BF)
     gain_part = jnp.sum(dxa * normed, axis=0, keepdims=True)
-    gain = jnp.concatenate([gain_part] * (384 - FACW), axis=0)
-    out_ref[:, FACW:] = jnp.transpose(gain)
+    low = g[2 * KDW :, :].astype(BF)
+    small = [mm(dq_ref[0:QHW, :], xa), mm(low[0:KHW, :], xa), mm(low[KHW:, :], xa)]
+    small += [gain_part] * GAIN_COPIES + [fgain_ref[...]] * GAIN_COPIES
+    out_ref[:, 2 * KDW + QDW :] = jnp.transpose(jnp.concatenate(small, axis=0))
     deal(ids_ref, sizes, out_ref, (kept_ref, sent_ref))
 
 
-def leave_query(sizes, ids, xa, dq, fgain, o, dhb):
-    depth = xa.shape[1]
+def leave_out(sizes, ids, o, dhb):
+    depth = o.shape[1]
     blocks = math.prod(sizes) // 2
-    columns = depth + 512
     return pl.pallas_call(
-        functools.partial(leave_query_kernel, sizes),
-        out_shape=(jax.ShapeDtypeStruct((blocks, depth // (2 * blocks), columns), BF),) * 2,
-        in_specs=[SCALAR] + [WHOLE] * 5,
+        functools.partial(leave_out_kernel, sizes),
+        out_shape=(jax.ShapeDtypeStruct((blocks, depth // (2 * blocks), depth), BF),) * 2,
+        in_specs=[SCALAR] + [WHOLE] * 2,
         out_specs=[WHOLE] * 2,
-        scratch_shapes=[pltpu.VMEM((depth, columns), F32)],
+        scratch_shapes=[pltpu.VMEM((depth, depth), F32)],
         compiler_params=pltpu.CompilerParams(vmem_limit_bytes=40 << 20),
         cost_estimate=SMALL,
-        name="leave_query",
-    )(ids, xa, dq, fgain, o, dhb)
-
-
-def leave_key(sizes, ids, x, xa, gain, dres, dq, kg, cosine, sine, weights):
+        name="leave_out",
+    )(ids, o, dhb)
+
+
+def leave_rest(sizes, ids, x, xa, gain, dres, dq, kg, fgain, cosine, sine, weights):
     length, depth = x.shape
     blocks = math.prod(sizes) // 2
     return pl.pallas_call(
-        functools.partial(leave_key_kernel, sizes),
+        functools.partial(leave_rest_kernel, sizes),
         out_shape=(jax.ShapeDtypeStruct((length, depth), BF),)
-        + (jax.ShapeDtypeStruct((blocks, depth // (2 * blocks), 384), BF),) * 2,
-        in_specs=[SCALAR] + [WHOLE] * (8 + len(weights)),
+        + (jax.ShapeDtypeStruct((blocks, depth // (2 * blocks), RESTW), BF),) * 2,
+        in_specs=[SCALAR] + [WHOLE] * (9 + len(weights)),
         out_specs=[WHOLE] * 3,
-        scratch_shapes=[pltpu.VMEM((depth, 384), F32)],
+        scratch_shapes=[pltpu.VMEM((depth, RESTW), F32)],
         compiler_params=pltpu.CompilerParams(vmem_limit_bytes=40 << 20),
         cost_estimate=SMALL,
-        name="leave_key",
-    )(ids, x, xa, gain, dres, dq, kg, cosine, sine, *weights)
-
-
-def end_query_kernel(sizes, ids_ref, own_ref, got_ref, proj_ref, qh_ref, qd_ref, gain_ref, t_s):
-    depth = proj_ref.shape[1]
-
+        name="leave_rest",
+    )(ids, x, xa, gain, dres, dq, kg, fgain, cosine, sine, *weights)
+
+
+def end_out_kernel(sizes, ids_ref, own_ref, got_ref, proj_ref):
     def write(rows, v):
-        proj_ref[rows, :] = v[:, 0:depth]
-        qd_ref[rows, :] = v[:, depth + QHW : depth + QFW]
-        t_s[rows, 0:128] = v[:, depth : depth + 128]
-        t_s[rows, 128:] = v[:, depth + 384 :]
+        proj_ref[rows, :] = v
+
+    collect(ids_ref, sizes, (own_ref, got_ref), write)
+
+
+def end_out(sizes, ids, own, got):
+    depth = own.shape[0] * own.shape[1] * 2
+    return pl.pallas_call(
+        functools.partial(end_out_kernel, sizes),
+        out_shape=jax.ShapeDtypeStruct((depth, depth), F32),
+        in_specs=[SCALAR] + [WHOLE] * 2,
+        out_specs=WHOLE,
+        compiler_params=pltpu.CompilerParams(vmem_limit_bytes=40 << 20),
+        cost_estimate=SMALL,
+        name="end_out",
+    )(ids, own, got)
+
+
+def end_rest_kernel(
+    sizes, ids_ref, own_ref, got_ref, kd_ref, vd_ref, qd_ref, qh_ref, kh_ref, vh_ref, a_ref, f_ref, t_s
+):
+    def write(rows, v):
+        kd_ref[rows, :] = v[:, 0:KDW]
+        vd_ref[rows, :] = v[:, KDW : 2 * KDW]
+        qd_ref[rows, :] = v[:, 2 * KDW : 2 * KDW + QDW]
+        t_s[rows, :] = v[:, 2 * KDW + QDW :]
 
     collect(ids_ref, sizes, (own_ref, got_ref), write)
     turned = jnp.transpose(t_s[...])
     qh_ref[...] = turned[0:QHW, :]
-    gain_ref[...] = turned[128 + QFW - 384 : 128 + QFW - 384 + 1, :]
-
-
-def end_query(sizes, ids, own, got):
+    kh_ref[...] = turned[QHW : QHW + KHW, :]
+    vh_ref[...] = turned[QHW + KHW : GAINS, :]
+    a_ref[...] = turned[GAINS : GAINS + 1, :]
+    f_ref[...] = turned[GAINS + GAIN_COPIES : GAINS + GAIN_COPIES + 1, :]
+
+
+def end_rest(sizes, ids, own, got):
     depth = own.shape[0] * own.shape[1] * 2
+    shapes = [(depth, KDW), (depth, KDW), (depth, QDW), (QHW, depth), (KHW, depth), (KHW, depth)]
+    shapes += [(1, depth), (1, depth)]
     return pl.pallas_call(
-        functools.partial(end_query_kernel, sizes),
-        out_shape=(
-            jax.ShapeDtypeStruct((depth, depth), F32),
-            jax.ShapeDtypeStruct((QHW, depth), F32),
-            jax.ShapeDtypeStruct((depth, QDW), F32),
-            jax.ShapeDtypeStruct((1, depth), F32),
-        ),
+        functools.partial(end_rest_kernel, sizes),
+        out_shape=tuple(jax.ShapeDtypeStruct(v, F32) for v in shapes),
         in_specs=[SCALAR] + [WHOLE] * 2,
-        out_specs=[WHOLE] * 4,
-        scratch_shapes=[pltpu.VMEM((depth, 256), F32)],
+        out_specs=[WHOLE] * 8,
+        scratch_shapes=[pltpu.VMEM((depth, SMALLS), F32)],
         compiler_params=pltpu.CompilerParams(vmem_limit_bytes=40 << 20),
-        name="end_query",
-    )(ids, own, got)
-
-
-def end_key_kernel(sizes, ids_ref, own_ref, got_ref, kd_ref, vd_ref, kh_ref, vh_ref, gain_ref, t_s):
-    def write(rows, v):
-        kd_ref[rows, :] = v[:, 0:KDW]
-        vd_ref[rows, :] = v[:, KDW : 2 * KDW]
-        t_s[rows, :] = v[:, 2 * KDW :]
-
-    collect(ids_ref, sizes, (own_ref, got_ref), write)
-    turned = jnp.transpose(t_s[...])
-    kh_ref[...] = turned[0:KHW, :]
-    vh_ref[...] = turned[KHW : 2 * KHW, :]
-    gain_ref[...] = turned[2 * KHW : 2 * KHW + 1, :]
-
-
-def end_key(sizes, ids, own, got):
-    depth = own.shape[0] * own.shape[1] * 2
-    return pl.pallas_call(
-        functools.partial(end_key_kernel, sizes),
-        out_shape=(
-            jax.ShapeDtypeStruct((depth, KDW), F32),
-            jax.ShapeDtypeStruct((depth, KDW), F32),
-            jax.ShapeDtypeStruct((KHW, depth), F32),
-            jax.ShapeDtypeStruct((KHW, depth), F32),
-            jax.ShapeDtypeStruct((1, depth), F32),
-        ),
-        in_specs=[SCALAR] + [WHOLE] * 2,
-        out_specs=[WHOLE] * 5,
-        scratch_shapes=[pltpu.VMEM((depth, 128), F32)],
-        name="end_key",
+        name="end_rest",
     )(ids, own, got)
 
 
@@ -663,23 +653,11 @@
             out.append(number)
         return jnp.stack(out)
 
-    def sum_all(self, kept, sent, plan, shared):
-        levels = self.levels(plan)
-        v = kept.astype(F32) + self.swap_masks(sent, *levels[0][1]).astype(F32)
-        for masks in levels[1:]:
-            low = v.astype(BF)
-            total = v[0]
-            for m in range(1, len(masks)):
-                total = total + self.swap_masks(low[m], *masks[m]).astype(F32)
-            v = total
-        for masks in self.levels(shared):
-            low = v.astype(BF)
-            for m in masks[1:]:
-                v = v + self.swap_masks(low, *m).astype(F32)
-        v = v.astype(BF)
-        for masks in reversed(levels[1:]):
-            v = jnp.stack([v] + [self.swap_masks(v, *m) for m in masks[1:]])
-        return v, self.swap_masks(v, *levels[0][1])
+    def swaps(self, low, masks):
+        return [self.swap_masks(low[m], *masks[m]) for m in range(1, len(masks))]
+
+    def swaps_whole(self, low, masks):
+        return [self.swap_masks(low, *m) for m in masks[1:]]
 
 
 def ffn_kernel(parts, plan, shards, blend, scal_ref, xf_ref, dy_ref, *refs):
@@ -821,15 +799,20 @@
     )(mine, *wholes)
 
 
-def unpack_kernel(scal_ref, first_ref, second_ref, gate_ref, up_ref, down_ref):
+def unpack_kernel(scal_ref, own_ref, got_ref, gate_ref, up_ref, down_ref):
     width = gate_ref.shape[0]
-    gate_ref[...] = first_ref[0, 0:width, :].astype(F32)
-    up_ref[...] = first_ref[0, width:, :].astype(F32)
-    down_ref[...] = second_ref[0].astype(F32)
-
-
-def unpack(mine, first, second):
-    parts, width, lanes = second.shape
+    for side, ref in enumerate((own_ref, got_ref)):
+
+        @pl.when(pl.program_id(0) % 2 == side)
+        def _(ref=ref):
+            gate_ref[...] = ref[0, 0:width, :].astype(F32)
+            up_ref[...] = ref[0, width : 2 * width, :].astype(F32)
+            down_ref[...] = ref[0, 2 * width :, :].astype(F32)
+
+
+def unpack(mine, own, got):
+    half, rows, lanes = own.shape
+    width, parts = rows // 3, 2 * half
     column = pl.BlockSpec((width, lanes), lambda q, s: (0, s[0] ^ q))
     return pl.pallas_call(
         unpack_kernel,
@@ -837,15 +820,13 @@
         grid_spec=pltpu.PrefetchScalarGridSpec(
             num_scalar_prefetch=1,
             grid=(parts,),
-            in_specs=[
-                pl.BlockSpec((1, 2 * width, lanes), lambda q, s: (q, 0, 0)),
-                pl.BlockSpec((1, width, lanes), lambda q, s: (q, 0, 0)),
-            ],
+            in_specs=[pl.BlockSpec((1, rows, lanes), lambda q, s: (q // 2, 0, 0))] * 2,
             out_specs=[column] * 3,
         ),
         compiler_params=pltpu.CompilerParams(dimension_semantics=("arbitrary",)),
+        cost_estimate=SMALL,
         name="unpack",
-    )(mine, first, second)
+    )(mine, own, got)
 
 
 def spread_pieces(grid, got, tie):
@@ -861,23 +842,18 @@
 
 
 def reduce_core(grid, even, odd):
-    held = even.astype(F32) + grid.swap(odd, "c", 1).astype(F32)
-    return [held[0]] + [held[k].astype(BF) for k in range(1, grid.y)]
-
-
-def reduce_part(grid, held):
-    total = held[0]
-    for k in range(1, grid.y):
-        total = total + grid.swap(held[k], "y", k).astype(F32)
-    return grid.unstack(total.astype(BF), "z")
-
-
-def spread_part(grid, mine):
-    column = [mine] + [grid.swap(mine, "y", k) for k in range(1, grid.y)]
-    pieces = []
-    for piece in column:
-        pieces += [piece, grid.swap(piece, "c", 1)]
-    return jnp.stack(pieces)
+    got = grid.swap(odd, "c", 1)
+    goes = [
+        (even[k].astype(F32) + got[k].astype(F32)).astype(BF) for k in range(1, grid.y)
+    ]
+    return (even[0], got[0]), goes
+
+
+def total_of(*terms):
+    total = terms[0].astype(F32)
+    for term in terms[1:]:
+        total = total + term.astype(F32)
+    return total
 
 
 def contract(left, right, left_dim, right_dim):
@@ -1014,54 +990,108 @@
         spot, dys + inners, parts, grid.z, width, depth,
         [pltpu.VMEM((width, depth), F32)], "down_grads",
     )
-    first_held = reduce_core(grid, *first_parts)
+    first_kept, first_goes = reduce_core(grid, *first_parts)
     for r in range(1, grid.x):
         got = grid.swap(results[r][1], "x", r)
-        d_norm_two = d_norm_two + after(got, second_parts[0], first_held[0]).astype(F32)
+        d_norm_two = d_norm_two + after(got, second_parts[0], first_goes[0]).astype(F32)
     grad_through, ffngain_part = norm_back(d_norm_two, normed_two, inverse_two, ffngain)
     d_residual = upstream.astype(jnp.float32) + grad_through
     d_res_low = d_residual.astype(jnp.bfloat16)
     d_attended = contract(d_res_low, outproj, 1, 1).astype(jnp.bfloat16)
-    d_attended = after(d_attended, first_held[-1])
+
+    plan, z_masks = ("c", "xy", "z"), grid.levels(("z",))[0]
+    split_z = depth // (parts * grid.tensor) >= 16
+    if not split_z:
+        plan = ("c", "xy")
+    levels = grid.levels(plan)
+    core_masks, xy_masks = levels[0], levels[1]
+    sizes = tuple(len(masks) for masks in levels)
+    ids = grid.numbers(plan)
+    shape = sizes[1:] + (depth // math.prod(sizes), -1)
+
+    def along_z(v):
+        low = v.astype(BF)
+        if split_z:
+            return total_of(v[0], *grid.swaps(low, z_masks)).astype(BF)
+        return total_of(v, *grid.swaps_whole(low, z_masks)).astype(BF)
+
+    def share_z(v):
+        return jnp.stack([v] + grid.swaps_whole(v, z_masks)) if split_z else v
+
+    second_kept, second_goes = reduce_core(grid, *second_parts)
+    kept, sent = leave_out(sizes, ids, attn_out, d_res_low)
+    out_sum = total_of(
+        kept.reshape(shape), grid.swap_masks(sent.reshape(shape), *core_masks[1])
+    )
+    out_low = out_sum.astype(BF)
+    d_attended = after(d_attended, first_goes[-1], second_goes[-1], out_low)
     back = attention_backward(
         scal, qfac, facs, start, attn_out, d_attended, lse, cosine, sine
     )
-    terms, dq = back[:-1], back[-1]
+    terms, dq = list(back[:-1]), back[-1]
+
+    first_got = [grid.swap(v, "y", k + 1) for k, v in enumerate(first_goes)]
+    second_got = [grid.swap(v, "y", k + 1) for k, v in enumerate(second_goes)]
+    out_got = grid.swaps(out_low, xy_masks)
+    out_first = after(out_sum[0], dq)
+    first_kept = (after(first_kept[0], dq), first_kept[1])
+    second_kept = (after(second_kept[0], dq), second_kept[1])
+    terms[1:] = [after(v, *second_got) for v in terms[1:]]
+    out_mine = along_z(total_of(out_first, *out_got))
+    out_mine = share_z(out_mine)
     near = terms[0].astype(F32)
     for r in range(1, grid.x):
         near = near + grid.swap(terms[r], "x", r).astype(F32)
-    low = near.astype(BF)
+    ffn_sum = jnp.concatenate(
+        [total_of(*first_kept, *first_got), total_of(*second_kept, *second_got)], axis=1
+    )
+    low = after(near.astype(BF), out_mine, *first_got)
     key_grads = near[0]
-    for k, r in enumerate(grid.rels("z")):
-        if k:
-            key_grads = key_grads + grid.swap(low[k], "z", r).astype(F32)
-
-    for r in range(1, grid.x):
-        ffn_out = ffn_out + grid.swap(after(results[r][0], d_res_low), "x", r).astype(F32)
-    mixed = (residual + ffn_out).astype(jnp.bfloat16)
-
-    first_mine = reduce_part(grid, first_held)
-    second_mine = reduce_part(grid, reduce_core(grid, *second_parts))
-    gate_part, up_part, down_part = unpack(
-        spot, spread_part(grid, first_mine), spread_part(grid, second_mine)
+    for i, r in enumerate(grid.rels("z")):
+        if i:
+            key_grads = key_grads + grid.swap(low[i], "z", r).astype(F32)
+    for k, bit in enumerate(grid.bits("z")):
+        rows = ffn_sum.shape[0] // 2
+        goes = ffn_sum[rows:].astype(BF)
+        if k == 0:
+            goes = after(goes, key_grads)
+        got = grid.swap(goes, "z", bit)
+        if k == 0:
+            first_z = got
+        ffn_sum = ffn_sum[:rows] + got.astype(F32)
+    out_mine = after(out_mine, key_grads)
+    out_others = grid.swaps_whole(out_mine, xy_masks)
+    out_own = jnp.stack([out_mine] + out_others)
+    out_other = grid.swap_masks(out_own, *core_masks[1])
+
+    def flat(v):
+        return v.reshape(math.prod(sizes) // 2, -1, v.shape[-1])
+
+    out_part = end_out(sizes, ids, flat(out_own), flat(out_other))
+    tokens_grad, kept, sent = leave_rest(
+        sizes, ids, x, xa, attngain[None, :], d_residual, dq, key_grads, ffngain_part[None, :],
+        cosine, sine, weights,
     )
-
-    plan, shared = ("c", "xy", "z"), ()
-    if depth // (parts * grid.tensor) < 16:
-        plan, shared = ("c", "xy"), ("z",)
-    sizes = tuple(len(masks) for masks in grid.levels(plan))
-    ids = grid.numbers(plan)
-    shape = sizes[1:] + (depth // math.prod(sizes), -1)
-    tokens_grad, kept, sent = leave_key(
-        sizes, ids, x, xa, attngain[None, :], d_residual, dq, key_grads, cosine, sine, weights
+    rest = total_of(kept.reshape(shape), grid.swap_masks(sent.reshape(shape), *core_masks[1]))
+    low = after(rest.astype(BF), *out_others)
+    rest = total_of(rest[0], *grid.swaps(low, xy_masks))
+    rest = after(rest, first_z)
+
+    ffn_got = [grid.swap(after(results[r][0], rest), "x", r) for r in range(1, grid.x)]
+    mixed = (residual + total_of(ffn_out, *ffn_got)).astype(jnp.bfloat16)
+
+    rest = along_z(rest)
+    mine = after(ffn_sum[0].astype(BF), rest)
+    rest = after(share_z(rest), *ffn_got)
+    rest = jnp.stack([rest] + grid.swaps_whole(rest, xy_masks))
+    rest = after(rest, out_part)
+    others = grid.swap_masks(rest, *core_masks[1])
+    mine = jnp.stack([mine] + [grid.swap(mine, "y", k) for k in range(1, grid.y)])
+    gate_part, up_part, down_part = unpack(spot, mine, grid.swap(mine, "c", 1))
+
+    kd_grad, vd_grad, qd_grad, qh_grad, kh_grad, vh_grad, again_grad, fgain_grad = end_rest(
+        sizes, ids, after(flat(rest), down_part), flat(others)
     )
-    sums = grid.sum_all(kept.reshape(shape), sent.reshape(shape), plan, shared)
-    flat = [v.reshape(kept.shape) for v in sums]
-    kd_grad, vd_grad, kh_grad, vh_grad, again_grad = end_key(sizes, ids, *flat)
-    kept, sent = leave_query(sizes, ids, xa, dq, ffngain_part[None, :], attn_out, d_res_low)
-    sums = grid.sum_all(kept.reshape(shape), sent.reshape(shape), plan, shared)
-    flat = [v.reshape(kept.shape) for v in sums]
-    out_part, qh_grad, qd_grad, fgain_grad = end_query(sizes, ids, *flat)
     return (
         mixed[None],
         tokens_grad[None],

time: 461 us -> 411 us (0.89)
  starting transfers between devices: 129 us -> 104 us
  waiting for transfers between devices: 176 us -> 165 us
  local copies, waits for them, and re-layouts: 25.9 us -> 15.9 us
    ppermute x34 -> x28, starting transfers between devices: 86.2 us -> 42.1 us  [swap(): return lax.ppermute(v, axis, [(i, i ^ r * stride) for i in range(total)])]
    ppermute x8, waiting for transfers between devices: 37.8 us -> 5.02 us  [swap_masks(): return lax.ppermute(v, 'dp', [(i, i ^ dp_mask) for i in range(self.dp)])]
    ppermute x16, starting transfers between devices: 27.2 us -> 51.4 us  [swap_masks(): lax.ppermute(v, 'tensor', [(i, i ^ tensor_mask) for i in range(self.tenso...]
    ppermute x16, waiting for transfers between devices: 26 us -> 40.3 us  [swap_masks(): lax.ppermute(v, 'tensor', [(i, i ^ tensor_mask) for i in range(self.tenso...]
    unnamed x107 -> x83, local copies, waits for them, and re-layouts: 17.5 us -> 9.06 us
    ppermute x4, waiting for transfers between devices: 2.91 us -> 10.3 us  [swap_masks(): return lax.ppermute(v, ('dp', 'tensor'), pairs)]
    ppermute x8, starting transfers between devices: 9.36 us -> 3.08 us  [swap_masks(): return lax.ppermute(v, 'dp', [(i, i ^ dp_mask) for i in range(self.dp)])]
    ppermute x34 -> x28, waiting for transfers between devices: 109 us -> 109 us  [swap(): return lax.ppermute(v, axis, [(i, i ^ r * stride) for i in range(total)])]
  transfers between devices with their start and end apart: 62 -> 56, of which waited for: 25 -> 29; matrix products, arithmetic and copies ran while one was open for 7% -> 7% of each run, Pallas kernels for 14% -> 14%
where the time goes in v3:
time: 411 us; the launch traced here: 406 us
  waiting for transfers between devices  165 us (40%)
  starting transfers between devices  104 us (25%)
  Pallas kernels  94 us (23%)
  other arithmetic  21.6 us (5%)
  local copies, waits for them, and re-layouts  15.9 us (4%)
    ppermute x28, waiting for transfers between devices, swap(): return lax.ppermute(v, axis, [(i, i ^ r * stride) for i in range(total)])  109 us
    ppermute x16, starting transfers between devices, swap_masks(): lax.ppermute(v, 'tensor', [(i, i ^ tensor_mask) for i in range(self.tenso...  51.4 us
    ppermute x28, starting transfers between devices, swap(): return lax.ppermute(v, axis, [(i, i ^ r * stride) for i in range(total)])  42.1 us
    ppermute x16, waiting for transfers between devices, swap_masks(): lax.ppermute(v, 'tensor', [(i, i ^ tensor_mask) for i in range(self.tenso...  40.3 us
    pallas_call x4, Pallas kernels, ffn(): pl.pallas_call(functools.partial(ffn_kernel, parts, plan, shards, bool(be...  32.2 us
    pallas_call x1, Pallas kernels, attention_backward(): pl.pallas_call(functools.partial(backward_kernel, across), out_shape=(jax...  14.3 us
    pallas_call x2, Pallas kernels, grads(): pl.pallas_call(kernel, out_shape=(jax.ShapeDtypeStruct((parts // 2, zs, r...  14.3 us
    pallas_call x1, Pallas kernels, attention_forward(): pl.pallas_call(functools.partial(forward_kernel, len(facs)), out_shape=(j...  11.7 us
  transfers between devices with their start and end apart: 56, of which 29 were waited for; matrix products, arithmetic and copies ran while one was open for 7% of the time, Pallas kernels for 14%

profile of v3, /device:TPU:0, one launch (start us, length us, event | category | flops | bytes accessed | tf_op | source)
XLA Modules:
  0.0 406.1 jit_solution(7327724357619387503)
XLA Ops:
  11.8 4.1 %collective-permute-start = (bf16[320,256]{1,0:T(8,128)(2,1)S(1)}, bf16[320,256]{1,0:T(8,128)(2,1)S(1)}, u32[]{:S(2)}, u32[]{:S(2)}) collective-permute-start(bf16[320,256]{1,0:T(8,128)(2,1)S(1)} %get-tuple-element.87), channel_id=1, source_target_pairs={{0,4},{1,5},{2,6},{3,7},{4,0},{5,1},{6,2},{7,3},{8,12},{9,13},{10,... | collective-permute-start | bytes 491528 | tf_op jit(solution)/shard_map/ppermute | solution.py:596
  19.5 5.7 %collective-permute-done = bf16[320,256]{1,0:T(8,128)(2,1)S(1)} collective-permute-done((bf16[320,256]{1,0:T(8,128)(2,1)S(1)}, bf16[320,256]{1,0:T(8,128)(2,1)S(1)}, u32[]{:S(2)}, u32[]{:S(2)}) %collective-permute-start) | collective-permute-done | bytes 163872 | tf_op jit(solution)/shard_map/ppermute | solution.py:596
  29.2 4.9 %collective-permute-start.3 = (bf16[1,3,352,256]{3,2,1,0:T(8,128)(2,1)S(1)}, bf16[1,3,352,256]{3,2,1,0:T(8,128)(2,1)}, u32[]{:S(2)}, u32[]{:S(2)}) collective-permute-start(bf16[1,3,352,256]{3,2,1,0:T(8,128)(2,1)S(1)} %maximum_bitcast_fusion), channel_id=1, source_target_pairs={{0,4},{1,5},{2,6},{3,7},{4,0},{5,1},{6,2},{7,3},{8,12},{9,13},{10,... | collective-permute-start | bytes 1622024 | tf_op jit(solution)/shard_map/ppermute | solution.py:596
  35.0 23.3 %collective-permute-done.3.refs_3_ = bf16[1,3,352,256]{3,2,1,0:T(8,128)(2,1)} collective-permute-done((bf16[1,3,352,256]{3,2,1,0:T(8,128)(2,1)S(1)}, bf16[1,3,352,256]{3,2,1,0:T(8,128)(2,1)}, u32[]{:S(2)}, u32[]{:S(2)}) %collective-permute-start.3) | collective-permute-done | bytes 540704 | tf_op jit(solution)/shard_map/ppermute | solution.py:596
  65.5 22.7 %collective-permute-done.4.dy_ref.refs_1_ = bf16[256,1024]{1,0:T(8,128)(2,1)} collective-permute-done((bf16[256,1024]{1,0:T(8,128)(2,1)}, bf16[256,1024]{1,0:T(8,128)(2,1)}, u32[]{:S(2)}, u32[]{:S(2)}) %collective-permute-start.4) | collective-permute-done | bytes 524320 | tf_op jit(solution)/shard_map/ppermute | solution.py:596
  88.2 11.7 %attention_forward.1 = (bf16[256,1024]{1,0:T(8,128)(2,1)}, f32[16,256,128]{2,1,0:T(8,128)}) custom-call(s32[2]{0:T(128)} %pad_add_fusion.scal_ref, bf16[480,256]{1,0:T(8,128)(2,1)} %copy-done.11, bf16[4,320,256]{2,1,0:T(8,128)(2,1)} %pad_maximum_fusion.4.refs_0_, bf16[4,320,256]{2,1,0:T(8,128)(2,1)} %collective-permute-done.5.refs_1_, ...), custom_call_target="tpu_custom_call" | custom-call | flops 1000 | bytes 1000 | tf_op jit(solution)/shard_map/attention_forward/pallas_call | solution.py:158
  102.5 24.5 %collective-permute-done.8.refs_2_ = bf16[2,3,352,256]{3,2,1,0:T(8,128)(2,1)} collective-permute-done((bf16[2,3,352,256]{3,2,1,0:T(8,128)(2,1)}, bf16[2,3,352,256]{3,2,1,0:T(8,128)(2,1)}, u32[]{:S(2)}, u32[]{:S(2)}) %collective-permute-start.8) | collective-permute-done | bytes 1081376 | tf_op jit(solution)/shard_map/ppermute | solution.py:596
  128.9 7.7 %collective-permute-done.11.refs_5_ = bf16[1,3,352,256]{3,2,1,0:T(8,128)(2,1)} collective-permute-done((bf16[1,3,352,256]{3,2,1,0:T(8,128)(2,1)}, bf16[1,3,352,256]{3,2,1,0:T(8,128)(2,1)}, u32[]{:S(2)}, u32[]{:S(2)}) %collective-permute-start.11) | collective-permute-done | bytes 540704 | tf_op jit(solution)/shard_map/ppermute | solution.py:596
  137.6 5.9 %collective-permute-start.13 = (bf16[256,1024]{1,0:T(8,128)(2,1)}, bf16[256,1024]{1,0:T(8,128)(2,1)}, u32[]{:S(2)}, u32[]{:S(2)}) collective-permute-start(bf16[256,1024]{1,0:T(8,128)(2,1)} %multiply_convert_fusion.xf_ref.refs_0_), channel_id=1, source_target_pairs={{0,1},{1,0},{2,3},{3,2},{4,5},{5,4},{6,7},{7,6},{8,9},{9,8},{10,11... | collective-permute-start | bytes 1572872 | tf_op jit(solution)/shard_map/ppermute | solution.py:596
  144.2 7.9 %ffn_early.2 = (f32[256,1024]{1,0:T(8,128)}, f32[256,1024]{1,0:T(8,128)}, bf16[1,256,704]{2,1,0:T(8,128)(2,1)}, bf16[1,256,704]{2,1,0:T(8,128)(2,1)}, bf16[1,256,704]{2,1,0:T(8,128)(2,1)}) custom-call(s32[2]{0:T(128)} %pad_add_fusion.1.scal_ref, bf16[256,1024]{1,0:T(8,128)(2,1)} %multiply_convert_fusion.xf_ref.refs_0_, ...), custom_call_target="tpu_custom_call" | custom-call | flops 1000 | bytes 1000 | tf_op jit(solution)/shard_map/ffn_early/pallas_call | solution.py:722
  152.0 4.4 %collective-permute-done.13.xf_ref.refs_1_ = bf16[256,1024]{1,0:T(8,128)(2,1)} collective-permute-done((bf16[256,1024]{1,0:T(8,128)(2,1)}, bf16[256,1024]{1,0:T(8,128)(2,1)}, u32[]{:S(2)}, u32[]{:S(2)}) %collective-permute-start.13) | collective-permute-done | bytes 524320 | tf_op jit(solution)/shard_map/ppermute | solution.py:596
  156.5 7.9 %ffn_early.3 = (f32[256,1024]{1,0:T(8,128)}, f32[256,1024]{1,0:T(8,128)}, bf16[1,256,704]{2,1,0:T(8,128)(2,1)}, bf16[1,256,704]{2,1,0:T(8,128)(2,1)}, bf16[1,256,704]{2,1,0:T(8,128)(2,1)}) custom-call(s32[2]{0:T(128)} %pad_add_fusion.1.scal_ref, bf16[256,1024]{1,0:T(8,128)(2,1)} %collective-permute-done.13.xf_ref.refs_1_, ...), custom_call_target="tpu_custom_call" | custom-call | flops 1000 | bytes 1000 | tf_op jit(solution)/shard_map/ffn_early/pallas_call | solution.py:722
  164.4 8.4 %ffn_late.2 = (f32[256,1024]{1,0:T(8,128)}, f32[256,1024]{1,0:T(8,128)}, bf16[1,256,704]{2,1,0:T(8,128)(2,1)}, bf16[1,256,704]{2,1,0:T(8,128)(2,1)}, bf16[1,256,704]{2,1,0:T(8,128)(2,1)}) custom-call(s32[2]{0:T(128)} %pad_add_fusion.1.scal_ref, bf16[256,1024]{1,0:T(8,128)(2,1)} %multiply_convert_fusion.xf_ref.refs_0_, ...), custom_call_target="tpu_custom_call" | custom-call | flops 1000 | bytes 1000 | tf_op jit(solution)/shard_map/ffn_late/pallas_call | solution.py:722
  172.8 8.1 %ffn_late.3 = (bf16[256,1024]{1,0:T(8,128)(2,1)}, bf16[256,1024]{1,0:T(8,128)(2,1)}, bf16[1,256,704]{2,1,0:T(8,128)(2,1)}, bf16[1,256,704]{2,1,0:T(8,128)(2,1)}, bf16[1,256,704]{2,1,0:T(8,128)(2,1)}) custom-call(s32[2]{0:T(128)} %pad_add_fusion.1.scal_ref, bf16[256,1024]{1,0:T(8,128)(2,1)} %collective-permute-done.13.xf_ref.refs_1_, ...), custom_call_target="tpu_custom_call" | custom-call | flops 1000 | bytes 1000 | tf_op jit(solution)/shard_map/ffn_late/pallas_call | solution.py:722
  180.9 9.0 %gate_up_grads.1 = (bf16[2,4,704,256]{3,2,1,0:T(8,128)(2,1)}, bf16[2,4,704,256]{3,2,1,0:T(8,128)(2,1)}) custom-call(s32[2]{0:T(128)} %pad_add_fusion.1.scal_ref, bf16[256,1024]{1,0:T(8,128)(2,1)} %multiply_convert_fusion.xf_ref.refs_0_, bf16[256,1024]{1,0:T(8,128)(2,1)} %collective-permute-done.13.xf_ref.refs_1_, ...), custom_call_target="tpu_custom_call" | custom-call | flops 1000 | bytes 1000 | tf_op jit(solution)/shard_map/gate_up_grads/pallas_call | solution.py:790
  191.6 5.3 %down_grads.1 = (bf16[2,4,352,256]{3,2,1,0:T(8,128)(2,1)}, bf16[2,4,352,256]{3,2,1,0:T(8,128)(2,1)}) custom-call(s32[2]{0:T(128)} %pad_add_fusion.1.scal_ref, bf16[256,1024]{1,0:T(8,128)(2,1)} %bitcast.19.dy_ref.refs_0_, bf16[256,1024]{1,0:T(8,128)(2,1)} %collective-permute-done.4.dy_ref.refs_1_, bf16[1,256,704]{2,1,0:T(8,128)(2,1)} %get-tuple-element.106.refs_2_, ...), custom_call_target="tpu_custom_call" | custom-call | flops 1000 | bytes 1000 | tf_op jit(solution)/shard_map/down_grads/pallas_call | solution.py:790
  200.5 3.9 collective-permute-done.14
  221.3 14.3 %attention_backward.1 = (bf16[4,320,256]{2,1,0:T(8,128)(2,1)}, bf16[4,320,256]{2,1,0:T(8,128)(2,1)}, bf16[480,256]{1,0:T(8,128)(2,1)}) custom-call(s32[2]{0:T(128)} %pad_add_fusion.scal_ref, bf16[480,256]{1,0:T(8,128)(2,1)} %copy-done.11, bf16[4,320,256]{2,1,0:T(8,128)(2,1)} %pad_maximum_fusion.4.refs_0_, ...), custom_call_target="tpu_custom_call" | custom-call | flops 1000 | bytes 1000 | tf_op jit(solution)/shard_map/attention_backward/pallas_call | solution.py:304
  236.9 7.6 %collective-permute-start.19 = (bf16[4,320,256]{2,1,0:T(8,128)(2,1)}, bf16[4,320,256]{2,1,0:T(8,128)(2,1)S(1)}, u32[]{:S(2)}, u32[]{:S(2)}) collective-permute-start(bf16[4,320,256]{2,1,0:T(8,128)(2,1)} %get-tuple-element.130), channel_id=1, source_target_pairs={{0,1},{1,0},{2,3},{3,2},{4,5},{5,4},{6,7},{7,6},{8,9},{9,8},{10,11... | collective-permute-start | bytes 1966088 | tf_op jit(solution)/shard_map/ppermute | solution.py:596
  245.7 13.2 %collective-permute-start.23 = (bf16[32,1024]{1,0:T(8,128)(2,1)S(1)}, bf16[32,1024]{1,0:T(8,128)(2,1)S(1)}, u32[]{:S(2)}, u32[]{:S(2)}) collective-permute-start(bf16[32,1024]{1,0:T(8,128)(2,1)S(1)} %get-tuple-element.179), channel_id=1, source_target_pairs={{0,2},{1,3},{2,0},{3,1},{4,6},{5,7},{6,4},{7,5},{8,10},{9,11},{10,... | collective-permute-start | bytes 196616 | tf_op jit(solution)/shard_map/ppermute | solution.py:628
  258.8 18.7 %collective-permute-start.24 = (bf16[32,1024]{1,0:T(8,128)(2,1)S(1)}, bf16[32,1024]{1,0:T(8,128)(2,1)S(1)}, u32[]{:S(2)}, u32[]{:S(2)}) collective-permute-start(bf16[32,1024]{1,0:T(8,128)(2,1)S(1)} %get-tuple-element.181), channel_id=1, source_target_pairs={{0,4},{1,5},{2,6},{3,7},{4,0},{5,1},{6,2},{7,3},{8,12},{9,13},{10,... | collective-permute-start | bytes 196616 | tf_op jit(solution)/shard_map/ppermute | solution.py:628
  279.0 3.5 collective-permute-done.24
  305.3 4.6 %leave_rest.1 = (bf16[256,1024]{1,0:T(8,128)(2,1)}, bf16[16,32,896]{2,1,0:T(8,128)(2,1)S(1)}, bf16[16,32,896]{2,1,0:T(8,128)(2,1)S(1)}) custom-call(s32[3]{0:T(128)S(1)} %pad_add_fusion.2.ids_ref, bf16[256,1024]{1,0:T(8,128)(2,1)S(1)} %bitcast.167, bf16[256,1024]{1,0:T(8,128)(2,1)S(1)} %get-tuple-element.103.xa_ref, f32[1,1024]{1,0:T(1,128)S(1)} %bitcast.181, ...), custom_call_target="tpu_custom_call" | custom-call | flops 1000 | bytes 1000 | tf_op jit(solution)/shard_map/leave_rest/pallas_call | solution.py:502
  316.7 4.6 %collective-permute-done.34 = bf16[4,32,1024]{2,1,0:T(8,128)(2,1)S(1)} collective-permute-done((bf16[4,32,1024]{2,1,0:T(8,128)(2,1)S(1)}, bf16[4,32,1024]{2,1,0:T(8,128)(2,1)S(1)}, u32[]{:S(2)}, u32[]{:S(2)}) %collective-permute-start.34) | collective-permute-done | bytes 262176 | tf_op jit(solution)/shard_map/ppermute | solution.py:626
  322.1 6.1 %collective-permute-done.36 = bf16[4,32,1024]{2,1,0:T(8,128)(2,1)S(1)} collective-permute-done((bf16[4,32,1024]{2,1,0:T(8,128)(2,1)S(1)}, bf16[4,32,1024]{2,1,0:T(8,128)(2,1)S(1)}, u32[]{:S(2)}, u32[]{:S(2)}) %collective-permute-start.36) | collective-permute-done | bytes 262176 | tf_op jit(solution)/shard_map/ppermute | solution.py:631
  331.8 6.4 %collective-permute-done.40 = bf16[2,1056,256]{2,1,0:T(8,128)(2,1)S(1)} collective-permute-done((bf16[2,1056,256]{2,1,0:T(8,128)(2,1)S(1)}, bf16[2,1056,256]{2,1,0:T(8,128)(2,1)S(1)}, u32[]{:S(2)}, u32[]{:S(2)}) %collective-permute-start.40) | collective-permute-done | bytes 1081376 | tf_op jit(solution)/shard_map/ppermute | solution.py:596
  345.9 8.2 %collective-permute-done.42 = bf16[32,896]{1,0:T(8,128)(2,1)S(1)} collective-permute-done((bf16[32,896]{1,0:T(8,128)(2,1)S(1)}, bf16[32,896]{1,0:T(8,128)(2,1)S(1)}, u32[]{:S(2)}, u32[]{:S(2)}) %collective-permute-start.42) | collective-permute-done | bytes 57376 | tf_op jit(solution)/shard_map/ppermute | solution.py:628
  354.1 15.1 %collective-permute-done.43 = bf16[32,896]{1,0:T(8,128)(2,1)S(1)} collective-permute-done((bf16[32,896]{1,0:T(8,128)(2,1)S(1)}, bf16[32,896]{1,0:T(8,128)(2,1)S(1)}, u32[]{:S(2)}, u32[]{:S(2)}) %collective-permute-start.43) | collective-permute-done | bytes 57376 | tf_op jit(solution)/shard_map/ppermute | solution.py:628
  386.7 3.5 end_out.1
  391.9 3.4 collective-permute-done.50
  396.7 5.5 %unpack.1 = (f32[352,1024]{1,0:T(8,128)}, f32[352,1024]{1,0:T(8,128)}, f32[352,1024]{1,0:T(8,128)}) custom-call(s32[2]{0:T(128)} %pad_add_fusion.1.scal_ref, bf16[2,1056,256]{2,1,0:T(8,128)(2,1)} %copy-done.28, bf16[2,1056,256]{2,1,0:T(8,128)(2,1)} %collective-permute-done.54.got_ref), custom_call_target="tpu_custom_call" | custom-call | flops 1000 | bytes 1000 | tf_op jit(solution)/shard_map/unpack/pallas_call | solution.py:817
  402.2 3.8 end_rest.1
  (229 shorter events, 120.0 us)
Async XLA Ops:
  11.8 13.5 %collective-permute-start = (bf16[320,256]{1,0:T(8,128)(2,1)S(1)}, bf16[320,256]{1,0:T(8,128)(2,1)S(1)}, u32[]{:S(2)}, u32[]{:S(2)}) collective-permute-start(bf16[320,256]{1,0:T(8,128)(2,1)S(1)} %get-tuple-element.87), channel_id=1, source_target_pairs={{0,4},{1,5},{2,6},{3,7},{4,0},{5,1},{6,2},{7,3},{8,12},{9,13},{10,... | collective-permute-start | bytes 491528 | tf_op jit(solution)/shard_map/ppermute | solution.py:596
  29.2 29.1 %collective-permute-start.3 = (bf16[1,3,352,256]{3,2,1,0:T(8,128)(2,1)S(1)}, bf16[1,3,352,256]{3,2,1,0:T(8,128)(2,1)}, u32[]{:S(2)}, u32[]{:S(2)}) collective-permute-start(bf16[1,3,352,256]{3,2,1,0:T(8,128)(2,1)S(1)} %maximum_bitcast_fusion), channel_id=1, source_target_pairs={{0,4},{1,5},{2,6},{3,7},{4,0},{5,1},{6,2},{7,3},{8,12},{9,13},{10,... | collective-permute-start | bytes 1622024 | tf_op jit(solution)/shard_map/ppermute | solution.py:596
  60.2 39.7 %collective-permute-start.6 = (bf16[2,3,352,256]{3,2,1,0:T(8,128)(2,1)}, bf16[2,3,352,256]{3,2,1,0:T(8,128)(2,1)}, u32[]{:S(2)}, u32[]{:S(2)}) collective-permute-start(bf16[2,3,352,256]{3,2,1,0:T(8,128)(2,1)} %constant_dynamic-update-slice_fusion), channel_id=1, source_target_pairs={{0,2},{1,3},{2,0},{3,1},{4,6},{5,7},{6,4},{7,5},{8,10},{9,11},{10,... | collective-permute-start | bytes 3244040 | tf_op jit(solution)/shard_map/ppermute | solution.py:596
  60.2 28.0 %collective-permute-start.5 = (bf16[4,320,256]{2,1,0:T(8,128)(2,1)}, bf16[4,320,256]{2,1,0:T(8,128)(2,1)}, u32[]{:S(2)}, u32[]{:S(2)}) collective-permute-start(bf16[4,320,256]{2,1,0:T(8,128)(2,1)} %pad_maximum_fusion.4.refs_0_), channel_id=1, source_target_pairs={{0,1},{1,0},{2,3},{3,2},{4,5},{5,4},{6,7},{7,6},{8,9},{9,8},{10,11... | collective-permute-start | bytes 1966088 | tf_op jit(solution)/shard_map/ppermute | solution.py:596
  61.7 26.5 %collective-permute-start.4 = (bf16[256,1024]{1,0:T(8,128)(2,1)}, bf16[256,1024]{1,0:T(8,128)(2,1)}, u32[]{:S(2)}, u32[]{:S(2)}) collective-permute-start(bf16[256,1024]{1,0:T(8,128)(2,1)} %bitcast.19.dy_ref.refs_0_), channel_id=1, source_target_pairs={{0,1},{1,0},{2,3},{3,2},{4,5},{5,4},{6,7},{7,6},{8,9},{9,8},{10,11... | collective-permute-start | bytes 1572872 | tf_op jit(solution)/shard_map/ppermute | solution.py:596
  99.9 27.1 %collective-permute-start.8 = (bf16[2,3,352,256]{3,2,1,0:T(8,128)(2,1)}, bf16[2,3,352,256]{3,2,1,0:T(8,128)(2,1)}, u32[]{:S(2)}, u32[]{:S(2)}) collective-permute-start(bf16[2,3,352,256]{3,2,1,0:T(8,128)(2,1)} %collective-permute-done.6.refs_0_), channel_id=1, source_target_pairs={{0,16},{8,24},{16,0},{24,8},{1,17},{9,25},{17,1},{25,9},{2,18},{10... | collective-permute-start | bytes 3244040 | tf_op jit(solution)/shard_map/ppermute | solution.py:596
  101.5 35.1 %collective-permute-start.11 = (bf16[1,3,352,256]{3,2,1,0:T(8,128)(2,1)}, bf16[1,3,352,256]{3,2,1,0:T(8,128)(2,1)}, u32[]{:S(2)}, u32[]{:S(2)}) collective-permute-start(bf16[1,3,352,256]{3,2,1,0:T(8,128)(2,1)} %collective-permute-done.3.refs_3_), channel_id=1, source_target_pairs={{0,16},{8,24},{16,0},{24,8},{1,17},{9,25},{17,1},{25,9},{2,18},{10... | collective-permute-start | bytes 1622024 | tf_op jit(solution)/shard_map/ppermute | solution.py:596
  102.0 42.1 %collective-permute-start.10 = (bf16[1,3,352,256]{3,2,1,0:T(8,128)(2,1)}, bf16[1,3,352,256]{3,2,1,0:T(8,128)(2,1)}, u32[]{:S(2)}, u32[]{:S(2)}) collective-permute-start(bf16[1,3,352,256]{3,2,1,0:T(8,128)(2,1)} %collective-permute-done.3.refs_3_), channel_id=1, source_target_pairs={{0,8},{8,0},{16,24},{24,16},{1,9},{9,1},{17,25},{25,17},{2,10},{10... | collective-permute-start | bytes 1622024 | tf_op jit(solution)/shard_map/ppermute | solution.py:596
  102.0 62.3 %collective-permute-start.7 = (bf16[2,3,352,256]{3,2,1,0:T(8,128)(2,1)}, bf16[2,3,352,256]{3,2,1,0:T(8,128)(2,1)}, u32[]{:S(2)}, u32[]{:S(2)}) collective-permute-start(bf16[2,3,352,256]{3,2,1,0:T(8,128)(2,1)} %collective-permute-done.6.refs_0_), channel_id=1, source_target_pairs={{0,8},{8,0},{16,24},{24,16},{1,9},{9,1},{17,25},{25,17},{2,10},{10... | collective-permute-start | bytes 3244040 | tf_op jit(solution)/shard_map/ppermute | solution.py:596
  127.1 37.3 %collective-permute-start.9 = (bf16[2,3,352,256]{3,2,1,0:T(8,128)(2,1)}, bf16[2,3,352,256]{3,2,1,0:T(8,128)(2,1)}, u32[]{:S(2)}, u32[]{:S(2)}) collective-permute-start(bf16[2,3,352,256]{3,2,1,0:T(8,128)(2,1)} %collective-permute-done.8.refs_2_), channel_id=1, source_target_pairs={{0,8},{8,0},{16,24},{24,16},{1,9},{9,1},{17,25},{25,17},{2,10},{10... | collective-permute-start | bytes 3244040 | tf_op jit(solution)/shard_map/ppermute | solution.py:596
  137.6 18.8 %collective-permute-start.13 = (bf16[256,1024]{1,0:T(8,128)(2,1)}, bf16[256,1024]{1,0:T(8,128)(2,1)}, u32[]{:S(2)}, u32[]{:S(2)}) collective-permute-start(bf16[256,1024]{1,0:T(8,128)(2,1)} %multiply_convert_fusion.xf_ref.refs_0_), channel_id=1, source_target_pairs={{0,1},{1,0},{2,3},{3,2},{4,5},{5,4},{6,7},{7,6},{8,9},{9,8},{10,11... | collective-permute-start | bytes 1572872 | tf_op jit(solution)/shard_map/ppermute | solution.py:596
  189.8 14.7 %collective-permute-start.14 = (bf16[256,1024]{1,0:T(8,128)(2,1)}, bf16[256,1024]{1,0:T(8,128)(2,1)}, u32[]{:S(2)}, u32[]{:S(2)}) collective-permute-start(bf16[256,1024]{1,0:T(8,128)(2,1)} %get-tuple-element.105), channel_id=1, source_target_pairs={{0,1},{1,0},{2,3},{3,2},{4,5},{5,4},{6,7},{7,6},{8,9},{9,8},{10,11... | collective-permute-start | bytes 1572872 | tf_op jit(solution)/shard_map/ppermute | solution.py:596
  196.9 13.2 %collective-permute-start.16 = (bf16[2,4,352,256]{3,2,1,0:T(8,128)(2,1)}, bf16[2,4,352,256]{3,2,1,0:T(8,128)(2,1)S(1)}, u32[]{:S(2)}, u32[]{:S(2)}) collective-permute-start(bf16[2,4,352,256]{3,2,1,0:T(8,128)(2,1)} %get-tuple-element.122), channel_id=1, source_target_pairs={{0,8},{8,0},{16,24},{24,16},{1,9},{9,1},{17,25},{25,17},{2,10},{10... | collective-permute-start | bytes 4325384 | tf_op jit(solution)/shard_map/ppermute | solution.py:596
  211.3 25.5 %collective-permute-start.18 = (bf16[4,352,256]{2,1,0:T(8,128)(2,1)}, bf16[4,352,256]{2,1,0:T(8,128)(2,1)}, u32[]{:S(2)}, u32[]{:S(2)}) collective-permute-start(bf16[4,352,256]{2,1,0:T(8,128)(2,1)} %fusion.7), channel_id=1, source_target_pairs={{0,16},{8,24},{16,0},{24,8},{1,17},{9,25},{17,1},{25,9},{2,18},{10... | collective-permute-start | bytes 2162696 | tf_op jit(solution)/shard_map/ppermute | solution.py:596
  214.8 29.7 %collective-permute-start.20 = (bf16[4,32,1024]{2,1,0:T(8,128)(2,1)S(1)}, bf16[4,32,1024]{2,1,0:T(8,128)(2,1)S(1)}, u32[]{:S(2)}, u32[]{:S(2)}) collective-permute-start(bf16[4,32,1024]{2,1,0:T(8,128)(2,1)S(1)} %get-tuple-element.170), channel_id=1, source_target_pairs={{0,16},{8,24},{16,0},{24,8},{1,17},{9,25},{17,1},{25,9},{2,18},{10... | collective-permute-start | bytes 786440 | tf_op jit(solution)/shard_map/ppermute | solution.py:626
  216.3 28.2 %collective-permute-start.21 = (bf16[4,32,1024]{2,1,0:T(8,128)(2,1)S(1)}, bf16[4,32,1024]{2,1,0:T(8,128)(2,1)S(1)}, u32[]{:S(2)}, u32[]{:S(2)}) collective-permute-start(bf16[4,32,1024]{2,1,0:T(8,128)(2,1)S(1)} %get-tuple-element.172), channel_id=1, source_target_pairs={{0,1},{1,0},{2,3},{3,2},{4,5},{5,4},{6,7},{7,6},{8,9},{9,8},{10,11... | collective-permute-start | bytes 786440 | tf_op jit(solution)/shard_map/ppermute | solution.py:628
  218.0 26.5 %collective-permute-start.22 = (bf16[4,32,1024]{2,1,0:T(8,128)(2,1)S(1)}, bf16[4,32,1024]{2,1,0:T(8,128)(2,1)}, u32[]{:S(2)}, u32[]{:S(2)}) collective-permute-start(bf16[4,32,1024]{2,1,0:T(8,128)(2,1)S(1)} %get-tuple-element.171), channel_id=1, source_target_pairs={{0,17},{1,16},{2,19},{3,18},{4,21},{5,20},{6,23},{7,22},{8,25},{9,... | collective-permute-start | bytes 786440 | tf_op jit(solution)/shard_map/ppermute | solution.py:631
  219.9 74.0 %collective-permute-start.29 = (bf16[4,704,256]{2,1,0:T(8,128)(2,1)}, bf16[4,704,256]{2,1,0:T(8,128)(2,1)S(1)}, u32[]{:S(2)}, u32[]{:S(2)}) collective-permute-start(bf16[4,704,256]{2,1,0:T(8,128)(2,1)} %fusion.4), channel_id=1, source_target_pairs={{0,16},{8,24},{16,0},{24,8},{1,17},{9,25},{17,1},{25,9},{2,18},{10... | collective-permute-start | bytes 4325384 | tf_op jit(solution)/shard_map/ppermute | solution.py:596
  236.9 56.9 %collective-permute-start.19 = (bf16[4,320,256]{2,1,0:T(8,128)(2,1)}, bf16[4,320,256]{2,1,0:T(8,128)(2,1)S(1)}, u32[]{:S(2)}, u32[]{:S(2)}) collective-permute-start(bf16[4,320,256]{2,1,0:T(8,128)(2,1)} %get-tuple-element.130), channel_id=1, source_target_pairs={{0,1},{1,0},{2,3},{3,2},{4,5},{5,4},{6,7},{7,6},{8,9},{9,8},{10,11... | collective-permute-start | bytes 1966088 | tf_op jit(solution)/shard_map/ppermute | solution.py:596
  245.7 33.3 %collective-permute-start.23 = (bf16[32,1024]{1,0:T(8,128)(2,1)S(1)}, bf16[32,1024]{1,0:T(8,128)(2,1)S(1)}, u32[]{:S(2)}, u32[]{:S(2)}) collective-permute-start(bf16[32,1024]{1,0:T(8,128)(2,1)S(1)} %get-tuple-element.179), channel_id=1, source_target_pairs={{0,2},{1,3},{2,0},{3,1},{4,6},{5,7},{6,4},{7,5},{8,10},{9,11},{10,... | collective-permute-start | bytes 196616 | tf_op jit(solution)/shard_map/ppermute | solution.py:628
  258.8 23.6 %collective-permute-start.24 = (bf16[32,1024]{1,0:T(8,128)(2,1)S(1)}, bf16[32,1024]{1,0:T(8,128)(2,1)S(1)}, u32[]{:S(2)}, u32[]{:S(2)}) collective-permute-start(bf16[32,1024]{1,0:T(8,128)(2,1)S(1)} %get-tuple-element.181), channel_id=1, source_target_pairs={{0,4},{1,5},{2,6},{3,7},{4,0},{5,1},{6,2},{7,3},{8,12},{9,13},{10,... | collective-permute-start | bytes 196616 | tf_op jit(solution)/shard_map/ppermute | solution.py:628
  311.9 26.3 %collective-permute-start.40 = (bf16[2,1056,256]{2,1,0:T(8,128)(2,1)S(1)}, bf16[2,1056,256]{2,1,0:T(8,128)(2,1)S(1)}, u32[]{:S(2)}, u32[]{:S(2)}) collective-permute-start(bf16[2,1056,256]{2,1,0:T(8,128)(2,1)S(1)} %fusion.2), channel_id=1, source_target_pairs={{0,2},{1,3},{2,0},{3,1},{4,6},{5,7},{6,4},{7,5},{8,10},{9,11},{10,... | collective-permute-start | bytes 3244040 | tf_op jit(solution)/shard_map/ppermute | solution.py:596
  313.5 14.7 %collective-permute-start.36 = (bf16[4,32,1024]{2,1,0:T(8,128)(2,1)S(1)}, bf16[4,32,1024]{2,1,0:T(8,128)(2,1)S(1)}, u32[]{:S(2)}, u32[]{:S(2)}) collective-permute-start(bf16[4,32,1024]{2,1,0:T(8,128)(2,1)S(1)} %pad_maximum_fusion.5), channel_id=1, source_target_pairs={{0,17},{1,16},{2,19},{3,18},{4,21},{5,20},{6,23},{7,22},{8,25},{9,... | collective-permute-start | bytes 786440 | tf_op jit(solution)/shard_map/ppermute | solution.py:631
  328.3 11.9 %collective-permute-start.37 = (bf16[4,32,896]{2,1,0:T(8,128)(2,1)S(1)}, bf16[4,32,896]{2,1,0:T(8,128)(2,1)S(1)}, u32[]{:S(2)}, u32[]{:S(2)}) collective-permute-start(bf16[4,32,896]{2,1,0:T(8,128)(2,1)S(1)} %get-tuple-element.173), channel_id=1, source_target_pairs={{0,16},{8,24},{16,0},{24,8},{1,17},{9,25},{17,1},{25,9},{2,18},{10... | collective-permute-start | bytes 688136 | tf_op jit(solution)/shard_map/ppermute | solution.py:626
  329.1 11.9 %collective-permute-start.39 = (bf16[4,32,896]{2,1,0:T(8,128)(2,1)S(1)}, bf16[4,32,896]{2,1,0:T(8,128)(2,1)S(1)}, u32[]{:S(2)}, u32[]{:S(2)}) collective-permute-start(bf16[4,32,896]{2,1,0:T(8,128)(2,1)S(1)} %get-tuple-element.174), channel_id=1, source_target_pairs={{0,17},{1,16},{2,19},{3,18},{4,21},{5,20},{6,23},{7,22},{8,25},{9,... | collective-permute-start | bytes 688136 | tf_op jit(solution)/shard_map/ppermute | solution.py:631
  338.5 30.6 %collective-permute-start.52 = (bf16[1,1056,256]{2,1,0:T(8,128)(2,1)S(1)}, bf16[1,1056,256]{2,1,0:T(8,128)(2,1)S(1)}, u32[]{:S(2)}, u32[]{:S(2)}) collective-permute-start(bf16[1,1056,256]{2,1,0:T(8,128)(2,1)S(1)} %slice.222), channel_id=1, source_target_pairs={{0,4},{1,5},{2,6},{3,7},{4,0},{5,1},{6,2},{7,3},{8,12},{9,13},{10,... | collective-permute-start | bytes 1622024 | tf_op jit(solution)/shard_map/ppermute | solution.py:596
  341.2 12.9 %collective-permute-start.42 = (bf16[32,896]{1,0:T(8,128)(2,1)S(1)}, bf16[32,896]{1,0:T(8,128)(2,1)S(1)}, u32[]{:S(2)}, u32[]{:S(2)}) collective-permute-start(bf16[32,896]{1,0:T(8,128)(2,1)S(1)} %get-tuple-element.182), channel_id=1, source_target_pairs={{0,2},{1,3},{2,0},{3,1},{4,6},{5,7},{6,4},{7,5},{8,10},{9,11},{10,... | collective-permute-start | bytes 172040 | tf_op jit(solution)/shard_map/ppermute | solution.py:628
  342.3 26.8 %collective-permute-start.43 = (bf16[32,896]{1,0:T(8,128)(2,1)S(1)}, bf16[32,896]{1,0:T(8,128)(2,1)S(1)}, u32[]{:S(2)}, u32[]{:S(2)}) collective-permute-start(bf16[32,896]{1,0:T(8,128)(2,1)S(1)} %get-tuple-element.184), channel_id=1, source_target_pairs={{0,4},{1,5},{2,6},{3,7},{4,0},{5,1},{6,2},{7,3},{8,12},{9,13},{10,... | collective-permute-start | bytes 172040 | tf_op jit(solution)/shard_map/ppermute | solution.py:628
  343.9 25.2 %collective-permute-start.44 = (bf16[32,896]{1,0:T(8,128)(2,1)S(1)}, bf16[32,896]{1,0:T(8,128)(2,1)S(1)}, u32[]{:S(2)}, u32[]{:S(2)}) collective-permute-start(bf16[32,896]{1,0:T(8,128)(2,1)S(1)} %get-tuple-element.183), channel_id=1, source_target_pairs={{0,6},{1,7},{2,4},{3,5},{4,2},{5,3},{6,0},{7,1},{8,14},{9,15},{10,... | collective-permute-start | bytes 172040 | tf_op jit(solution)/shard_map/ppermute | solution.py:628
  345.8 40.9 %collective-permute-start.51 = (bf16[4,4,32,1024]{3,2,1,0:T(8,128)(2,1)S(1)}, bf16[4,4,32,1024]{3,2,1,0:T(8,128)(2,1)S(1)}, u32[]{:S(2)}, u32[]{:S(2)}) collective-permute-start(bf16[4,4,32,1024]{3,2,1,0:T(8,128)(2,1)S(1)} %pad_maximum_fusion.2), channel_id=1, source_target_pairs={{0,8},{8,0},{16,24},{24,16},{1,9},{9,1},{17,25},{25,17},{2,10},{10... | collective-permute-start | bytes 3145736 | tf_op jit(solution)/shard_map/ppermute | solution.py:626
  369.3 17.1 %collective-permute-start.53 = (bf16[1056,256]{1,0:T(8,128)(2,1)S(1)}, bf16[1056,256]{1,0:T(8,128)(2,1)S(1)}, u32[]{:S(2)}, u32[]{:S(2)}) collective-permute-start(bf16[1056,256]{1,0:T(8,128)(2,1)S(1)} %fusion.8), channel_id=1, source_target_pairs={{0,16},{8,24},{16,0},{24,8},{1,17},{9,25},{17,1},{25,9},{2,18},{10... | collective-permute-start | bytes 1622024 | tf_op jit(solution)/shard_map/ppermute | solution.py:596
  369.5 13.5 %collective-permute-start.41 = (bf16[256,1024]{1,0:T(8,128)(2,1)S(1)}, bf16[256,1024]{1,0:T(8,128)(2,1)S(1)}, u32[]{:S(2)}, u32[]{:S(2)}) collective-permute-start(bf16[256,1024]{1,0:T(8,128)(2,1)S(1)} %copy-done.40), channel_id=1, source_target_pairs={{0,1},{1,0},{2,3},{3,2},{4,5},{5,4},{6,7},{7,6},{8,9},{9,8},{10,11... | collective-permute-start | bytes 1572872 | tf_op jit(solution)/shard_map/ppermute | solution.py:596
  (65 other events, 724.3 us)

commit v4 on v3

--- a/solution.py
+++ b/solution.py
@@ -833,12 +833,8 @@
     entries = []
     for k in range(grid.y):
         piece = got if k == 0 else grid.swap(got, "y", k)
-        entries.append((2 * k, piece))
-    return [
-        pair
-        for q, piece in entries
-        for pair in ((q, piece), (q + 1, grid.swap(after(piece, tie), "c", 1)))
-    ]
+        entries += [(2 * k, piece), (2 * k + 1, grid.swap(after(piece, tie), "c", 1))]
+    return entries
 
 
 def reduce_core(grid, even, odd):
@@ -911,60 +907,49 @@
         [lax.dynamic_slice_in_dim(v, spot[0] * lanes, lanes, 1) for v in own]
     )
     dys = [upstream] + [grid.swap(upstream, "x", r) for r in range(1, grid.x)]
-    far = grid.bits("z")[::-1]
-    held, rels = payload[None], [0]
-
     xa, qfac, fac = enter(x, attngain[None, :], weights, cosine, sine)
-    near = jnp.stack(grid.direct(fac, "z"))
-    held = after(held, near)
-    arrived = [grid.swap(held, "z", far[0])] if far else []
+    rels = grid.rels("z")[1:]
+    near = [fac] + [grid.swap(fac, "z", r) for r in rels[:-1]]
+    near = near + [grid.swap(after(fac, *dys[1:]), "z", r) for r in rels[-1:]]
+    near = jnp.stack(near)
     facs = [near] + [grid.swap(near, "x", r) for r in range(1, grid.x)]
-    stages = []
-    for k, bit in enumerate(far):
-        got = arrived[k]
-        new = [r ^ bit for r in rels]
-        if k + 1 < len(far):
-            held = jnp.concatenate([held, got], axis=0)
-            arrived.append(grid.swap(held, "z", far[k + 1]))
-        rels = rels + new
-        stages.append((new, got))
-    qfac = after(qfac, held, *dys[1:])
+    shards = [payload]
+    for bit in grid.bits("z")[::-1]:
+        got = [grid.swap(v, "z", bit) for v in shards]
+        shards = shards + [after(v, near) for v in got]
+    remote = shards[1:]
+
+    nearby = jnp.stack(remote[:-1]) if len(remote) > 1 else None
+    if len(remote) > 1:
+        qfac = after(qfac, nearby)
     attn_out, lse = attention_forward(scal, qfac, facs, start)
-    stages = [
-        [
-            (new, q, v)
-            for q, v in spread_pieces(
-                grid, after(got, attn_out) if k == len(stages) - 1 else got, attn_out
-            )
-        ]
-        for k, (new, got) in enumerate(stages)
-    ]
+    early, late = [], []
+    if len(remote) > 1:
+        slots = list(range(1, len(remote)))
+        early = [(slots, q, v) for q, v in spread_pieces(grid, nearby, attn_out)]
 
     local = x.astype(F32)
     residual = local + jnp.dot(attn_out, outproj, preferred_element_type=jnp.float32)
     inverse_two = lax.rsqrt(jnp.mean(residual * residual, axis=-1, keepdims=True) + EPS)
     normed_two = residual * inverse_two
     input_two = (normed_two * ffngain).astype(jnp.bfloat16)
-    xfs = [input_two] + [grid.swap(input_two, "x", r) for r in range(1, grid.x)]
-
-    early, late, filled = [], [], 1
-    for entries in stages[:-1]:
-        for rels, q, v in entries:
-            early.append(([filled + i for i in range(len(rels))], q, v))
-        filled += len(entries[0][0])
-    for rels, q, v in stages[-1] if stages else []:
-        late.append((list(range(len(rels))), q, v))
-
-
+    xfs = [input_two] + [
+        grid.swap(input_two, "x", r) for r in range(1, grid.x)
+    ]
+
+    across = xfs[-1]
     results = [None] * grid.x
     firsts = []
     for k in range(grid.x):
-        kind = BF if k and not late else F32
+        kind = BF if k and not remote else F32
         if k:
             xfs[k] = after(xfs[k], firsts[0][0])
         firsts.append(
             ffn(spot, xfs[k], dys[k], own, early, parts, width, (), kind, "ffn_early")
         )
+    if remote:
+        last = after(remote[-1], attn_out)[None]
+        late = [([0], q, v) for q, v in spread_pieces(grid, last, after(firsts[0][0], across))]
     for k in reversed(range(grid.x)):
         first = firsts[k]
         if late:

time: 411 us -> 366 us (0.89); the launches traced: 406 us -> 366 us
  waiting for transfers between devices: 165 us -> 111 us
  starting transfers between devices: 104 us -> 119 us
  local copies, waits for them, and re-layouts: 15.9 us -> 11.5 us
    ppermute x28 -> x29, waiting for transfers between devices: 109 us -> 52.4 us  [swap(): return lax.ppermute(v, axis, [(i, i ^ r * stride) for i in range(total)])]
    ppermute x16, starting transfers between devices: 51.4 us -> 63.9 us  [swap_masks(): lax.ppermute(v, 'tensor', [(i, i ^ tensor_mask) for i in range(self.tenso...]
    unnamed x83 -> x86, local copies, waits for them, and re-layouts: 9.06 us -> 5.9 us
    ppermute x28 -> x29, starting transfers between devices: 42.1 us -> 42.9 us  [swap(): return lax.ppermute(v, axis, [(i, i ^ r * stride) for i in range(total)])]
  transfers between devices with their start and end apart: 56 -> 57, of which waited for: 29 -> 26; matrix products, arithmetic and copies ran while one was open for 7% -> 9% of each run, Pallas kernels for 14% -> 17%
where the time goes in v4:
time: 366 us
  starting transfers between devices  119 us (33%)
  waiting for transfers between devices  111 us (30%)
  Pallas kernels  93.5 us (26%)
  other arithmetic  25.3 us (7%)
  local copies, waits for them, and re-layouts  11.5 us (3%)
    ppermute x16, starting transfers between devices, swap_masks(): lax.ppermute(v, 'tensor', [(i, i ^ tensor_mask) for i in range(self.tenso...  63.9 us
    ppermute x29, waiting for transfers between devices, swap(): return lax.ppermute(v, axis, [(i, i ^ r * stride) for i in range(total)])  52.4 us
    ppermute x16, waiting for transfers between devices, swap_masks(): lax.ppermute(v, 'tensor', [(i, i ^ tensor_mask) for i in range(self.tenso...  43.1 us
    ppermute x29, starting transfers between devices, swap(): return lax.ppermute(v, axis, [(i, i ^ r * stride) for i in range(total)])  42.9 us
    pallas_call x4, Pallas kernels, ffn(): pl.pallas_call(functools.partial(ffn_kernel, parts, plan, shards, bool(be...  31.8 us
    pallas_call x1, Pallas kernels, attention_backward(): pl.pallas_call(functools.partial(backward_kernel, across), out_shape=(jax...  14.3 us
    pallas_call x2, Pallas kernels, grads(): pl.pallas_call(kernel, out_shape=(jax.ShapeDtypeStruct((parts // 2, zs, r...  14.2 us
    pallas_call x1, Pallas kernels, attention_forward(): pl.pallas_call(functools.partial(forward_kernel, len(facs)), out_shape=(j...  11.7 us
  transfers between devices with their start and end apart: 57, of which 26 were waited for; matrix products, arithmetic and copies ran while one was open for 9% of the time, Pallas kernels for 17%

profile of v4, /device:TPU:0, one launch (start us, length us, event | category | flops | bytes accessed | tf_op | source)
XLA Modules:
  0.0 365.9 jit_solution(17701632310517806184)
XLA Ops:
  18.2 3.6 collective-permute-start.4
  21.8 20.7 %collective-permute-done.1 = bf16[320,256]{1,0:T(8,128)(2,1)S(1)} collective-permute-done((bf16[320,256]{1,0:T(8,128)(2,1)S(1)}, bf16[320,256]{1,0:T(8,128)(2,1)S(1)}, u32[]{:S(2)}, u32[]{:S(2)}) %collective-permute-start.1) | collective-permute-done | bytes 163872 | tf_op jit(solution)/shard_map/ppermute | solution.py:596
  58.1 7.4 %collective-permute-done.7 = bf16[3,352,256]{2,1,0:T(8,128)(2,1)} collective-permute-done((bf16[3,352,256]{2,1,0:T(8,128)(2,1)}, bf16[3,352,256]{2,1,0:T(8,128)(2,1)}, u32[]{:S(2)}, u32[]{:S(2)}) %collective-permute-start.7) | collective-permute-done | bytes 540704 | tf_op jit(solution)/shard_map/ppermute | solution.py:596
  65.5 11.7 %attention_forward.1 = (bf16[256,1024]{1,0:T(8,128)(2,1)}, f32[16,256,128]{2,1,0:T(8,128)}) custom-call(s32[2]{0:T(128)} %pad_add_fusion.scal_ref, bf16[480,256]{1,0:T(8,128)(2,1)} %copy-done.9, bf16[4,320,256]{2,1,0:T(8,128)(2,1)} %pad_maximum_fusion.5.refs_0_, bf16[4,320,256]{2,1,0:T(8,128)(2,1)} %collective-permute-done.6.refs_1_, ...), custom_call_target="tpu_custom_call" | custom-call | flops 1000 | bytes 1000 | tf_op jit(solution)/shard_map/attention_forward/pallas_call | solution.py:158
  81.5 5.7 %collective-permute-start.11 = (bf16[256,1024]{1,0:T(8,128)(2,1)}, bf16[256,1024]{1,0:T(8,128)(2,1)}, u32[]{:S(2)}, u32[]{:S(2)}) collective-permute-start(bf16[256,1024]{1,0:T(8,128)(2,1)} %multiply_convert_fusion.xf_ref.refs_0_), channel_id=1, source_target_pairs={{0,1},{1,0},{2,3},{3,2},{4,5},{5,4},{6,7},{7,6},{8,9},{9,8},{10,11... | collective-permute-start | bytes 1572872 | tf_op jit(solution)/shard_map/ppermute | solution.py:596
  87.8 9.6 %ffn_early.2 = (f32[256,1024]{1,0:T(8,128)}, f32[256,1024]{1,0:T(8,128)}, bf16[1,256,1056]{2,1,0:T(8,128)(2,1)}, bf16[1,256,1056]{2,1,0:T(8,128)(2,1)}, bf16[1,256,1056]{2,1,0:T(8,128)(2,1)}) custom-call(s32[2]{0:T(128)} %pad_add_fusion.1.scal_ref, bf16[256,1024]{1,0:T(8,128)(2,1)} %multiply_convert_fusion.xf_ref.refs_0_, bf16[256,1024]{1,0:T(8,128)(2,1)} %bitcast.187, ...), custom_call_target="tpu_custom_call" | custom-call | flops 1000 | bytes 1000 | tf_op jit(solution)/shard_map/ffn_early/pallas_call | solution.py:722
  100.2 9.6 %ffn_early.3 = (f32[256,1024]{1,0:T(8,128)}, f32[256,1024]{1,0:T(8,128)}, bf16[1,256,1056]{2,1,0:T(8,128)(2,1)}, bf16[1,256,1056]{2,1,0:T(8,128)(2,1)}, bf16[1,256,1056]{2,1,0:T(8,128)(2,1)}) custom-call(s32[2]{0:T(128)} %pad_add_fusion.1.scal_ref, bf16[256,1024]{1,0:T(8,128)(2,1)} %collective-permute-done.11.xf_ref.refs_1_, ...), custom_call_target="tpu_custom_call" | custom-call | flops 1000 | bytes 1000 | tf_op jit(solution)/shard_map/ffn_early/pallas_call | solution.py:722
  110.8 6.5 %ffn_late.2 = (f32[256,1024]{1,0:T(8,128)}, f32[256,1024]{1,0:T(8,128)}, bf16[1,256,352]{2,1,0:T(8,128)(2,1)}, bf16[1,256,352]{2,1,0:T(8,128)(2,1)}, bf16[1,256,352]{2,1,0:T(8,128)(2,1)}) custom-call(s32[2]{0:T(128)} %pad_add_fusion.1.scal_ref, bf16[256,1024]{1,0:T(8,128)(2,1)} %multiply_convert_fusion.xf_ref.refs_0_, bf16[256,1024]{1,0:T(8,128)(2,1)} %bitcast.188, ...), custom_call_target="tpu_custom_call" | custom-call | flops 1000 | bytes 1000 | tf_op jit(solution)/shard_map/ffn_late/pallas_call | solution.py:722
  117.3 6.1 %ffn_late.3 = (bf16[256,1024]{1,0:T(8,128)(2,1)}, bf16[256,1024]{1,0:T(8,128)(2,1)}, bf16[1,256,352]{2,1,0:T(8,128)(2,1)}, bf16[1,256,352]{2,1,0:T(8,128)(2,1)}, bf16[1,256,352]{2,1,0:T(8,128)(2,1)}) custom-call(s32[2]{0:T(128)} %pad_add_fusion.1.scal_ref, bf16[256,1024]{1,0:T(8,128)(2,1)} %collective-permute-done.11.xf_ref.refs_1_, ...), custom_call_target="tpu_custom_call" | custom-call | flops 1000 | bytes 1000 | tf_op jit(solution)/shard_map/ffn_late/pallas_call | solution.py:722
  123.4 8.9 %gate_up_grads.1 = (bf16[2,4,704,256]{3,2,1,0:T(8,128)(2,1)}, bf16[2,4,704,256]{3,2,1,0:T(8,128)(2,1)}) custom-call(s32[2]{0:T(128)} %pad_add_fusion.1.scal_ref, bf16[256,1024]{1,0:T(8,128)(2,1)} %multiply_convert_fusion.xf_ref.refs_0_, bf16[256,1024]{1,0:T(8,128)(2,1)} %collective-permute-done.11.xf_ref.refs_1_, ...), custom_call_target="tpu_custom_call" | custom-call | flops 1000 | bytes 1000 | tf_op jit(solution)/shard_map/gate_up_grads/pallas_call | solution.py:790
  134.2 5.3 %down_grads.1 = (bf16[2,4,352,256]{3,2,1,0:T(8,128)(2,1)}, bf16[2,4,352,256]{3,2,1,0:T(8,128)(2,1)}) custom-call(s32[2]{0:T(128)} %pad_add_fusion.1.scal_ref, bf16[256,1024]{1,0:T(8,128)(2,1)} %bitcast.189, bf16[256,1024]{1,0:T(8,128)(2,1)} %collective-permute-done.3.dy_ref.refs_1_, bf16[1,256,1056]{2,1,0:T(8,128)(2,1)} %get-tuple-element.114.refs_2_, ...), custom_call_target="tpu_custom_call" | custom-call | flops 1000 | bytes 1000 | tf_op jit(solution)/shard_map/down_grads/pallas_call | solution.py:790
  139.7 3.4 fusion.4
  143.1 3.9 %collective-permute-done.15 = bf16[256,1024]{1,0:T(8,128)(2,1)} collective-permute-done((bf16[256,1024]{1,0:T(8,128)(2,1)}, bf16[256,1024]{1,0:T(8,128)(2,1)}, u32[]{:S(2)}, u32[]{:S(2)}) %collective-permute-start.15) | collective-permute-done | bytes 524320 | tf_op jit(solution)/shard_map/ppermute | solution.py:596
  162.8 14.3 %attention_backward.1 = (bf16[4,320,256]{2,1,0:T(8,128)(2,1)}, bf16[4,320,256]{2,1,0:T(8,128)(2,1)}, bf16[480,256]{1,0:T(8,128)(2,1)}) custom-call(s32[2]{0:T(128)} %pad_add_fusion.scal_ref, bf16[480,256]{1,0:T(8,128)(2,1)} %copy-done.9, bf16[4,320,256]{2,1,0:T(8,128)(2,1)} %pad_maximum_fusion.5.refs_0_, ...), custom_call_target="tpu_custom_call" | custom-call | flops 1000 | bytes 1000 | tf_op jit(solution)/shard_map/attention_backward/pallas_call | solution.py:304
  178.5 7.4 %collective-permute-start.20 = (bf16[4,320,256]{2,1,0:T(8,128)(2,1)}, bf16[4,320,256]{2,1,0:T(8,128)(2,1)S(1)}, u32[]{:S(2)}, u32[]{:S(2)}) collective-permute-start(bf16[4,320,256]{2,1,0:T(8,128)(2,1)} %get-tuple-element.138), channel_id=1, source_target_pairs={{0,1},{1,0},{2,3},{3,2},{4,5},{5,4},{6,7},{7,6},{8,9},{9,8},{10,11... | collective-permute-start | bytes 1966088 | tf_op jit(solution)/shard_map/ppermute | solution.py:596
  187.9 23.7 %collective-permute-start.24 = (bf16[32,1024]{1,0:T(8,128)(2,1)S(1)}, bf16[32,1024]{1,0:T(8,128)(2,1)S(1)}, u32[]{:S(2)}, u32[]{:S(2)}) collective-permute-start(bf16[32,1024]{1,0:T(8,128)(2,1)S(1)} %get-tuple-element.187), channel_id=1, source_target_pairs={{0,2},{1,3},{2,0},{3,1},{4,6},{5,7},{6,4},{7,5},{8,10},{9,11},{10,... | collective-permute-start | bytes 196616 | tf_op jit(solution)/shard_map/ppermute | solution.py:628
  211.7 22.5 %collective-permute-start.25 = (bf16[32,1024]{1,0:T(8,128)(2,1)S(1)}, bf16[32,1024]{1,0:T(8,128)(2,1)S(1)}, u32[]{:S(2)}, u32[]{:S(2)}) collective-permute-start(bf16[32,1024]{1,0:T(8,128)(2,1)S(1)} %get-tuple-element.189), channel_id=1, source_target_pairs={{0,4},{1,5},{2,6},{3,7},{4,0},{5,1},{6,2},{7,3},{8,12},{9,13},{10,... | collective-permute-start | bytes 196616 | tf_op jit(solution)/shard_map/ppermute | solution.py:628
  236.5 3.8 %collective-permute-done.26 = bf16[32,1024]{1,0:T(8,128)(2,1)S(1)} collective-permute-done((bf16[32,1024]{1,0:T(8,128)(2,1)S(1)}, bf16[32,1024]{1,0:T(8,128)(2,1)S(1)}, u32[]{:S(2)}, u32[]{:S(2)}) %collective-permute-start.26) | collective-permute-done | bytes 65568 | tf_op jit(solution)/shard_map/ppermute | solution.py:628
  245.5 6.1 %collective-permute-done.28 = bf16[32,1024]{1,0:T(8,128)(2,1)S(1)} collective-permute-done((bf16[32,1024]{1,0:T(8,128)(2,1)S(1)}, bf16[32,1024]{1,0:T(8,128)(2,1)S(1)}, u32[]{:S(2)}, u32[]{:S(2)}) %collective-permute-start.28) | collective-permute-done | bytes 65568 | tf_op jit(solution)/shard_map/ppermute | solution.py:628
  252.0 4.0 %collective-permute-start.31 = (bf16[320,256]{1,0:T(8,128)(2,1)S(1)}, bf16[320,256]{1,0:T(8,128)(2,1)S(1)}, u32[]{:S(2)}, u32[]{:S(2)}) collective-permute-start(bf16[320,256]{1,0:T(8,128)(2,1)S(1)} %get-tuple-element.184), channel_id=1, source_target_pairs={{0,4},{1,5},{2,6},{3,7},{4,0},{5,1},{6,2},{7,3},{8,12},{9,13},{10,... | collective-permute-start | bytes 491528 | tf_op jit(solution)/shard_map/ppermute | solution.py:596
  261.3 3.7 collective-permute-done.33
  265.1 4.6 %leave_rest.1 = (bf16[256,1024]{1,0:T(8,128)(2,1)}, bf16[16,32,896]{2,1,0:T(8,128)(2,1)S(1)}, bf16[16,32,896]{2,1,0:T(8,128)(2,1)S(1)}) custom-call(s32[3]{0:T(128)S(1)} %pad_add_fusion.2.ids_ref, bf16[256,1024]{1,0:T(8,128)(2,1)S(1)} %bitcast.168, bf16[256,1024]{1,0:T(8,128)(2,1)S(1)} %copy-done.17, f32[1,1024]{1,0:T(1,128)S(1)} %bitcast.182, ...), custom_call_target="tpu_custom_call" | custom-call | flops 1000 | bytes 1000 | tf_op jit(solution)/shard_map/leave_rest/pallas_call | solution.py:502
  271.9 3.4 collective-permute-start.37
  275.6 4.9 %collective-permute-done.35 = bf16[4,32,1024]{2,1,0:T(8,128)(2,1)S(1)} collective-permute-done((bf16[4,32,1024]{2,1,0:T(8,128)(2,1)S(1)}, bf16[4,32,1024]{2,1,0:T(8,128)(2,1)S(1)}, u32[]{:S(2)}, u32[]{:S(2)}) %collective-permute-start.35) | collective-permute-done | bytes 262176 | tf_op jit(solution)/shard_map/ppermute | solution.py:626
  281.0 6.3 %collective-permute-done.37 = bf16[4,32,1024]{2,1,0:T(8,128)(2,1)S(1)} collective-permute-done((bf16[4,32,1024]{2,1,0:T(8,128)(2,1)S(1)}, bf16[4,32,1024]{2,1,0:T(8,128)(2,1)S(1)}, u32[]{:S(2)}, u32[]{:S(2)}) %collective-permute-start.37) | collective-permute-done | bytes 262176 | tf_op jit(solution)/shard_map/ppermute | solution.py:631
  290.9 7.1 %collective-permute-done.41 = bf16[2,1056,256]{2,1,0:T(8,128)(2,1)S(1)} collective-permute-done((bf16[2,1056,256]{2,1,0:T(8,128)(2,1)S(1)}, bf16[2,1056,256]{2,1,0:T(8,128)(2,1)S(1)}, u32[]{:S(2)}, u32[]{:S(2)}) %collective-permute-start.41) | collective-permute-done | bytes 1081376 | tf_op jit(solution)/shard_map/ppermute | solution.py:596
  305.2 7.9 %collective-permute-done.43 = bf16[32,896]{1,0:T(8,128)(2,1)S(1)} collective-permute-done((bf16[32,896]{1,0:T(8,128)(2,1)S(1)}, bf16[32,896]{1,0:T(8,128)(2,1)S(1)}, u32[]{:S(2)}, u32[]{:S(2)}) %collective-permute-start.43) | collective-permute-done | bytes 57376 | tf_op jit(solution)/shard_map/ppermute | solution.py:628
  313.1 15.3 %collective-permute-done.44 = bf16[32,896]{1,0:T(8,128)(2,1)S(1)} collective-permute-done((bf16[32,896]{1,0:T(8,128)(2,1)S(1)}, bf16[32,896]{1,0:T(8,128)(2,1)S(1)}, u32[]{:S(2)}, u32[]{:S(2)}) %collective-permute-start.44) | collective-permute-done | bytes 57376 | tf_op jit(solution)/shard_map/ppermute | solution.py:628
  339.2 3.4 collective-permute-done.42
  346.2 3.5 end_out.1
  356.5 5.5 %unpack.1 = (f32[352,1024]{1,0:T(8,128)}, f32[352,1024]{1,0:T(8,128)}, f32[352,1024]{1,0:T(8,128)}) custom-call(s32[2]{0:T(128)} %pad_add_fusion.1.scal_ref, bf16[2,1056,256]{2,1,0:T(8,128)(2,1)} %copy-done.27, bf16[2,1056,256]{2,1,0:T(8,128)(2,1)} %collective-permute-done.55.got_ref), custom_call_target="tpu_custom_call" | custom-call | flops 1000 | bytes 1000 | tf_op jit(solution)/shard_map/unpack/pallas_call | solution.py:817
  362.0 3.8 %end_rest.1 = (f32[1024,128]{1,0:T(8,128)}, f32[1024,128]{1,0:T(8,128)}, f32[1024,384]{1,0:T(8,128)}, f32[96,1024]{1,0:T(8,128)}, f32[32,1024]{1,0:T(8,128)}, /*...) custom-call(s32[3]{0:T(128)S(1)} %pad_add_fusion.2.ids_ref, bf16[16,32,896]{2,1,0:T(8,128)(2,1)S(1)} %bitcast.170, ...), custom_call_target="tpu_custom_call" | custom-call | tf_op jit(solution)/shard_map/end_rest/pallas_call | solution.py:557
  (234 shorter events, 110.3 us)
Async XLA Ops:
  0.7 17.5 %collective-permute-start.3 = (bf16[256,1024]{1,0:T(8,128)(2,1)}, bf16[256,1024]{1,0:T(8,128)(2,1)}, u32[]{:S(2)}, u32[]{:S(2)}) collective-permute-start(bf16[256,1024]{1,0:T(8,128)(2,1)} %bitcast.186), channel_id=1, source_target_pairs={{0,1},{1,0},{2,3},{3,2},{4,5},{5,4},{6,7},{7,6},{8,9},{9,8},{10,11... | collective-permute-start | bytes 1572872 | tf_op jit(solution)/shard_map/ppermute | solution.py:596
  6.6 39.1 %collective-permute-start = (bf16[3,352,256]{2,1,0:T(8,128)(2,1)}, bf16[3,352,256]{2,1,0:T(8,128)(2,1)}, u32[]{:S(2)}, u32[]{:S(2)}) collective-permute-start(bf16[3,352,256]{2,1,0:T(8,128)(2,1)} %pad_maximum_fusion.6), channel_id=1, source_target_pairs={{0,4},{1,5},{2,6},{3,7},{4,0},{5,1},{6,2},{7,3},{8,12},{9,13},{10,... | collective-permute-start | bytes 1622024 | tf_op jit(solution)/shard_map/ppermute | solution.py:596
  9.2 36.5 %collective-permute-start.5 = (bf16[3,352,256]{2,1,0:T(8,128)(2,1)}, bf16[3,352,256]{2,1,0:T(8,128)(2,1)}, u32[]{:S(2)}, u32[]{:S(2)}) collective-permute-start(bf16[3,352,256]{2,1,0:T(8,128)(2,1)} %pad_maximum_fusion.6), channel_id=1, source_target_pairs={{0,2},{1,3},{2,0},{3,1},{4,6},{5,7},{6,4},{7,5},{8,10},{9,11},{10,... | collective-permute-start | bytes 1622024 | tf_op jit(solution)/shard_map/ppermute | solution.py:596
  17.4 25.2 %collective-permute-start.1 = (bf16[320,256]{1,0:T(8,128)(2,1)S(1)}, bf16[320,256]{1,0:T(8,128)(2,1)S(1)}, u32[]{:S(2)}, u32[]{:S(2)}) collective-permute-start(bf16[320,256]{1,0:T(8,128)(2,1)S(1)} %get-tuple-element.92), channel_id=1, source_target_pairs={{0,4},{1,5},{2,6},{3,7},{4,0},{5,1},{6,2},{7,3},{8,12},{9,13},{10,... | collective-permute-start | bytes 491528 | tf_op jit(solution)/shard_map/ppermute | solution.py:596
  17.8 24.8 %collective-permute-start.2 = (bf16[320,256]{1,0:T(8,128)(2,1)S(1)}, bf16[320,256]{1,0:T(8,128)(2,1)S(1)}, u32[]{:S(2)}, u32[]{:S(2)}) collective-permute-start(bf16[320,256]{1,0:T(8,128)(2,1)S(1)} %get-tuple-element.92), channel_id=1, source_target_pairs={{0,2},{1,3},{2,0},{3,1},{4,6},{5,7},{6,4},{7,5},{8,10},{9,11},{10,... | collective-permute-start | bytes 491528 | tf_op jit(solution)/shard_map/ppermute | solution.py:596
  18.2 26.5 %collective-permute-start.4 = (bf16[320,256]{1,0:T(8,128)(2,1)S(1)}, bf16[320,256]{1,0:T(8,128)(2,1)S(1)}, u32[]{:S(2)}, u32[]{:S(2)}) collective-permute-start(bf16[320,256]{1,0:T(8,128)(2,1)S(1)} %get-tuple-element.92), channel_id=1, source_target_pairs={{0,6},{1,7},{2,4},{3,5},{4,2},{5,3},{6,0},{7,1},{8,14},{9,15},{10,... | collective-permute-start | bytes 491528 | tf_op jit(solution)/shard_map/ppermute | solution.py:596
  47.9 29.3 %collective-permute-start.9 = (bf16[2,3,352,256]{3,2,1,0:T(8,128)(2,1)}, bf16[2,3,352,256]{3,2,1,0:T(8,128)(2,1)}, u32[]{:S(2)}, u32[]{:S(2)}) collective-permute-start(bf16[2,3,352,256]{3,2,1,0:T(8,128)(2,1)} %pad_maximum_fusion.1.refs_3_), channel_id=1, source_target_pairs={{0,16},{8,24},{16,0},{24,8},{1,17},{9,25},{17,1},{25,9},{2,18},{10... | collective-permute-start | bytes 3244040 | tf_op jit(solution)/shard_map/ppermute | solution.py:596
  49.5 16.0 %collective-permute-start.6 = (bf16[4,320,256]{2,1,0:T(8,128)(2,1)}, bf16[4,320,256]{2,1,0:T(8,128)(2,1)}, u32[]{:S(2)}, u32[]{:S(2)}) collective-permute-start(bf16[4,320,256]{2,1,0:T(8,128)(2,1)} %pad_maximum_fusion.5.refs_0_), channel_id=1, source_target_pairs={{0,1},{1,0},{2,3},{3,2},{4,5},{5,4},{6,7},{7,6},{8,9},{9,8},{10,11... | collective-permute-start | bytes 1966088 | tf_op jit(solution)/shard_map/ppermute | solution.py:596
  50.3 15.2 %collective-permute-start.7 = (bf16[3,352,256]{2,1,0:T(8,128)(2,1)}, bf16[3,352,256]{2,1,0:T(8,128)(2,1)}, u32[]{:S(2)}, u32[]{:S(2)}) collective-permute-start(bf16[3,352,256]{2,1,0:T(8,128)(2,1)} %collective-permute-done), channel_id=1, source_target_pairs={{0,2},{1,3},{2,0},{3,1},{4,6},{5,7},{6,4},{7,5},{8,10},{9,11},{10,... | collective-permute-start | bytes 1622024 | tf_op jit(solution)/shard_map/ppermute | solution.py:596
  79.6 20.1 %collective-permute-start.13 = (bf16[1,3,352,256]{3,2,1,0:T(8,128)(2,1)}, bf16[1,3,352,256]{3,2,1,0:T(8,128)(2,1)}, u32[]{:S(2)}, u32[]{:S(2)}) collective-permute-start(bf16[1,3,352,256]{3,2,1,0:T(8,128)(2,1)} %bitcast.24.refs_0_), channel_id=1, source_target_pairs={{0,16},{8,24},{16,0},{24,8},{1,17},{9,25},{17,1},{25,9},{2,18},{10... | collective-permute-start | bytes 1622024 | tf_op jit(solution)/shard_map/ppermute | solution.py:596
  81.5 18.2 %collective-permute-start.11 = (bf16[256,1024]{1,0:T(8,128)(2,1)}, bf16[256,1024]{1,0:T(8,128)(2,1)}, u32[]{:S(2)}, u32[]{:S(2)}) collective-permute-start(bf16[256,1024]{1,0:T(8,128)(2,1)} %multiply_convert_fusion.xf_ref.refs_0_), channel_id=1, source_target_pairs={{0,1},{1,0},{2,3},{3,2},{4,5},{5,4},{6,7},{7,6},{8,9},{9,8},{10,11... | collective-permute-start | bytes 1572872 | tf_op jit(solution)/shard_map/ppermute | solution.py:596
  132.3 14.7 %collective-permute-start.15 = (bf16[256,1024]{1,0:T(8,128)(2,1)}, bf16[256,1024]{1,0:T(8,128)(2,1)}, u32[]{:S(2)}, u32[]{:S(2)}) collective-permute-start(bf16[256,1024]{1,0:T(8,128)(2,1)} %get-tuple-element.113), channel_id=1, source_target_pairs={{0,1},{1,0},{2,3},{3,2},{4,5},{5,4},{6,7},{7,6},{8,9},{9,8},{10,11... | collective-permute-start | bytes 1572872 | tf_op jit(solution)/shard_map/ppermute | solution.py:596
  139.5 12.8 %collective-permute-start.17 = (bf16[2,4,352,256]{3,2,1,0:T(8,128)(2,1)}, bf16[2,4,352,256]{3,2,1,0:T(8,128)(2,1)S(1)}, u32[]{:S(2)}, u32[]{:S(2)}) collective-permute-start(bf16[2,4,352,256]{3,2,1,0:T(8,128)(2,1)} %get-tuple-element.130), channel_id=1, source_target_pairs={{0,8},{8,0},{16,24},{24,16},{1,9},{9,1},{17,25},{25,17},{2,10},{10... | collective-permute-start | bytes 4325384 | tf_op jit(solution)/shard_map/ppermute | solution.py:596
  153.6 24.9 %collective-permute-start.19 = (bf16[4,352,256]{2,1,0:T(8,128)(2,1)}, bf16[4,352,256]{2,1,0:T(8,128)(2,1)}, u32[]{:S(2)}, u32[]{:S(2)}) collective-permute-start(bf16[4,352,256]{2,1,0:T(8,128)(2,1)} %fusion.7), channel_id=1, source_target_pairs={{0,16},{8,24},{16,0},{24,8},{1,17},{9,25},{17,1},{25,9},{2,18},{10... | collective-permute-start | bytes 2162696 | tf_op jit(solution)/shard_map/ppermute | solution.py:596
  156.9 29.1 %collective-permute-start.21 = (bf16[4,32,1024]{2,1,0:T(8,128)(2,1)S(1)}, bf16[4,32,1024]{2,1,0:T(8,128)(2,1)S(1)}, u32[]{:S(2)}, u32[]{:S(2)}) collective-permute-start(bf16[4,32,1024]{2,1,0:T(8,128)(2,1)S(1)} %get-tuple-element.178), channel_id=1, source_target_pairs={{0,16},{8,24},{16,0},{24,8},{1,17},{9,25},{17,1},{25,9},{2,18},{10... | collective-permute-start | bytes 786440 | tf_op jit(solution)/shard_map/ppermute | solution.py:626
  157.8 28.2 %collective-permute-start.22 = (bf16[4,32,1024]{2,1,0:T(8,128)(2,1)S(1)}, bf16[4,32,1024]{2,1,0:T(8,128)(2,1)}, u32[]{:S(2)}, u32[]{:S(2)}) collective-permute-start(bf16[4,32,1024]{2,1,0:T(8,128)(2,1)S(1)} %get-tuple-element.180), channel_id=1, source_target_pairs={{0,1},{1,0},{2,3},{3,2},{4,5},{5,4},{6,7},{7,6},{8,9},{9,8},{10,11... | collective-permute-start | bytes 786440 | tf_op jit(solution)/shard_map/ppermute | solution.py:628
  159.5 27.1 %collective-permute-start.23 = (bf16[4,32,1024]{2,1,0:T(8,128)(2,1)S(1)}, bf16[4,32,1024]{2,1,0:T(8,128)(2,1)}, u32[]{:S(2)}, u32[]{:S(2)}) collective-permute-start(bf16[4,32,1024]{2,1,0:T(8,128)(2,1)S(1)} %get-tuple-element.179), channel_id=1, source_target_pairs={{0,17},{1,16},{2,19},{3,18},{4,21},{5,20},{6,23},{7,22},{8,25},{9,... | collective-permute-start | bytes 786440 | tf_op jit(solution)/shard_map/ppermute | solution.py:631
  162.0 90.0 %collective-permute-start.30 = (bf16[4,704,256]{2,1,0:T(8,128)(2,1)}, bf16[4,704,256]{2,1,0:T(8,128)(2,1)S(1)}, u32[]{:S(2)}, u32[]{:S(2)}) collective-permute-start(bf16[4,704,256]{2,1,0:T(8,128)(2,1)} %fusion.4), channel_id=1, source_target_pairs={{0,16},{8,24},{16,0},{24,8},{1,17},{9,25},{17,1},{25,9},{2,18},{10... | collective-permute-start | bytes 4325384 | tf_op jit(solution)/shard_map/ppermute | solution.py:596
  178.5 73.2 %collective-permute-start.20 = (bf16[4,320,256]{2,1,0:T(8,128)(2,1)}, bf16[4,320,256]{2,1,0:T(8,128)(2,1)S(1)}, u32[]{:S(2)}, u32[]{:S(2)}) collective-permute-start(bf16[4,320,256]{2,1,0:T(8,128)(2,1)} %get-tuple-element.138), channel_id=1, source_target_pairs={{0,1},{1,0},{2,3},{3,2},{4,5},{5,4},{6,7},{7,6},{8,9},{9,8},{10,11... | collective-permute-start | bytes 1966088 | tf_op jit(solution)/shard_map/ppermute | solution.py:596
  187.9 47.7 %collective-permute-start.24 = (bf16[32,1024]{1,0:T(8,128)(2,1)S(1)}, bf16[32,1024]{1,0:T(8,128)(2,1)S(1)}, u32[]{:S(2)}, u32[]{:S(2)}) collective-permute-start(bf16[32,1024]{1,0:T(8,128)(2,1)S(1)} %get-tuple-element.187), channel_id=1, source_target_pairs={{0,2},{1,3},{2,0},{3,1},{4,6},{5,7},{6,4},{7,5},{8,10},{9,11},{10,... | collective-permute-start | bytes 196616 | tf_op jit(solution)/shard_map/ppermute | solution.py:628
  211.7 24.9 %collective-permute-start.25 = (bf16[32,1024]{1,0:T(8,128)(2,1)S(1)}, bf16[32,1024]{1,0:T(8,128)(2,1)S(1)}, u32[]{:S(2)}, u32[]{:S(2)}) collective-permute-start(bf16[32,1024]{1,0:T(8,128)(2,1)S(1)} %get-tuple-element.189), channel_id=1, source_target_pairs={{0,4},{1,5},{2,6},{3,7},{4,0},{5,1},{6,2},{7,3},{8,12},{9,13},{10,... | collective-permute-start | bytes 196616 | tf_op jit(solution)/shard_map/ppermute | solution.py:628
  271.6 26.3 %collective-permute-start.41 = (bf16[2,1056,256]{2,1,0:T(8,128)(2,1)S(1)}, bf16[2,1056,256]{2,1,0:T(8,128)(2,1)S(1)}, u32[]{:S(2)}, u32[]{:S(2)}) collective-permute-start(bf16[2,1056,256]{2,1,0:T(8,128)(2,1)S(1)} %fusion.2), channel_id=1, source_target_pairs={{0,2},{1,3},{2,0},{3,1},{4,6},{5,7},{6,4},{7,5},{8,10},{9,11},{10,... | collective-permute-start | bytes 3244040 | tf_op jit(solution)/shard_map/ppermute | solution.py:596
  271.9 15.4 %collective-permute-start.37 = (bf16[4,32,1024]{2,1,0:T(8,128)(2,1)S(1)}, bf16[4,32,1024]{2,1,0:T(8,128)(2,1)S(1)}, u32[]{:S(2)}, u32[]{:S(2)}) collective-permute-start(bf16[4,32,1024]{2,1,0:T(8,128)(2,1)S(1)} %pad_maximum_fusion.7), channel_id=1, source_target_pairs={{0,17},{1,16},{2,19},{3,18},{4,21},{5,20},{6,23},{7,22},{8,25},{9,... | collective-permute-start | bytes 786440 | tf_op jit(solution)/shard_map/ppermute | solution.py:631
  287.4 11.9 %collective-permute-start.38 = (bf16[4,32,896]{2,1,0:T(8,128)(2,1)S(1)}, bf16[4,32,896]{2,1,0:T(8,128)(2,1)S(1)}, u32[]{:S(2)}, u32[]{:S(2)}) collective-permute-start(bf16[4,32,896]{2,1,0:T(8,128)(2,1)S(1)} %get-tuple-element.181), channel_id=1, source_target_pairs={{0,16},{8,24},{16,0},{24,8},{1,17},{9,25},{17,1},{25,9},{2,18},{10... | collective-permute-start | bytes 688136 | tf_op jit(solution)/shard_map/ppermute | solution.py:626
  288.1 12.3 %collective-permute-start.40 = (bf16[4,32,896]{2,1,0:T(8,128)(2,1)S(1)}, bf16[4,32,896]{2,1,0:T(8,128)(2,1)S(1)}, u32[]{:S(2)}, u32[]{:S(2)}) collective-permute-start(bf16[4,32,896]{2,1,0:T(8,128)(2,1)S(1)} %get-tuple-element.182), channel_id=1, source_target_pairs={{0,17},{1,16},{2,19},{3,18},{4,21},{5,20},{6,23},{7,22},{8,25},{9,... | collective-permute-start | bytes 688136 | tf_op jit(solution)/shard_map/ppermute | solution.py:631
  298.3 30.2 %collective-permute-start.53 = (bf16[1,1056,256]{2,1,0:T(8,128)(2,1)S(1)}, bf16[1,1056,256]{2,1,0:T(8,128)(2,1)S(1)}, u32[]{:S(2)}, u32[]{:S(2)}) collective-permute-start(bf16[1,1056,256]{2,1,0:T(8,128)(2,1)S(1)} %slice.222), channel_id=1, source_target_pairs={{0,4},{1,5},{2,6},{3,7},{4,0},{5,1},{6,2},{7,3},{8,12},{9,13},{10,... | collective-permute-start | bytes 1622024 | tf_op jit(solution)/shard_map/ppermute | solution.py:596
  300.6 12.6 %collective-permute-start.43 = (bf16[32,896]{1,0:T(8,128)(2,1)S(1)}, bf16[32,896]{1,0:T(8,128)(2,1)S(1)}, u32[]{:S(2)}, u32[]{:S(2)}) collective-permute-start(bf16[32,896]{1,0:T(8,128)(2,1)S(1)} %get-tuple-element.190), channel_id=1, source_target_pairs={{0,2},{1,3},{2,0},{3,1},{4,6},{5,7},{6,4},{7,5},{8,10},{9,11},{10,... | collective-permute-start | bytes 172040 | tf_op jit(solution)/shard_map/ppermute | solution.py:628
  302.0 26.4 %collective-permute-start.44 = (bf16[32,896]{1,0:T(8,128)(2,1)S(1)}, bf16[32,896]{1,0:T(8,128)(2,1)S(1)}, u32[]{:S(2)}, u32[]{:S(2)}) collective-permute-start(bf16[32,896]{1,0:T(8,128)(2,1)S(1)} %get-tuple-element.192), channel_id=1, source_target_pairs={{0,4},{1,5},{2,6},{3,7},{4,0},{5,1},{6,2},{7,3},{8,12},{9,13},{10,... | collective-permute-start | bytes 172040 | tf_op jit(solution)/shard_map/ppermute | solution.py:628
  303.0 25.5 %collective-permute-start.45 = (bf16[32,896]{1,0:T(8,128)(2,1)S(1)}, bf16[32,896]{1,0:T(8,128)(2,1)S(1)}, u32[]{:S(2)}, u32[]{:S(2)}) collective-permute-start(bf16[32,896]{1,0:T(8,128)(2,1)S(1)} %get-tuple-element.191), channel_id=1, source_target_pairs={{0,6},{1,7},{2,4},{3,5},{4,2},{5,3},{6,0},{7,1},{8,14},{9,15},{10,... | collective-permute-start | bytes 172040 | tf_op jit(solution)/shard_map/ppermute | solution.py:628
  305.2 41.0 %collective-permute-start.52 = (bf16[4,4,32,1024]{3,2,1,0:T(8,128)(2,1)S(1)}, bf16[4,4,32,1024]{3,2,1,0:T(8,128)(2,1)S(1)}, u32[]{:S(2)}, u32[]{:S(2)}) collective-permute-start(bf16[4,4,32,1024]{3,2,1,0:T(8,128)(2,1)S(1)} %pad_maximum_fusion.3), channel_id=1, source_target_pairs={{0,8},{8,0},{16,24},{24,16},{1,9},{9,1},{17,25},{25,17},{2,10},{10... | collective-permute-start | bytes 3145736 | tf_op jit(solution)/shard_map/ppermute | solution.py:626
  328.6 17.4 %collective-permute-start.54 = (bf16[1056,256]{1,0:T(8,128)(2,1)S(1)}, bf16[1056,256]{1,0:T(8,128)(2,1)S(1)}, u32[]{:S(2)}, u32[]{:S(2)}) collective-permute-start(bf16[1056,256]{1,0:T(8,128)(2,1)S(1)} %fusion.8), channel_id=1, source_target_pairs={{0,16},{8,24},{16,0},{24,8},{1,17},{9,25},{17,1},{25,9},{2,18},{10... | collective-permute-start | bytes 1622024 | tf_op jit(solution)/shard_map/ppermute | solution.py:596
  328.7 13.8 %collective-permute-start.42 = (bf16[256,1024]{1,0:T(8,128)(2,1)S(1)}, bf16[256,1024]{1,0:T(8,128)(2,1)S(1)}, u32[]{:S(2)}, u32[]{:S(2)}) collective-permute-start(bf16[256,1024]{1,0:T(8,128)(2,1)S(1)} %copy-done.42), channel_id=1, source_target_pairs={{0,1},{1,0},{2,3},{3,2},{4,5},{5,4},{6,7},{7,6},{8,9},{9,8},{10,11... | collective-permute-start | bytes 1572872 | tf_op jit(solution)/shard_map/ppermute | solution.py:596
  (68 other events, 709.5 us)

commit v5 on v4

--- a/solution.py
+++ b/solution.py
@@ -1040,6 +1040,7 @@
         goes = ffn_sum[rows:].astype(BF)
         if k == 0:
             goes = after(goes, key_grads)
+            dq = after(dq, goes)
         got = grid.swap(goes, "z", bit)
         if k == 0:
             first_z = got

time: 366 us -> 363 us (level)
  waiting for transfers between devices: 111 us -> 102 us
  starting transfers between devices: 119 us -> 126 us
    ppermute x29, starting transfers between devices: 42.9 us -> 53.1 us  [swap(): return lax.ppermute(v, axis, [(i, i ^ r * stride) for i in range(total)])]
    ppermute x29, waiting for transfers between devices: 52.4 us -> 42.8 us  [swap(): return lax.ppermute(v, axis, [(i, i ^ r * stride) for i in range(total)])]
    ppermute x16, waiting for transfers between devices: 43.1 us -> 36.4 us  [swap_masks(): lax.ppermute(v, 'tensor', [(i, i ^ tensor_mask) for i in range(self.tenso...]
    ppermute x4, starting transfers between devices: 8.69 us -> 2.63 us  [swap_masks(): return lax.ppermute(v, ('dp', 'tensor'), pairs)]
    ppermute x8, waiting for transfers between devices: 5.86 us -> 10.7 us  [swap_masks(): return lax.ppermute(v, 'dp', [(i, i ^ dp_mask) for i in range(self.dp)])]
  transfers between devices with their start and end apart: 57 -> 57, of which waited for: 26 -> 23; matrix products, arithmetic and copies ran while one was open for 9% -> 9% of each run, Pallas kernels for 17% -> 18%
where the time goes in v5:
time: 363 us
  starting transfers between devices  126 us (35%)
  waiting for transfers between devices  102 us (28%)
  Pallas kernels  93.5 us (26%)
  other arithmetic  24.6 us (7%)
  local copies, waits for them, and re-layouts  11.3 us (3%)
    ppermute x16, starting transfers between devices, swap_masks(): lax.ppermute(v, 'tensor', [(i, i ^ tensor_mask) for i in range(self.tenso...  66.2 us
    ppermute x29, starting transfers between devices, swap(): return lax.ppermute(v, axis, [(i, i ^ r * stride) for i in range(total)])  53.1 us
    ppermute x29, waiting for transfers between devices, swap(): return lax.ppermute(v, axis, [(i, i ^ r * stride) for i in range(total)])  42.8 us
    ppermute x16, waiting for transfers between devices, swap_masks(): lax.ppermute(v, 'tensor', [(i, i ^ tensor_mask) for i in range(self.tenso...  36.4 us
    pallas_call x4, Pallas kernels, ffn(): pl.pallas_call(functools.partial(ffn_kernel, parts, plan, shards, bool(be...  31.8 us
    pallas_call x1, Pallas kernels, attention_backward(): pl.pallas_call(functools.partial(backward_kernel, across), out_shape=(jax...  14.3 us
    pallas_call x2, Pallas kernels, grads(): pl.pallas_call(kernel, out_shape=(jax.ShapeDtypeStruct((parts // 2, zs, r...  14.3 us
    ppermute x4, waiting for transfers between devices, swap_masks(): return lax.ppermute(v, ('dp', 'tensor'), pairs)  11.8 us
  transfers between devices with their start and end apart: 57, of which 23 were waited for; matrix products, arithmetic and copies ran while one was open for 9% of the time, Pallas kernels for 18%

profile of v5, /device:TPU:0, one launch (start us, length us, event | category | flops | bytes accessed | tf_op | source)
XLA Modules:
  0.0 363.1 jit_solution(17280918742094169585)
XLA Ops:
  0.7 3.0 collective-permute-start.3
  18.2 3.6 collective-permute-start.4
  21.8 20.7 %collective-permute-done.1 = bf16[320,256]{1,0:T(8,128)(2,1)S(1)} collective-permute-done((bf16[320,256]{1,0:T(8,128)(2,1)S(1)}, bf16[320,256]{1,0:T(8,128)(2,1)S(1)}, u32[]{:S(2)}, u32[]{:S(2)}) %collective-permute-start.1) | collective-permute-done | bytes 163872 | tf_op jit(solution)/shard_map/ppermute | solution.py:596
  50.3 3.0 collective-permute-start.7
  58.2 7.3 %collective-permute-done.7 = bf16[3,352,256]{2,1,0:T(8,128)(2,1)} collective-permute-done((bf16[3,352,256]{2,1,0:T(8,128)(2,1)}, bf16[3,352,256]{2,1,0:T(8,128)(2,1)}, u32[]{:S(2)}, u32[]{:S(2)}) %collective-permute-start.7) | collective-permute-done | bytes 540704 | tf_op jit(solution)/shard_map/ppermute | solution.py:596
  65.5 11.7 %attention_forward.1 = (bf16[256,1024]{1,0:T(8,128)(2,1)}, f32[16,256,128]{2,1,0:T(8,128)}) custom-call(s32[2]{0:T(128)} %pad_add_fusion.scal_ref, bf16[480,256]{1,0:T(8,128)(2,1)} %copy-done.9, bf16[4,320,256]{2,1,0:T(8,128)(2,1)} %pad_maximum_fusion.5.refs_0_, bf16[4,320,256]{2,1,0:T(8,128)(2,1)} %collective-permute-done.6.refs_1_, ...), custom_call_target="tpu_custom_call" | custom-call | flops 1000 | bytes 1000 | tf_op jit(solution)/shard_map/attention_forward/pallas_call | solution.py:158
  81.5 5.7 %collective-permute-start.11 = (bf16[256,1024]{1,0:T(8,128)(2,1)}, bf16[256,1024]{1,0:T(8,128)(2,1)}, u32[]{:S(2)}, u32[]{:S(2)}) collective-permute-start(bf16[256,1024]{1,0:T(8,128)(2,1)} %multiply_convert_fusion.xf_ref.refs_0_), channel_id=1, source_target_pairs={{0,1},{1,0},{2,3},{3,2},{4,5},{5,4},{6,7},{7,6},{8,9},{9,8},{10,11... | collective-permute-start | bytes 1572872 | tf_op jit(solution)/shard_map/ppermute | solution.py:596
  87.8 9.6 %ffn_early.2 = (f32[256,1024]{1,0:T(8,128)}, f32[256,1024]{1,0:T(8,128)}, bf16[1,256,1056]{2,1,0:T(8,128)(2,1)}, bf16[1,256,1056]{2,1,0:T(8,128)(2,1)}, bf16[1,256,1056]{2,1,0:T(8,128)(2,1)}) custom-call(s32[2]{0:T(128)} %pad_add_fusion.1.scal_ref, bf16[256,1024]{1,0:T(8,128)(2,1)} %multiply_convert_fusion.xf_ref.refs_0_, bf16[256,1024]{1,0:T(8,128)(2,1)} %bitcast.187, ...), custom_call_target="tpu_custom_call" | custom-call | flops 1000 | bytes 1000 | tf_op jit(solution)/shard_map/ffn_early/pallas_call | solution.py:722
  100.2 9.6 %ffn_early.3 = (f32[256,1024]{1,0:T(8,128)}, f32[256,1024]{1,0:T(8,128)}, bf16[1,256,1056]{2,1,0:T(8,128)(2,1)}, bf16[1,256,1056]{2,1,0:T(8,128)(2,1)}, bf16[1,256,1056]{2,1,0:T(8,128)(2,1)}) custom-call(s32[2]{0:T(128)} %pad_add_fusion.1.scal_ref, bf16[256,1024]{1,0:T(8,128)(2,1)} %collective-permute-done.11.xf_ref.refs_1_, ...), custom_call_target="tpu_custom_call" | custom-call | flops 1000 | bytes 1000 | tf_op jit(solution)/shard_map/ffn_early/pallas_call | solution.py:722
  110.8 6.5 %ffn_late.2 = (f32[256,1024]{1,0:T(8,128)}, f32[256,1024]{1,0:T(8,128)}, bf16[1,256,352]{2,1,0:T(8,128)(2,1)}, bf16[1,256,352]{2,1,0:T(8,128)(2,1)}, bf16[1,256,352]{2,1,0:T(8,128)(2,1)}) custom-call(s32[2]{0:T(128)} %pad_add_fusion.1.scal_ref, bf16[256,1024]{1,0:T(8,128)(2,1)} %multiply_convert_fusion.xf_ref.refs_0_, bf16[256,1024]{1,0:T(8,128)(2,1)} %bitcast.188, ...), custom_call_target="tpu_custom_call" | custom-call | flops 1000 | bytes 1000 | tf_op jit(solution)/shard_map/ffn_late/pallas_call | solution.py:722
  117.3 6.1 %ffn_late.3 = (bf16[256,1024]{1,0:T(8,128)(2,1)}, bf16[256,1024]{1,0:T(8,128)(2,1)}, bf16[1,256,352]{2,1,0:T(8,128)(2,1)}, bf16[1,256,352]{2,1,0:T(8,128)(2,1)}, bf16[1,256,352]{2,1,0:T(8,128)(2,1)}) custom-call(s32[2]{0:T(128)} %pad_add_fusion.1.scal_ref, bf16[256,1024]{1,0:T(8,128)(2,1)} %collective-permute-done.11.xf_ref.refs_1_, ...), custom_call_target="tpu_custom_call" | custom-call | flops 1000 | bytes 1000 | tf_op jit(solution)/shard_map/ffn_late/pallas_call | solution.py:722
  123.4 8.9 %gate_up_grads.1 = (bf16[2,4,704,256]{3,2,1,0:T(8,128)(2,1)}, bf16[2,4,704,256]{3,2,1,0:T(8,128)(2,1)}) custom-call(s32[2]{0:T(128)} %pad_add_fusion.1.scal_ref, bf16[256,1024]{1,0:T(8,128)(2,1)} %multiply_convert_fusion.xf_ref.refs_0_, bf16[256,1024]{1,0:T(8,128)(2,1)} %collective-permute-done.11.xf_ref.refs_1_, ...), custom_call_target="tpu_custom_call" | custom-call | flops 1000 | bytes 1000 | tf_op jit(solution)/shard_map/gate_up_grads/pallas_call | solution.py:790
  134.2 5.4 %down_grads.1 = (bf16[2,4,352,256]{3,2,1,0:T(8,128)(2,1)}, bf16[2,4,352,256]{3,2,1,0:T(8,128)(2,1)}) custom-call(s32[2]{0:T(128)} %pad_add_fusion.1.scal_ref, bf16[256,1024]{1,0:T(8,128)(2,1)} %bitcast.189, bf16[256,1024]{1,0:T(8,128)(2,1)} %collective-permute-done.3.dy_ref.refs_1_, bf16[1,256,1056]{2,1,0:T(8,128)(2,1)} %get-tuple-element.115.refs_2_, ...), custom_call_target="tpu_custom_call" | custom-call | flops 1000 | bytes 1000 | tf_op jit(solution)/shard_map/down_grads/pallas_call | solution.py:790
  139.7 3.4 fusion.4
  143.1 3.9 %collective-permute-done.15 = bf16[256,1024]{1,0:T(8,128)(2,1)} collective-permute-done((bf16[256,1024]{1,0:T(8,128)(2,1)}, bf16[256,1024]{1,0:T(8,128)(2,1)}, u32[]{:S(2)}, u32[]{:S(2)}) %collective-permute-start.15) | collective-permute-done | bytes 524320 | tf_op jit(solution)/shard_map/ppermute | solution.py:596
  163.1 14.3 %attention_backward.1 = (bf16[4,320,256]{2,1,0:T(8,128)(2,1)}, bf16[4,320,256]{2,1,0:T(8,128)(2,1)}, bf16[480,256]{1,0:T(8,128)(2,1)}) custom-call(s32[2]{0:T(128)} %pad_add_fusion.scal_ref, bf16[480,256]{1,0:T(8,128)(2,1)} %copy-done.9, bf16[4,320,256]{2,1,0:T(8,128)(2,1)} %pad_maximum_fusion.5.refs_0_, ...), custom_call_target="tpu_custom_call" | custom-call | flops 1000 | bytes 1000 | tf_op jit(solution)/shard_map/attention_backward/pallas_call | solution.py:304
  177.3 8.4 %collective-permute-done.22 = bf16[4,32,1024]{2,1,0:T(8,128)(2,1)S(1)} collective-permute-done((bf16[4,32,1024]{2,1,0:T(8,128)(2,1)S(1)}, bf16[4,32,1024]{2,1,0:T(8,128)(2,1)S(1)}, u32[]{:S(2)}, u32[]{:S(2)}) %collective-permute-start.22) | collective-permute-done | bytes 262176 | tf_op jit(solution)/shard_map/ppermute | solution.py:626
  187.1 15.4 %collective-permute-start.25 = (bf16[32,1024]{1,0:T(8,128)(2,1)S(1)}, bf16[32,1024]{1,0:T(8,128)(2,1)S(1)}, u32[]{:S(2)}, u32[]{:S(2)}) collective-permute-start(bf16[32,1024]{1,0:T(8,128)(2,1)S(1)} %get-tuple-element.189), channel_id=1, source_target_pairs={{0,2},{1,3},{2,0},{3,1},{4,6},{5,7},{6,4},{7,5},{8,10},{9,11},{10,... | collective-permute-start | bytes 196616 | tf_op jit(solution)/shard_map/ppermute | solution.py:628
  202.5 22.5 %collective-permute-start.26 = (bf16[32,1024]{1,0:T(8,128)(2,1)S(1)}, bf16[32,1024]{1,0:T(8,128)(2,1)S(1)}, u32[]{:S(2)}, u32[]{:S(2)}) collective-permute-start(bf16[32,1024]{1,0:T(8,128)(2,1)S(1)} %get-tuple-element.191), channel_id=1, source_target_pairs={{0,4},{1,5},{2,6},{3,7},{4,0},{5,1},{6,2},{7,3},{8,12},{9,13},{10,... | collective-permute-start | bytes 196616 | tf_op jit(solution)/shard_map/ppermute | solution.py:628
  226.4 7.6 %collective-permute-start.21 = (bf16[4,320,256]{2,1,0:T(8,128)(2,1)S(1)}, bf16[4,320,256]{2,1,0:T(8,128)(2,1)S(1)}, u32[]{:S(2)}, u32[]{:S(2)}) collective-permute-start(bf16[4,320,256]{2,1,0:T(8,128)(2,1)S(1)} %copy-done.40), channel_id=1, source_target_pairs={{0,1},{1,0},{2,3},{3,2},{4,5},{5,4},{6,7},{7,6},{8,9},{9,8},{10,11... | collective-permute-start | bytes 1966088 | tf_op jit(solution)/shard_map/ppermute | solution.py:596
  239.9 4.1 %collective-permute-done.30 = bf16[32,1024]{1,0:T(8,128)(2,1)S(1)} collective-permute-done((bf16[32,1024]{1,0:T(8,128)(2,1)S(1)}, bf16[32,1024]{1,0:T(8,128)(2,1)S(1)}, u32[]{:S(2)}, u32[]{:S(2)}) %collective-permute-start.30) | collective-permute-done | bytes 65568 | tf_op jit(solution)/shard_map/ppermute | solution.py:628
  254.2 3.3 collective-permute-done.32
  257.6 4.6 %leave_rest.1 = (bf16[256,1024]{1,0:T(8,128)(2,1)}, bf16[16,32,896]{2,1,0:T(8,128)(2,1)S(1)}, bf16[16,32,896]{2,1,0:T(8,128)(2,1)S(1)}) custom-call(s32[3]{0:T(128)S(1)} %pad_add_fusion.2.ids_ref, bf16[256,1024]{1,0:T(8,128)(2,1)S(1)} %bitcast.168, bf16[256,1024]{1,0:T(8,128)(2,1)S(1)} %copy-done.17, f32[1,1024]{1,0:T(1,128)S(1)} %bitcast.182, ...), custom_call_target="tpu_custom_call" | custom-call | flops 1000 | bytes 1000 | tf_op jit(solution)/shard_map/leave_rest/pallas_call | solution.py:502
  263.8 8.9 %collective-permute-start.36 = (bf16[4,32,1024]{2,1,0:T(8,128)(2,1)S(1)}, bf16[4,32,1024]{2,1,0:T(8,128)(2,1)S(1)}, u32[]{:S(2)}, u32[]{:S(2)}) collective-permute-start(bf16[4,32,1024]{2,1,0:T(8,128)(2,1)S(1)} %pad_maximum_fusion.7), channel_id=1, source_target_pairs={{0,1},{1,0},{2,3},{3,2},{4,5},{5,4},{6,7},{7,6},{8,9},{9,8},{10,11... | collective-permute-start | bytes 786440 | tf_op jit(solution)/shard_map/ppermute | solution.py:628
  273.6 6.2 %collective-permute-done.36 = bf16[4,32,1024]{2,1,0:T(8,128)(2,1)S(1)} collective-permute-done((bf16[4,32,1024]{2,1,0:T(8,128)(2,1)S(1)}, bf16[4,32,1024]{2,1,0:T(8,128)(2,1)S(1)}, u32[]{:S(2)}, u32[]{:S(2)}) %collective-permute-start.36) | collective-permute-done | bytes 262176 | tf_op jit(solution)/shard_map/ppermute | solution.py:628
  279.8 5.5 %collective-permute-done.37 = bf16[4,32,1024]{2,1,0:T(8,128)(2,1)S(1)} collective-permute-done((bf16[4,32,1024]{2,1,0:T(8,128)(2,1)S(1)}, bf16[4,32,1024]{2,1,0:T(8,128)(2,1)S(1)}, u32[]{:S(2)}, u32[]{:S(2)}) %collective-permute-start.37) | collective-permute-done | bytes 262176 | tf_op jit(solution)/shard_map/ppermute | solution.py:631
  294.8 3.6 %collective-permute-done.40 = bf16[4,32,896]{2,1,0:T(8,128)(2,1)S(1)} collective-permute-done((bf16[4,32,896]{2,1,0:T(8,128)(2,1)S(1)}, bf16[4,32,896]{2,1,0:T(8,128)(2,1)S(1)}, u32[]{:S(2)}, u32[]{:S(2)}) %collective-permute-start.40) | collective-permute-done | bytes 229408 | tf_op jit(solution)/shard_map/ppermute | solution.py:631
  304.1 15.1 %collective-permute-done.44 = bf16[32,896]{1,0:T(8,128)(2,1)S(1)} collective-permute-done((bf16[32,896]{1,0:T(8,128)(2,1)S(1)}, bf16[32,896]{1,0:T(8,128)(2,1)S(1)}, u32[]{:S(2)}, u32[]{:S(2)}) %collective-permute-start.44) | collective-permute-done | bytes 57376 | tf_op jit(solution)/shard_map/ppermute | solution.py:628
  320.2 8.9 %collective-permute-start.42 = (bf16[256,1024]{1,0:T(8,128)(2,1)S(1)}, bf16[256,1024]{1,0:T(8,128)(2,1)S(1)}, u32[]{:S(2)}, u32[]{:S(2)}) collective-permute-start(bf16[256,1024]{1,0:T(8,128)(2,1)S(1)} %copy-done.41), channel_id=1, source_target_pairs={{0,1},{1,0},{2,3},{3,2},{4,5},{5,4},{6,7},{7,6},{8,9},{9,8},{10,11... | collective-permute-start | bytes 1572872 | tf_op jit(solution)/shard_map/ppermute | solution.py:596
  344.0 3.5 end_out.1
  353.6 5.5 %unpack.1 = (f32[352,1024]{1,0:T(8,128)}, f32[352,1024]{1,0:T(8,128)}, f32[352,1024]{1,0:T(8,128)}) custom-call(s32[2]{0:T(128)} %pad_add_fusion.1.scal_ref, bf16[2,1056,256]{2,1,0:T(8,128)(2,1)} %copy-done.28, bf16[2,1056,256]{2,1,0:T(8,128)(2,1)} %collective-permute-done.55.got_ref), custom_call_target="tpu_custom_call" | custom-call | flops 1000 | bytes 1000 | tf_op jit(solution)/shard_map/unpack/pallas_call | solution.py:817
  359.2 3.8 %end_rest.1 = (f32[1024,128]{1,0:T(8,128)}, f32[1024,128]{1,0:T(8,128)}, f32[1024,384]{1,0:T(8,128)}, f32[96,1024]{1,0:T(8,128)}, f32[32,1024]{1,0:T(8,128)}, /*...) custom-call(s32[3]{0:T(128)S(1)} %pad_add_fusion.2.ids_ref, bf16[16,32,896]{2,1,0:T(8,128)(2,1)S(1)} %bitcast.170, ...), custom_call_target="tpu_custom_call" | custom-call | tf_op jit(solution)/shard_map/end_rest/pallas_call | solution.py:557
  (232 shorter events, 111.3 us)
Async XLA Ops:
  0.7 17.5 %collective-permute-start.3 = (bf16[256,1024]{1,0:T(8,128)(2,1)}, bf16[256,1024]{1,0:T(8,128)(2,1)}, u32[]{:S(2)}, u32[]{:S(2)}) collective-permute-start(bf16[256,1024]{1,0:T(8,128)(2,1)} %bitcast.186), channel_id=1, source_target_pairs={{0,1},{1,0},{2,3},{3,2},{4,5},{5,4},{6,7},{7,6},{8,9},{9,8},{10,11... | collective-permute-start | bytes 1572872 | tf_op jit(solution)/shard_map/ppermute | solution.py:596
  6.6 39.1 %collective-permute-start = (bf16[3,352,256]{2,1,0:T(8,128)(2,1)}, bf16[3,352,256]{2,1,0:T(8,128)(2,1)}, u32[]{:S(2)}, u32[]{:S(2)}) collective-permute-start(bf16[3,352,256]{2,1,0:T(8,128)(2,1)} %pad_maximum_fusion.6), channel_id=1, source_target_pairs={{0,4},{1,5},{2,6},{3,7},{4,0},{5,1},{6,2},{7,3},{8,12},{9,13},{10,... | collective-permute-start | bytes 1622024 | tf_op jit(solution)/shard_map/ppermute | solution.py:596
  9.2 36.5 %collective-permute-start.5 = (bf16[3,352,256]{2,1,0:T(8,128)(2,1)}, bf16[3,352,256]{2,1,0:T(8,128)(2,1)}, u32[]{:S(2)}, u32[]{:S(2)}) collective-permute-start(bf16[3,352,256]{2,1,0:T(8,128)(2,1)} %pad_maximum_fusion.6), channel_id=1, source_target_pairs={{0,2},{1,3},{2,0},{3,1},{4,6},{5,7},{6,4},{7,5},{8,10},{9,11},{10,... | collective-permute-start | bytes 1622024 | tf_op jit(solution)/shard_map/ppermute | solution.py:596
  17.4 25.2 %collective-permute-start.1 = (bf16[320,256]{1,0:T(8,128)(2,1)S(1)}, bf16[320,256]{1,0:T(8,128)(2,1)S(1)}, u32[]{:S(2)}, u32[]{:S(2)}) collective-permute-start(bf16[320,256]{1,0:T(8,128)(2,1)S(1)} %get-tuple-element.93), channel_id=1, source_target_pairs={{0,4},{1,5},{2,6},{3,7},{4,0},{5,1},{6,2},{7,3},{8,12},{9,13},{10,... | collective-permute-start | bytes 491528 | tf_op jit(solution)/shard_map/ppermute | solution.py:596
  17.8 24.8 %collective-permute-start.2 = (bf16[320,256]{1,0:T(8,128)(2,1)S(1)}, bf16[320,256]{1,0:T(8,128)(2,1)S(1)}, u32[]{:S(2)}, u32[]{:S(2)}) collective-permute-start(bf16[320,256]{1,0:T(8,128)(2,1)S(1)} %get-tuple-element.93), channel_id=1, source_target_pairs={{0,2},{1,3},{2,0},{3,1},{4,6},{5,7},{6,4},{7,5},{8,10},{9,11},{10,... | collective-permute-start | bytes 491528 | tf_op jit(solution)/shard_map/ppermute | solution.py:596
  18.2 26.5 %collective-permute-start.4 = (bf16[320,256]{1,0:T(8,128)(2,1)S(1)}, bf16[320,256]{1,0:T(8,128)(2,1)S(1)}, u32[]{:S(2)}, u32[]{:S(2)}) collective-permute-start(bf16[320,256]{1,0:T(8,128)(2,1)S(1)} %get-tuple-element.93), channel_id=1, source_target_pairs={{0,6},{1,7},{2,4},{3,5},{4,2},{5,3},{6,0},{7,1},{8,14},{9,15},{10,... | collective-permute-start | bytes 491528 | tf_op jit(solution)/shard_map/ppermute | solution.py:596
  48.0 29.3 %collective-permute-start.9 = (bf16[2,3,352,256]{3,2,1,0:T(8,128)(2,1)}, bf16[2,3,352,256]{3,2,1,0:T(8,128)(2,1)}, u32[]{:S(2)}, u32[]{:S(2)}) collective-permute-start(bf16[2,3,352,256]{3,2,1,0:T(8,128)(2,1)} %pad_maximum_fusion.1.refs_3_), channel_id=1, source_target_pairs={{0,16},{8,24},{16,0},{24,8},{1,17},{9,25},{17,1},{25,9},{2,18},{10... | collective-permute-start | bytes 3244040 | tf_op jit(solution)/shard_map/ppermute | solution.py:596
  49.5 16.0 %collective-permute-start.6 = (bf16[4,320,256]{2,1,0:T(8,128)(2,1)}, bf16[4,320,256]{2,1,0:T(8,128)(2,1)}, u32[]{:S(2)}, u32[]{:S(2)}) collective-permute-start(bf16[4,320,256]{2,1,0:T(8,128)(2,1)} %pad_maximum_fusion.5.refs_0_), channel_id=1, source_target_pairs={{0,1},{1,0},{2,3},{3,2},{4,5},{5,4},{6,7},{7,6},{8,9},{9,8},{10,11... | collective-permute-start | bytes 1966088 | tf_op jit(solution)/shard_map/ppermute | solution.py:596
  50.3 15.2 %collective-permute-start.7 = (bf16[3,352,256]{2,1,0:T(8,128)(2,1)}, bf16[3,352,256]{2,1,0:T(8,128)(2,1)}, u32[]{:S(2)}, u32[]{:S(2)}) collective-permute-start(bf16[3,352,256]{2,1,0:T(8,128)(2,1)} %collective-permute-done), channel_id=1, source_target_pairs={{0,2},{1,3},{2,0},{3,1},{4,6},{5,7},{6,4},{7,5},{8,10},{9,11},{10,... | collective-permute-start | bytes 1622024 | tf_op jit(solution)/shard_map/ppermute | solution.py:596
  79.6 20.1 %collective-permute-start.13 = (bf16[1,3,352,256]{3,2,1,0:T(8,128)(2,1)}, bf16[1,3,352,256]{3,2,1,0:T(8,128)(2,1)}, u32[]{:S(2)}, u32[]{:S(2)}) collective-permute-start(bf16[1,3,352,256]{3,2,1,0:T(8,128)(2,1)} %bitcast.24.refs_0_), channel_id=1, source_target_pairs={{0,16},{8,24},{16,0},{24,8},{1,17},{9,25},{17,1},{25,9},{2,18},{10... | collective-permute-start | bytes 1622024 | tf_op jit(solution)/shard_map/ppermute | solution.py:596
  81.5 18.2 %collective-permute-start.11 = (bf16[256,1024]{1,0:T(8,128)(2,1)}, bf16[256,1024]{1,0:T(8,128)(2,1)}, u32[]{:S(2)}, u32[]{:S(2)}) collective-permute-start(bf16[256,1024]{1,0:T(8,128)(2,1)} %multiply_convert_fusion.xf_ref.refs_0_), channel_id=1, source_target_pairs={{0,1},{1,0},{2,3},{3,2},{4,5},{5,4},{6,7},{7,6},{8,9},{9,8},{10,11... | collective-permute-start | bytes 1572872 | tf_op jit(solution)/shard_map/ppermute | solution.py:596
  132.3 14.7 %collective-permute-start.15 = (bf16[256,1024]{1,0:T(8,128)(2,1)}, bf16[256,1024]{1,0:T(8,128)(2,1)}, u32[]{:S(2)}, u32[]{:S(2)}) collective-permute-start(bf16[256,1024]{1,0:T(8,128)(2,1)} %get-tuple-element.114), channel_id=1, source_target_pairs={{0,1},{1,0},{2,3},{3,2},{4,5},{5,4},{6,7},{7,6},{8,9},{9,8},{10,11... | collective-permute-start | bytes 1572872 | tf_op jit(solution)/shard_map/ppermute | solution.py:596
  139.5 14.1 %collective-permute-start.17 = (bf16[2,4,352,256]{3,2,1,0:T(8,128)(2,1)}, bf16[2,4,352,256]{3,2,1,0:T(8,128)(2,1)S(1)}, u32[]{:S(2)}, u32[]{:S(2)}) collective-permute-start(bf16[2,4,352,256]{3,2,1,0:T(8,128)(2,1)} %get-tuple-element.131), channel_id=1, source_target_pairs={{0,8},{8,0},{16,24},{24,16},{1,9},{9,1},{17,25},{25,17},{2,10},{10... | collective-permute-start | bytes 4325384 | tf_op jit(solution)/shard_map/ppermute | solution.py:596
  155.3 71.1 %collective-permute-start.20 = (bf16[4,352,256]{2,1,0:T(8,128)(2,1)}, bf16[4,352,256]{2,1,0:T(8,128)(2,1)}, u32[]{:S(2)}, u32[]{:S(2)}) collective-permute-start(bf16[4,352,256]{2,1,0:T(8,128)(2,1)} %fusion.7), channel_id=1, source_target_pairs={{0,16},{8,24},{16,0},{24,8},{1,17},{9,25},{17,1},{25,9},{2,18},{10... | collective-permute-start | bytes 2162696 | tf_op jit(solution)/shard_map/ppermute | solution.py:596
  156.8 29.0 %collective-permute-start.22 = (bf16[4,32,1024]{2,1,0:T(8,128)(2,1)S(1)}, bf16[4,32,1024]{2,1,0:T(8,128)(2,1)S(1)}, u32[]{:S(2)}, u32[]{:S(2)}) collective-permute-start(bf16[4,32,1024]{2,1,0:T(8,128)(2,1)S(1)} %get-tuple-element.180), channel_id=1, source_target_pairs={{0,16},{8,24},{16,0},{24,8},{1,17},{9,25},{17,1},{25,9},{2,18},{10... | collective-permute-start | bytes 786440 | tf_op jit(solution)/shard_map/ppermute | solution.py:626
  158.0 27.8 %collective-permute-start.23 = (bf16[4,32,1024]{2,1,0:T(8,128)(2,1)S(1)}, bf16[4,32,1024]{2,1,0:T(8,128)(2,1)}, u32[]{:S(2)}, u32[]{:S(2)}) collective-permute-start(bf16[4,32,1024]{2,1,0:T(8,128)(2,1)S(1)} %get-tuple-element.182), channel_id=1, source_target_pairs={{0,1},{1,0},{2,3},{3,2},{4,5},{5,4},{6,7},{7,6},{8,9},{9,8},{10,11... | collective-permute-start | bytes 786440 | tf_op jit(solution)/shard_map/ppermute | solution.py:628
  159.7 26.1 %collective-permute-start.24 = (bf16[4,32,1024]{2,1,0:T(8,128)(2,1)S(1)}, bf16[4,32,1024]{2,1,0:T(8,128)(2,1)}, u32[]{:S(2)}, u32[]{:S(2)}) collective-permute-start(bf16[4,32,1024]{2,1,0:T(8,128)(2,1)S(1)} %get-tuple-element.181), channel_id=1, source_target_pairs={{0,17},{1,16},{2,19},{3,18},{4,21},{5,20},{6,23},{7,22},{8,25},{9,... | collective-permute-start | bytes 786440 | tf_op jit(solution)/shard_map/ppermute | solution.py:631
  161.9 82.2 %collective-permute-start.19 = (bf16[4,704,256]{2,1,0:T(8,128)(2,1)}, bf16[4,704,256]{2,1,0:T(8,128)(2,1)}, u32[]{:S(2)}, u32[]{:S(2)}) collective-permute-start(bf16[4,704,256]{2,1,0:T(8,128)(2,1)} %fusion.4), channel_id=1, source_target_pairs={{0,16},{8,24},{16,0},{24,8},{1,17},{9,25},{17,1},{25,9},{2,18},{10... | collective-permute-start | bytes 4325384 | tf_op jit(solution)/shard_map/ppermute | solution.py:596
  187.1 47.0 %collective-permute-start.25 = (bf16[32,1024]{1,0:T(8,128)(2,1)S(1)}, bf16[32,1024]{1,0:T(8,128)(2,1)S(1)}, u32[]{:S(2)}, u32[]{:S(2)}) collective-permute-start(bf16[32,1024]{1,0:T(8,128)(2,1)S(1)} %get-tuple-element.189), channel_id=1, source_target_pairs={{0,2},{1,3},{2,0},{3,1},{4,6},{5,7},{6,4},{7,5},{8,10},{9,11},{10,... | collective-permute-start | bytes 196616 | tf_op jit(solution)/shard_map/ppermute | solution.py:628
  202.5 31.6 %collective-permute-start.26 = (bf16[32,1024]{1,0:T(8,128)(2,1)S(1)}, bf16[32,1024]{1,0:T(8,128)(2,1)S(1)}, u32[]{:S(2)}, u32[]{:S(2)}) collective-permute-start(bf16[32,1024]{1,0:T(8,128)(2,1)S(1)} %get-tuple-element.191), channel_id=1, source_target_pairs={{0,4},{1,5},{2,6},{3,7},{4,0},{5,1},{6,2},{7,3},{8,12},{9,13},{10,... | collective-permute-start | bytes 196616 | tf_op jit(solution)/shard_map/ppermute | solution.py:628
  226.4 20.1 %collective-permute-start.21 = (bf16[4,320,256]{2,1,0:T(8,128)(2,1)S(1)}, bf16[4,320,256]{2,1,0:T(8,128)(2,1)S(1)}, u32[]{:S(2)}, u32[]{:S(2)}) collective-permute-start(bf16[4,320,256]{2,1,0:T(8,128)(2,1)S(1)} %copy-done.40), channel_id=1, source_target_pairs={{0,1},{1,0},{2,3},{3,2},{4,5},{5,4},{6,7},{7,6},{8,9},{9,8},{10,11... | collective-permute-start | bytes 1966088 | tf_op jit(solution)/shard_map/ppermute | solution.py:596
  262.2 11.1 %collective-permute-start.34 = (bf16[4,4,32,896]{3,2,1,0:T(8,128)(2,1)S(1)}, bf16[4,4,32,896]{3,2,1,0:T(8,128)(2,1)S(1)}, u32[]{:S(2)}, u32[]{:S(2)}) collective-permute-start(bf16[4,4,32,896]{3,2,1,0:T(8,128)(2,1)S(1)} %bitcast.185), channel_id=1, source_target_pairs={{0,8},{8,0},{16,24},{24,16},{1,9},{9,1},{17,25},{25,17},{2,10},{10... | collective-permute-start | bytes 2752520 | tf_op jit(solution)/shard_map/ppermute | solution.py:626
  262.2 26.8 %collective-permute-start.41 = (bf16[2,1056,256]{2,1,0:T(8,128)(2,1)S(1)}, bf16[2,1056,256]{2,1,0:T(8,128)(2,1)S(1)}, u32[]{:S(2)}, u32[]{:S(2)}) collective-permute-start(bf16[2,1056,256]{2,1,0:T(8,128)(2,1)S(1)} %fusion.2), channel_id=1, source_target_pairs={{0,2},{1,3},{2,0},{3,1},{4,6},{5,7},{6,4},{7,5},{8,10},{9,11},{10,... | collective-permute-start | bytes 3244040 | tf_op jit(solution)/shard_map/ppermute | solution.py:596
  262.9 10.7 %collective-permute-start.35 = (bf16[4,32,1024]{2,1,0:T(8,128)(2,1)S(1)}, bf16[4,32,1024]{2,1,0:T(8,128)(2,1)S(1)}, u32[]{:S(2)}, u32[]{:S(2)}) collective-permute-start(bf16[4,32,1024]{2,1,0:T(8,128)(2,1)S(1)} %pad_maximum_fusion.7), channel_id=1, source_target_pairs={{0,16},{8,24},{16,0},{24,8},{1,17},{9,25},{17,1},{25,9},{2,18},{10... | collective-permute-start | bytes 786440 | tf_op jit(solution)/shard_map/ppermute | solution.py:626
  263.8 16.1 %collective-permute-start.36 = (bf16[4,32,1024]{2,1,0:T(8,128)(2,1)S(1)}, bf16[4,32,1024]{2,1,0:T(8,128)(2,1)S(1)}, u32[]{:S(2)}, u32[]{:S(2)}) collective-permute-start(bf16[4,32,1024]{2,1,0:T(8,128)(2,1)S(1)} %pad_maximum_fusion.7), channel_id=1, source_target_pairs={{0,1},{1,0},{2,3},{3,2},{4,5},{5,4},{6,7},{7,6},{8,9},{9,8},{10,11... | collective-permute-start | bytes 786440 | tf_op jit(solution)/shard_map/ppermute | solution.py:628
  272.7 12.6 %collective-permute-start.37 = (bf16[4,32,1024]{2,1,0:T(8,128)(2,1)S(1)}, bf16[4,32,1024]{2,1,0:T(8,128)(2,1)S(1)}, u32[]{:S(2)}, u32[]{:S(2)}) collective-permute-start(bf16[4,32,1024]{2,1,0:T(8,128)(2,1)S(1)} %pad_maximum_fusion.7), channel_id=1, source_target_pairs={{0,17},{1,16},{2,19},{3,18},{4,21},{5,20},{6,23},{7,22},{8,25},{9,... | collective-permute-start | bytes 786440 | tf_op jit(solution)/shard_map/ppermute | solution.py:631
  289.3 29.9 %collective-permute-start.53 = (bf16[1,1056,256]{2,1,0:T(8,128)(2,1)S(1)}, bf16[1,1056,256]{2,1,0:T(8,128)(2,1)S(1)}, u32[]{:S(2)}, u32[]{:S(2)}) collective-permute-start(bf16[1,1056,256]{2,1,0:T(8,128)(2,1)S(1)} %slice.222), channel_id=1, source_target_pairs={{0,4},{1,5},{2,6},{3,7},{4,0},{5,1},{6,2},{7,3},{8,12},{9,13},{10,... | collective-permute-start | bytes 1622024 | tf_op jit(solution)/shard_map/ppermute | solution.py:596
  299.8 19.3 %collective-permute-start.44 = (bf16[32,896]{1,0:T(8,128)(2,1)S(1)}, bf16[32,896]{1,0:T(8,128)(2,1)S(1)}, u32[]{:S(2)}, u32[]{:S(2)}) collective-permute-start(bf16[32,896]{1,0:T(8,128)(2,1)S(1)} %get-tuple-element.194), channel_id=1, source_target_pairs={{0,4},{1,5},{2,6},{3,7},{4,0},{5,1},{6,2},{7,3},{8,12},{9,13},{10,... | collective-permute-start | bytes 172040 | tf_op jit(solution)/shard_map/ppermute | solution.py:628
  301.2 17.9 %collective-permute-start.45 = (bf16[32,896]{1,0:T(8,128)(2,1)S(1)}, bf16[32,896]{1,0:T(8,128)(2,1)S(1)}, u32[]{:S(2)}, u32[]{:S(2)}) collective-permute-start(bf16[32,896]{1,0:T(8,128)(2,1)S(1)} %get-tuple-element.193), channel_id=1, source_target_pairs={{0,6},{1,7},{2,4},{3,5},{4,2},{5,3},{6,0},{7,1},{8,14},{9,15},{10,... | collective-permute-start | bytes 172040 | tf_op jit(solution)/shard_map/ppermute | solution.py:628
  303.2 40.8 %collective-permute-start.52 = (bf16[4,4,32,1024]{3,2,1,0:T(8,128)(2,1)S(1)}, bf16[4,4,32,1024]{3,2,1,0:T(8,128)(2,1)S(1)}, u32[]{:S(2)}, u32[]{:S(2)}) collective-permute-start(bf16[4,4,32,1024]{3,2,1,0:T(8,128)(2,1)S(1)} %pad_maximum_fusion.3), channel_id=1, source_target_pairs={{0,8},{8,0},{16,24},{24,16},{1,9},{9,1},{17,25},{25,17},{2,10},{10... | collective-permute-start | bytes 3145736 | tf_op jit(solution)/shard_map/ppermute | solution.py:626
  319.3 24.4 %collective-permute-start.54 = (bf16[1056,256]{1,0:T(8,128)(2,1)S(1)}, bf16[1056,256]{1,0:T(8,128)(2,1)S(1)}, u32[]{:S(2)}, u32[]{:S(2)}) collective-permute-start(bf16[1056,256]{1,0:T(8,128)(2,1)S(1)} %fusion.8), channel_id=1, source_target_pairs={{0,16},{8,24},{16,0},{24,8},{1,17},{9,25},{17,1},{25,9},{2,18},{10... | collective-permute-start | bytes 1622024 | tf_op jit(solution)/shard_map/ppermute | solution.py:596
  320.2 20.0 %collective-permute-start.42 = (bf16[256,1024]{1,0:T(8,128)(2,1)S(1)}, bf16[256,1024]{1,0:T(8,128)(2,1)S(1)}, u32[]{:S(2)}, u32[]{:S(2)}) collective-permute-start(bf16[256,1024]{1,0:T(8,128)(2,1)S(1)} %copy-done.41), channel_id=1, source_target_pairs={{0,1},{1,0},{2,3},{3,2},{4,5},{5,4},{6,7},{7,6},{8,9},{9,8},{10,11... | collective-permute-start | bytes 1572872 | tf_op jit(solution)/shard_map/ppermute | solution.py:596
  (67 other events, 750.5 us)
